TPU v7x, 128 devices: a whole 4x4x4 slice. The times are simulated.
128 devices in a mesh: circ: 32 (over x_lo, z, y), radax: 4 (over x_hi, core).
Axes of the slice: x: 4 (x_hi: 2, x_lo: 2; x = x_hi * 2 + x_lo), y: 4, z: 4, core: 2. Of those that a mesh axis runs over, the one named last changes fastest.
Arguments:
- objective_grad: float32 [256, 64, 6, 256], P('circ', 'radax'), may hold values from -6 to 6
- adjoint_start: float32 [256, 64, 6, 256], P('circ', 'radax'), may hold values from -6 to 6
- jac_off: bfloat16 [6, 6, 256, 64, 6, 256], P(None, None, 'circ', 'radax'), may hold values from -0.625 to 0.625
- jac_diag: bfloat16 [6, 256, 64, 6, 256], P(None, 'circ', 'radax'), may hold values from -3 to 3, as said below
- precond: bfloat16 [6, 256, 64, 6, 256], P(None, 'circ', 'radax'), may hold values from -1 to 1
- face_cell: int32 [65536], P(('circ', 'radax')), may hold values from 0 to 32767
- face_side: int32 [65536], P(('circ', 'radax')), may hold values from 0 to 1
- design_grad: float32 [65536, 6, 128], P(('circ', 'radax')), may hold values from -0.0546875 to 0.0546875
Outputs:
- adjoint: float32 [256, 64, 6, 256], P('circ', 'radax')
- sensitivity: float32 [32, 128], P('circ', 'radax')
Inputs may be any that keep to these rules, and one draw needn't show every extreme that they name: face_cell indexes the cells of the device that holds the face. `jac_diag`: diagonal blocks: each diagonal entry between 1.5 and 3, off-diagonal entries of moderate size.
All inputs are finite; a program needn't handle non-finite values.
Results may differ from a plain program's by a relative error of at most 0.0003.
Values sent between devices are 32-bit elements; how exact they have to be, the bound alone decides.
No kernel may reach another device: no remote copies, remote signals or barrier semaphores. Data moves between devices by JAX's collectives and lax.ppermute only.
A program may use at most 256 MiB of HBM per device.

v0:
```python
import jax
import jax.numpy as jnp
from jax import lax
from jax.sharding import PartitionSpec as P

NDV = 128
ITERS = 2


def extended(cells, sides, width, closed):
    for axis, dim in sides:
        count = lax.axis_size(axis)
        ends = count if closed else count - 1
        head = lax.slice_in_dim(cells, 0, width, axis=dim)
        tail = lax.slice_in_dim(cells, cells.shape[dim] - width, cells.shape[dim], axis=dim)
        cells = jnp.concatenate(
            [
                lax.ppermute(tail, axis, [(i, (i + 1) % count) for i in range(ends)]),
                cells,
                lax.ppermute(head, axis, [((i + 1) % count, i) for i in range(ends)]),
            ],
            axis=dim,
        )
    return cells


def passed_along(block, axis, distance):
    devices = range(lax.axis_size(axis))
    route = [((i - distance) % len(devices), i) for i in devices]
    return lax.ppermute(block, axis, route)


def block_apply(blocks, vector):
    summed = blocks[0].astype(jnp.float32) * vector[:, :, 0:1, :]
    for column in range(1, vector.shape[2]):
        summed = summed + blocks[column].astype(jnp.float32) * vector[:, :, column : column + 1, :]
    return summed


def neighbour_fields(field):
    wrapped = extended(field, (("circ", 0),), 1, True)
    stacked = extended(field, (("radax", 1),), 1, False)
    circ_lower = wrapped[:-2]
    circ_upper = wrapped[2:]
    rad_lower = stacked[:, :-2]
    rad_upper = stacked[:, 2:]
    axial_pad = jnp.pad(field, ((0, 0), (0, 0), (0, 0), (1, 1)))
    ax_lower = axial_pad[..., :-2]
    ax_upper = axial_pad[..., 2:]
    return [circ_lower, circ_upper, rad_lower, rad_upper, ax_lower, ax_upper]


def body(
    objective_grad, adjoint_start, jac_off, jac_diag, precond, face_cell, face_side, design_grad
):
    adjoint = adjoint_start
    for iteration in range(ITERS):
        beside = neighbour_fields(adjoint)
        applied = block_apply(jac_diag, adjoint)
        for direction in range(6):
            applied = applied + block_apply(jac_off[direction], beside[direction])
        residual = objective_grad - applied
        adjoint = adjoint + block_apply(precond, residual)
    cells_rad = adjoint.shape[1]
    cells_ax = adjoint.shape[3]
    theta = face_cell // (cells_rad * cells_ax)
    radial = face_cell // cells_ax % cells_rad
    axial = face_cell % cells_ax
    picked = adjoint[theta, radial, :, axial]
    contrib = jnp.einsum("fi,fid->fd", picked, design_grad, precision=lax.Precision.HIGHEST)
    side_table = (face_side[None, :] == jnp.arange(2, dtype=jnp.int32)[:, None]).astype(jnp.float32)
    partial_sens = jnp.dot(side_table, contrib, precision=lax.Precision.HIGHEST)
    blocks_count = lax.axis_size("radax")
    owned = NDV // blocks_count
    arrived = passed_along(partial_sens[1:2], "circ", 1)
    blade_sum = lax.psum(partial_sens[0:1] + arrived, "radax")
    sensitivity = lax.dynamic_slice_in_dim(blade_sum, lax.axis_index("radax") * owned, owned, 1)
    return (adjoint, sensitivity)


def solution(mesh):
    in_specs = (
        P("circ", "radax", None, None),
        P("circ", "radax", None, None),
        P(None, None, "circ", "radax", None, None),
        P(None, "circ", "radax", None, None),
        P(None, "circ", "radax", None, None),
        P(("circ", "radax")),
        P(("circ", "radax")),
        P(("circ", "radax"), None, None),
    )
    out_specs = (P("circ", "radax", None, None), P("circ", "radax"))
    return jax.shard_map(body, mesh=mesh, in_specs=in_specs, out_specs=out_specs, check_vma=False)
```

profile of v0, /device:TPU:1, one launch (start us, length us, event | category | flops | bytes accessed | tf_op | source)
XLA Modules:
  0.0 715.4 jit_solution(132593685499630922)
XLA Ops:
  0.6 0.0 copy-start
  0.6 1.7 fusion.173
  2.4 2.1 collective-permute-start
  4.5 1.8 fusion.174
  6.3 2.9 collective-permute-start.3
  9.2 5.6 collective-permute-start.1
  14.8 5.4 collective-permute-start.2
  20.2 3.7 slice_bitcast_fusion.35
  23.9 2.7 fusion.172
  26.5 0.7 fusion.163
  27.2 9.9 %copy.72 = f32[8,16,6,256]{2,3,1,0:T(8,128)} copy(f32[8,16,6,256]{3,1,2,0:T(8,128)} %param.9) | data formatting | bytes 1572864 | tf_op args[1]
  37.2 6.1 copy.66
  43.2 6.1 copy.67
  49.3 6.1 copy.68
  55.4 7.5 %copy.69 = bf16[1,8,16,6,256]{3,4,2,1,0:T(8,128)(2,1)} copy(bf16[1,8,16,6,256]{4,2,3,1,0:T(8,128)(2,1)} %get-tuple-element.57) | data formatting | bytes 786432 | tf_op jit(solution)/shard_map/slice | solution.py:36
  62.9 7.3 %copy.70 = bf16[1,8,16,6,256]{3,4,2,1,0:T(8,128)(2,1)} copy(bf16[1,8,16,6,256]{4,2,3,1,0:T(8,128)(2,1)} %get-tuple-element.61) | data formatting | bytes 786432 | tf_op jit(solution)/shard_map/slice | solution.py:36
  70.2 7.3 %copy.71 = bf16[1,8,16,6,256]{3,4,2,1,0:T(8,128)(2,1)} copy(bf16[1,8,16,6,256]{4,2,3,1,0:T(8,128)(2,1)} %get-tuple-element.60) | data formatting | bytes 786432 | tf_op jit(solution)/shard_map/slice | solution.py:36
  77.5 0.0 collective-permute-done.2
  77.6 1.7 maximum_bitcast_fusion.4
  79.2 0.9 constant_dynamic-update-slice_fusion.1
  80.1 1.4 constant_dynamic-update-slice_fusion
  81.6 1.0 copy-done.5
  82.5 0.0 collective-permute-done.3
  82.5 2.3 dynamic-update-slice.1
  84.8 1.4 slice_bitcast_fusion.17
  86.2 0.0 collective-permute-done.1
  86.3 1.5 constant_dynamic-update-slice_fusion.2
  87.8 1.3 slice_bitcast_fusion.23
  89.0 1.3 slice_bitcast_fusion.29
  90.3 11.5 %fusion.69 = f32[8,16,6,256]{3,1,2,0:T(8,128)S(1)} fusion(f32[8,16,6,256]{3,1,2,0:T(8,128)S(1)} %copy-done.4, f32[8,16,256]{2,1,0:T(8,128)} %get-tuple-element.109, f32[8,16,256]{2,1,0:T(8,128)} %get-tuple-element.108, f32[8,16,256]{2,1,0:T(8,128)} %get-tuple-element.107, f32[8,16,256]{2,1,0:T(8,128)} %get-tuple-element.106, ...), kind=kLoop, calls=%fused_computation.230 | loop fusion | flops 24772608 | bytes 23592960 | tf_op jit(solution)/shard_map/sub | solution.py:62
  101.9 0.1 slice_bitcast_fusion.11
  102.0 37.3 %fusion.25 = f32[8,16,6,256]{2,3,1,0:T(8,128)S(1)} fusion(f32[8,16,6,256]{2,3,1,0:T(8,128)} %copy.72, bf16[1,8,16,6,256]{3,4,2,1,0:T(8,128)(2,1)} %copy.71, bf16[1,8,16,6,256]{3,4,2,1,0:T(8,128)(2,1)} %copy.70, bf16[1,8,16,6,256]{3,4,2,1,0:T(8,128)(2,1)} %copy.69, bf16[1,8,16,6,256]{3,4,2,1,0:T(8,128)(2,1)} %copy.68, bf16[1,8,16,6,256]{3,4,2,1,0:T(8,128)(2,1)} %copy.67, ...), kind=kLoop, calls=%fused_computation.68 | loop fusion | flops 3538944 | bytes 4718592 | tf_op jit(solution)/shard_map/add | solution.py:63
  139.3 5.7 copy-done.1
  145.0 1.1 fusion.171
  146.1 204.0 %slice_reduce_fusion.5 = (f32[8,16,256]{2,1,0:T(8,128)S(1)}, f32[8,16,256]{2,1,0:T(8,128)}, f32[8,16,256]{2,1,0:T(8,128)}, f32[8,16,256]{2,1,0:T(8,128)}, f32[8,...) fusion(f32[8,16,6,256]{2,3,1,0:T(8,128)} %copy-done.1), kind=kLoop, calls=%fused_computation.108 | loop fusion | bytes 119799808 | tf_op jit(solution)/shard_map/slice | solution.py:34
  350.1 2.2 copy.77
  352.2 1.9 collective-permute-start.6
  354.2 4.7 fusion.170
  358.8 2.9 copy.73
  361.7 0.0 collective-permute-start.4
  361.7 2.9 copy.75
  364.6 5.7 collective-permute-start.5
  370.2 0.9 copy.79
  371.2 3.6 collective-permute-start.7
  374.8 0.0 collective-permute-done.6
  374.8 1.2 copy.78
  375.9 58.9 %fusion.45 = (f32[8,16,256]{2,1,0:T(8,128)}, f32[8,16,256]{2,1,0:T(8,128)}, f32[8,16,256]{2,1,0:T(8,128)}, f32[8,16,256]{2,1,0:T(8,128)}, f32[8,16,256]{2,1,0:T(8,128)}, /*index=5*/f32[8,16,256]{2,1,0:T(8,128)}) fusion(f32[8,1,6,256]{2,3,1,0:T(8,128)S(1)} %copy.78, f32[8,16,6,256]{2,3,1,0:T(8,128)} %copy-done.1), kind=kLoop, calls=%fused_computation.88 | loop fusion | flops 196608 | bytes 1622016 | tf_op jit(solution)/shard_map/slice | solution.py:34
  434.9 1.2 copy.80
  436.0 68.3 %fusion.35 = (f32[8,16,256]{2,1,0:T(8,128)}, f32[8,16,256]{2,1,0:T(8,128)}, f32[8,16,256]{2,1,0:T(8,128)}, f32[8,16,256]{2,1,0:T(8,128)}, f32[8,16,256]{2,1,0:T(8,128)}, /*index=5*/f32[8,16,256]{2,1,0:T(8,128)}) fusion(f32[8,1,6,256]{2,3,1,0:T(8,128)S(1)} %copy.80, f32[8,16,6,256]{2,3,1,0:T(8,128)} %copy-done.1), kind=kLoop, calls=%fused_computation.78 | loop fusion | flops 196608 | bytes 1622016 | tf_op jit(solution)/shard_map/slice | solution.py:34
  504.3 2.9 copy.74
  507.2 60.7 %fusion.13 = (f32[8,16,256]{2,1,0:T(8,128)}, f32[8,16,256]{2,1,0:T(8,128)}, f32[8,16,256]{2,1,0:T(8,128)}, f32[8,16,256]{2,1,0:T(8,128)}, f32[8,16,256]{2,1,0:T(8,128)}, /*index=5*/f32[8,16,256]{2,1,0:T(8,128)}) fusion(f32[8,16,6,256]{2,3,1,0:T(8,128)} %copy-done.1, f32[1,16,6,256]{2,3,1,0:T(8,128)} %copy.74), kind=kLoop, calls=%fused_computation.56 | loop fusion | flops 196608 | bytes 1671168 | tf_op jit(solution)/shard_map/slice | solution.py:34
  567.9 2.9 copy.76
  570.8 67.6 %fusion.3 = (f32[8,16,256]{2,1,0:T(8,128)S(1)}, f32[8,16,256]{2,1,0:T(8,128)S(1)}, f32[8,16,256]{2,1,0:T(8,128)S(1)}, f32[8,16,256]{2,1,0:T(8,128)S(1)}, f32[8,1...) fusion(f32[8,16,6,256]{2,3,1,0:T(8,128)} %copy-done.1, f32[1,16,6,256]{2,3,1,0:T(8,128)} %copy.76), kind=kLoop, calls=%fused_computation.46 | loop fusion | flops 196608 | bytes 1671168 | tf_op jit(solution)/shard_map/slice | solution.py:34
  638.5 11.4 %fusion.81 = f32[8,16,6,256]{3,1,2,0:T(8,128)S(1)} fusion(f32[8,16,6,256]{3,1,2,0:T(8,128)S(1)} %copy-done.4, f32[8,16,256]{2,1,0:T(8,128)} %get-tuple-element.45, f32[8,16,256]{2,1,0:T(8,128)} %get-tuple-element.44, f32[8,16,256]{2,1,0:T(8,128)} %get-tuple-element.43, f32[8,16,256]{2,1,0:T(8,128)} %get-tuple-element.42, ...), kind=kLoop, calls=%fused_computation.242 | loop fusion | flops 24772608 | bytes 23592960 | tf_op jit(solution)/shard_map/sub | solution.py:62
  649.9 0.1 slice_bitcast_fusion.5
  650.0 0.0 copy-start.16
  650.0 37.8 %fusion.31 = f32[8,16,6,256]{2,3,1,0:T(8,128)} fusion(f32[8,16,6,256]{2,3,1,0:T(8,128)S(1)} %bitcast.308, bf16[1,8,16,6,256]{3,4,2,1,0:T(8,128)(2,1)} %copy.71, bf16[1,8,16,6,256]{3,4,2,1,0:T(8,128)(2,1)} %copy.70, bf16[1,8,16,6,256]{3,4,2,1,0:T(8,128)(2,1)} %copy.69, bf16[1,8,16,6,256]{3,4,2,1,0:T(8,128)(2,1)} %copy.68, ...), kind=kLoop, calls=%fused_computation.74 | loop fusion | flops 3538944 | bytes 4718592 | tf_op jit(solution)/shard_map/add | solution.py:63
  687.8 4.7 gather_fusion
  692.5 4.3 fusion.56
  696.9 0.2 fusion.155
  697.1 0.1 collective-permute-start.8
  697.2 10.8 %copy.81 = f32[8,16,6,256]{3,1,2,0:T(8,128)} copy(f32[8,16,6,256]{2,3,1,0:T(8,128)} %fusion.31) | data formatting | bytes 1572864
  708.0 6.6 psum.7
  714.6 0.6 constant_dynamic-slice_fusion
  (46 shorter events, 0.1 us)
Async XLA Ops:
  0.6 691.9 %copy-start = (f32[512,6,128]{2,0,1:T(8,128)S(1)}, f32[512,6,128]{2,0,1:T(8,128)}, u32[]{:S(2)}) copy-start(f32[512,6,128]{2,0,1:T(8,128)} %param.15) | copy-start | bytes 4718596
  2.4 76.8 %collective-permute-start = (f32[1,16,6,256]{3,1,2,0:T(8,128)}, f32[1,16,6,256]{3,1,2,0:T(8,128)}, u32[]{:S(2)}, u32[]{:S(2)}) collective-permute-start(f32[1,16,6,256]{3,1,2,0:T(8,128)} %get-tuple-element.119), channel_id=1, source_target_pairs={{0,4},{4,8},{8,12},{12,16},{16,20},{20,24},{24,28},{28,32},{32,36}... | collective-permute-start | bytes 294920 | tf_op jit(solution)/shard_map/ppermute | solution.py:18
  6.3 76.2 %collective-permute-start.3 = (f32[8,1,6,256]{3,1,2,0:T(1,128)}, f32[8,1,6,256]{3,1,2,0:T(1,128)}, u32[]{:S(2)}, u32[]{:S(2)}) collective-permute-start(f32[8,1,6,256]{3,1,2,0:T(1,128)} %get-tuple-element.122), channel_id=1, source_target_pairs={{1,0},{2,1},{3,2},{5,4},{6,5},{7,6},{9,8},{10,9},{11,10},{13,12},{... | collective-permute-start | bytes 147464 | tf_op jit(solution)/shard_map/ppermute | solution.py:20
  9.2 77.1 %collective-permute-start.1 = (f32[1,16,6,256]{3,1,2,0:T(8,128)}, f32[1,16,6,256]{3,1,2,0:T(8,128)}, u32[]{:S(2)}, u32[]{:S(2)}) collective-permute-start(f32[1,16,6,256]{3,1,2,0:T(8,128)} %get-tuple-element.120), channel_id=1, source_target_pairs={{4,0},{8,4},{12,8},{16,12},{20,16},{24,20},{28,24},{32,28},{36,32}... | collective-permute-start | bytes 294920 | tf_op jit(solution)/shard_map/ppermute | solution.py:20
  14.8 62.7 %collective-permute-start.2 = (f32[8,1,6,256]{3,1,2,0:T(1,128)}, f32[8,1,6,256]{3,1,2,0:T(1,128)}, u32[]{:S(2)}, u32[]{:S(2)}) collective-permute-start(f32[8,1,6,256]{3,1,2,0:T(1,128)} %get-tuple-element.121), channel_id=1, source_target_pairs={{0,1},{1,2},{2,3},{4,5},{5,6},{6,7},{8,9},{9,10},{10,11},{12,13},{... | collective-permute-start | bytes 147464 | tf_op jit(solution)/shard_map/ppermute | solution.py:18
  49.3 28.2 %copy-start.2 = (f32[8,16,6,256]{3,1,2,0:T(8,128)S(1)}, f32[8,16,6,256]{3,1,2,0:T(8,128)}, u32[]{:S(2)}) copy-start(f32[8,16,6,256]{3,1,2,0:T(8,128)} %param.9) | copy-start | bytes 2359300
  55.4 34.9 %copy-start.4 = (f32[8,16,6,256]{3,1,2,0:T(8,128)S(1)}, f32[8,16,6,256]{3,1,2,0:T(8,128)}, u32[]{:S(2)}) copy-start(f32[8,16,6,256]{3,1,2,0:T(8,128)} %param.8) | copy-start | bytes 2359300
  55.4 34.9 %copy-start.14 = (f32[8,16,256]{2,1,0:T(8,128)S(1)}, f32[8,16,256]{2,1,0:T(8,128)}, u32[]{:S(2)}) copy-start(f32[8,16,256]{2,1,0:T(8,128)} %get-tuple-element.99) | copy-start | bytes 393220
  55.4 34.9 %copy-start.15 = (f32[8,16,256]{2,1,0:T(8,128)S(1)}, f32[8,16,256]{2,1,0:T(8,128)}, u32[]{:S(2)}) copy-start(f32[8,16,256]{2,1,0:T(8,128)} %get-tuple-element.100) | copy-start | bytes 393220
  81.6 1.0 copy-start.5
  139.2 5.7 copy-start.1
  352.2 22.5 %collective-permute-start.6 = (f32[8,1,6,256]{3,0,2,1:T(8,128)}, f32[8,1,6,256]{3,0,2,1:T(8,128)}, u32[]{:S(2)}, u32[]{:S(2)}) collective-permute-start(f32[8,1,6,256]{3,0,2,1:T(8,128)} %copy.77), channel_id=1, source_target_pairs={{0,1},{1,2},{2,3},{4,5},{5,6},{6,7},{8,9},{9,10},{10,11},{12,13},{... | collective-permute-start | bytes 147464 | tf_op jit(solution)/shard_map/ppermute | solution.py:18
  361.7 142.6 %collective-permute-start.4 = (f32[1,16,6,256]{3,1,2,0:T(8,128)}, f32[1,16,6,256]{3,1,2,0:T(8,128)}, u32[]{:S(2)}, u32[]{:S(2)}) collective-permute-start(f32[1,16,6,256]{3,1,2,0:T(8,128)} %copy.73), channel_id=1, source_target_pairs={{0,4},{4,8},{8,12},{12,16},{16,20},{20,24},{24,28},{28,32},{32,36}... | collective-permute-start | bytes 294920 | tf_op jit(solution)/shard_map/ppermute | solution.py:18
  364.6 203.3 %collective-permute-start.5 = (f32[1,16,6,256]{3,1,2,0:T(8,128)}, f32[1,16,6,256]{3,1,2,0:T(8,128)}, u32[]{:S(2)}, u32[]{:S(2)}) collective-permute-start(f32[1,16,6,256]{3,1,2,0:T(8,128)} %copy.75), channel_id=1, source_target_pairs={{4,0},{8,4},{12,8},{16,12},{20,16},{24,20},{28,24},{32,28},{36,32}... | collective-permute-start | bytes 294920 | tf_op jit(solution)/shard_map/ppermute | solution.py:20
  371.2 63.7 %collective-permute-start.7 = (f32[8,1,6,256]{3,0,2,1:T(8,128)}, f32[8,1,6,256]{3,0,2,1:T(8,128)}, u32[]{:S(2)}, u32[]{:S(2)}) collective-permute-start(f32[8,1,6,256]{3,0,2,1:T(8,128)} %copy.79), channel_id=1, source_target_pairs={{1,0},{2,1},{3,2},{5,4},{6,5},{7,6},{9,8},{10,9},{11,10},{13,12},{... | collective-permute-start | bytes 147464 | tf_op jit(solution)/shard_map/ppermute | solution.py:20
  507.2 131.2 %copy-start.6 = (f32[8,16,256]{2,1,0:T(8,128)S(1)}, f32[8,16,256]{2,1,0:T(8,128)}, u32[]{:S(2)}) copy-start(f32[8,16,256]{2,1,0:T(8,128)} %get-tuple-element.35) | copy-start | bytes 393220
  507.2 131.2 %copy-start.7 = (f32[8,16,256]{2,1,0:T(8,128)S(1)}, f32[8,16,256]{2,1,0:T(8,128)}, u32[]{:S(2)}) copy-start(f32[8,16,256]{2,1,0:T(8,128)} %get-tuple-element.36) | copy-start | bytes 393220
  570.8 67.6 %copy-start.3 = (bf16[6,8,16,6,256]{4,2,3,1,0:T(8,128)(2,1)S(1)}, bf16[6,8,16,6,256]{4,2,3,1,0:T(8,128)(2,1)}, u32[]{:S(2)}) copy-start(bf16[6,8,16,6,256]{4,2,3,1,0:T(8,128)(2,1)} %param.11) | copy-start | bytes 7077892
  570.8 67.7 %copy-start.8 = (f32[8,16,256]{2,1,0:T(8,128)S(1)}, f32[8,16,256]{2,1,0:T(8,128)}, u32[]{:S(2)}) copy-start(f32[8,16,256]{2,1,0:T(8,128)} %get-tuple-element.10) | copy-start | bytes 393220
  570.8 67.7 %copy-start.9 = (f32[8,16,256]{2,1,0:T(8,128)S(1)}, f32[8,16,256]{2,1,0:T(8,128)}, u32[]{:S(2)}) copy-start(f32[8,16,256]{2,1,0:T(8,128)} %get-tuple-element.11) | copy-start | bytes 393220
  570.8 67.7 %copy-start.10 = (f32[8,16,256]{2,1,0:T(8,128)S(1)}, f32[8,16,256]{2,1,0:T(8,128)}, u32[]{:S(2)}) copy-start(f32[8,16,256]{2,1,0:T(8,128)} %get-tuple-element.12) | copy-start | bytes 393220
  570.8 67.7 %copy-start.11 = (f32[8,16,256]{2,1,0:T(8,128)S(1)}, f32[8,16,256]{2,1,0:T(8,128)}, u32[]{:S(2)}) copy-start(f32[8,16,256]{2,1,0:T(8,128)} %get-tuple-element.13) | copy-start | bytes 393220
  570.8 67.7 %copy-start.12 = (f32[8,16,256]{2,1,0:T(8,128)S(1)}, f32[8,16,256]{2,1,0:T(8,128)}, u32[]{:S(2)}) copy-start(f32[8,16,256]{2,1,0:T(8,128)} %get-tuple-element.14) | copy-start | bytes 393220
  570.8 67.7 %copy-start.13 = (f32[8,16,256]{2,1,0:T(8,128)S(1)}, f32[8,16,256]{2,1,0:T(8,128)}, u32[]{:S(2)}) copy-start(f32[8,16,256]{2,1,0:T(8,128)} %get-tuple-element.15) | copy-start | bytes 393220
  570.8 79.1 %slice-start = ((s8[16777216]{0:T(1024)(128)(4,1)}), s8[4194304]{0:T(1024)(128)(4,1)S(1)}, s32[]{:S(2)}) async-start(s8[16777216]{0:T(1024)(128)(4,1)} %bitcast.307), calls=%async_computation | async-start | bytes 8388608
  570.8 79.1 %slice-start.1 = ((s8[16777216]{0:T(1024)(128)(4,1)}), s8[4194304]{0:T(1024)(128)(4,1)S(1)}, s32[]{:S(2)}) async-start(s8[16777216]{0:T(1024)(128)(4,1)} %bitcast.307), calls=%async_computation.1 | async-start | bytes 8388608
  638.5 11.5 %slice-start.2 = ((s8[16777216]{0:T(1024)(128)(4,1)}), s8[4194304]{0:T(1024)(128)(4,1)S(1)}, s32[]{:S(2)}) async-start(s8[16777216]{0:T(1024)(128)(4,1)} %bitcast.307), calls=%async_computation.2 | async-start | bytes 8388608
  638.5 11.5 %slice-start.3 = ((s8[16777216]{0:T(1024)(128)(4,1)}), s8[4194304]{0:T(1024)(128)(4,1)S(1)}, s32[]{:S(2)}) async-start(s8[16777216]{0:T(1024)(128)(4,1)} %bitcast.307), calls=%async_computation.3 | async-start | bytes 8388608
  650.0 46.9 %copy-start.16 = (s32[512]{0:T(512)S(1)}, s32[512]{0:T(512)}, u32[]{:S(2)}) copy-start(s32[512]{0:T(512)} %param.14) | copy-start | bytes 6148
  697.1 10.9 %collective-permute-start.8 = (f32[1,128]{1,0:T(1,128)S(1)}, f32[1,128]{1,0:T(1,128)S(1)}, u32[]{:S(2)}, u32[]{:S(2)}) collective-permute-start(f32[1,128]{1,0:T(1,128)S(1)} %slice.839), channel_id=1, source_target_pairs={{124,0},{0,4},{4,8},{8,12},{12,16},{16,20},{20,24},{24,28},{28,32}... | collective-permute-start | bytes 1544 | tf_op jit(solution)/shard_map/ppermute | solution.py:30
where the time goes:
time: 725 us; the launch traced here: 715 us
  other arithmetic  356 us (49%)
  local copies, waits for them, and re-layouts  320 us (44%)
  starting transfers between devices  27.2 us (4%)
    slice x4, other arithmetic, block_apply(): summed = blocks[0].astype(jnp.float32) * vector[:, :, 0:1, :]  255 us
    slice x3, local copies, waits for them, and re-layouts, block_apply(): summed = blocks[0].astype(jnp.float32) * vector[:, :, 0:1, :]  213 us
    add x2, other arithmetic, body(): adjoint = adjoint + block_apply(precond, residual)  75.1 us
    slice x5, local copies, waits for them, and re-layouts, block_apply(): blocks[column].astype(jnp.float32) * vector[:, :, column:column + 1, :]  34.3 us
    unnamed x45, local copies, waits for them, and re-layouts  28.4 us
    sub x2, other arithmetic, body(): residual = objective_grad - applied  22.9 us
    ppermute x4, starting transfers between devices, extended(): lax.ppermute(head, axis, [((i + 1) % count, i) for i in range(ends)])  17.7 us
  transfers between devices with their start and end apart: 9, of which 0 were waited for; matrix products, arithmetic and copies ran while one was open for 39% of the time, Pallas kernels for 0%

commit v1 on v0

v1 whole, which is shorter than its diff:
```python
import functools

import jax
import jax.numpy as jnp
from jax import lax
from jax.experimental import pallas as pl
from jax.experimental.pallas import tpu as pltpu
from jax.sharding import PartitionSpec as P

F32 = jnp.float32
HIGH = lax.Precision.HIGHEST


def _vmem():
    return pl.BlockSpec(memory_space=pltpu.VMEM)


def _smem():
    return pl.BlockSpec(memory_space=pltpu.SMEM)


def _whole(shape):
    return pl.BlockSpec(shape, lambda t: (0,) * len(shape))


def send_faces(adj, even_ref, odd_ref, near_ref, far_ref):
    nt, nv, nq, _ = adj.shape
    c = lax.axis_index("circ")
    r = lax.axis_index("radax")
    t_even = jnp.where(c % 2 == 0, nt - 1, 0)
    even_ref[...] = adj[t_even]
    odd_ref[...] = adj[nt - 1 - t_even]
    up = r % 2 == 0
    for t in range(nt):
        for i in range(nv):
            low = adj[t, i, 0:1, :]
            high = adj[t, i, nq - 1 : nq, :]
            near_ref[i, t : t + 1, :] = jnp.where(up, high, low)
            far_ref[i, t : t + 1, :] = jnp.where(up, low, high)


def faces_kernel(adj_ref, even_ref, odd_ref, near_ref, far_ref):
    send_faces(adj_ref, even_ref, odd_ref, near_ref, far_ref)


def shift_lanes(plane, step):
    width = plane.shape[1]
    lane = lax.broadcasted_iota(jnp.int32, plane.shape, 1)
    edge = 0 if step == 1 else width - 1
    return jnp.where(lane == edge, 0.0, pltpu.roll(plane, step % width, 1))


def shift_rows(plane, step):
    rows = plane.shape[0]
    row = lax.broadcasted_iota(jnp.int32, plane.shape, 0)
    edge = 0 if step == 1 else rows - 1
    return jnp.where(row == edge, 0.0, pltpu.roll(plane, step % rows, 0))


def local_kernel(keep_edges, adj_ref, g_ref, off_ref, diag_ref, pre_ref, out_ref, *edge_refs):
    t = pl.program_id(0)
    nt, nv, nq, _ = adj_ref.shape
    below = jnp.maximum(t - 1, 0)
    above = jnp.minimum(t + 1, nt - 1)
    has_below = (t > 0).astype(F32)
    has_above = (t < nt - 1).astype(F32)
    acc = [g_ref[0, i] for i in range(nv)]
    for j in range(nv):
        here = adj_ref[t, j]
        fields = [
            adj_ref[below, j] * has_below,
            adj_ref[above, j] * has_above,
            shift_rows(here, 1),
            shift_rows(here, -1),
            shift_lanes(here, 1),
            shift_lanes(here, -1),
        ]
        for i in range(nv):
            acc[i] = acc[i] - diag_ref[j, 0, i].astype(F32) * here
        for k in range(6):
            for i in range(nv):
                block = off_ref[k, j, 0, i].astype(F32)
                acc[i] = acc[i] - block * fields[k]
                if keep_edges and k == 2:
                    edge_refs[0][j, i, pl.ds(t, 1), :] = block[0:1, :]
                if keep_edges and k == 3:
                    edge_refs[1][j, i, pl.ds(t, 1), :] = block[nq - 1 : nq, :]
    new = [adj_ref[t, i] for i in range(nv)]
    for j in range(nv):
        for i in range(nv):
            block = pre_ref[j, 0, i].astype(F32)
            new[i] = new[i] + block * acc[j]
            if keep_edges:
                edge_refs[2][j, i, pl.ds(t, 1), :] = block[0:1, :]
                edge_refs[3][j, i, pl.ds(t, 1), :] = block[nq - 1 : nq, :]
    for i in range(nv):
        out_ref[0, i] = new[i]


def local_part(adj, g, off, diag, pre, keep_edges):
    nt, nv, nq, na = adj.shape
    layer = pl.BlockSpec((1, nv, nq, na), lambda t: (t, 0, 0, 0))
    blocks = pl.BlockSpec((nv, 1, nv, nq, na), lambda t: (0, t, 0, 0, 0))
    out_shape = [jax.ShapeDtypeStruct(adj.shape, F32)]
    out_specs = [layer]
    if keep_edges:
        edge = (nv, nv, nt, na)
        out_shape += [jax.ShapeDtypeStruct(edge, F32)] * 4
        out_specs += [_whole(edge)] * 4
    return pl.pallas_call(
        functools.partial(local_kernel, keep_edges),
        grid=(nt,),
        in_specs=[
            _whole(adj.shape),
            layer,
            pl.BlockSpec((6, nv, 1, nv, nq, na), lambda t: (0, 0, t, 0, 0, 0)),
            blocks,
            blocks,
        ],
        out_specs=out_specs,
        out_shape=out_shape,
        compiler_params=pltpu.CompilerParams(vmem_limit_bytes=24 << 20),
        cost_estimate=pl.CostEstimate(flops=40_000_000, bytes_accessed=24_000_000, transcendentals=0),
        name="local_first" if keep_edges else "local_second",
    )(adj, g, off, diag, pre)


def apply_blocks(load, vectors):
    nv = len(vectors)
    out = []
    for i in range(nv):
        total = load(0, i) * vectors[0]
        for j in range(1, nv):
            total = total + load(j, i) * vectors[j]
        out.append(total)
    return out


def add_halos(adj_ref, even, odd, near, far, off_low, off_up, pre_first, pre_last, edges, out_ref):
    nt, nv, nq, _ = adj_ref.shape
    c = lax.axis_index("circ")
    r = lax.axis_index("radax")
    c_even = c % 2 == 0
    r_even = r % 2 == 0
    out_ref[...] = adj_ref[...]
    for t, low in ((0, True), (nt - 1, False)):
        off, pre = (off_low, pre_first) if low else (off_up, pre_last)
        pick = jnp.logical_not(c_even) if low else c_even
        halo = [jnp.where(pick, even[j], odd[j]) for j in range(nv)]
        extra = apply_blocks(lambda j, i: off[0, j, 0, i].astype(F32), halo)
        change = apply_blocks(lambda j, i: pre[j, 0, i].astype(F32), extra)
        for i in range(nv):
            out_ref[t, i] = out_ref[t, i] - change[i]
    last = lax.axis_size("radax") - 1
    for q, low in ((0, True), (nq - 1, False)):
        off, pre = (edges[0], edges[2]) if low else (edges[1], edges[3])
        pick = jnp.logical_not(r_even) if low else r_even
        inside = (r > 0) if low else (r < last)
        halo = [jnp.where(inside, jnp.where(pick, near[j], far[j]), 0.0) for j in range(nv)]
        extra = apply_blocks(lambda j, i: off[j, i], halo)
        change = apply_blocks(lambda j, i: pre[j, i], extra)
        for t in range(nt):
            for i in range(nv):
                out_ref[t, i, q : q + 1, :] = out_ref[t, i, q : q + 1, :] - change[i][t : t + 1, :]


def halo_kernel(adj_ref, even, odd, near, far, off_low, off_up, pre_first, pre_last, e0, e1, e2, e3,
                out_ref, even_out, odd_out, near_out, far_out):
    add_halos(adj_ref, even, odd, near, far, off_low, off_up, pre_first, pre_last, (e0, e1, e2, e3), out_ref)
    send_faces(out_ref, even_out, odd_out, near_out, far_out)


def final_kernel(adj_ref, even, odd, near, far, off_low, off_up, pre_first, pre_last, e0, e1, e2, e3,
                 cell_ref, side_ref, design_ref, out_ref, lower_ref, upper_ref, by_cell, picked):
    add_halos(adj_ref, even, odd, near, far, off_low, off_up, pre_first, pre_last, (e0, e1, e2, e3), out_ref)
    nt, nv, nq, na = adj_ref.shape
    halves = na // 128
    for t in range(nt):
        for i in range(nv):
            for qt in range(nq // 8):
                for h in range(halves):
                    first = ((t * nq + qt * 8) * halves + h) * 8 + i
                    by_cell[pl.ds(first, 8, stride=8 * halves), :] = out_ref[
                        t, i, qt * 8 : qt * 8 + 8, h * 128 : h * 128 + 128
                    ]
    faces = design_ref.shape[1]
    lane = lax.broadcasted_iota(jnp.int32, (8, 128), 1)

    def pick(f, carry):
        cell = cell_ref[f]
        row = pl.multiple_of((cell // 128) * 8, 8)
        tile = by_cell[pl.ds(row, 8), :]
        kept = jnp.where(lane == cell % 128, tile, 0.0)
        picked[pl.ds(f, 8, stride=faces), :] = kept
        return carry

    lax.fori_loop(0, faces, pick, 0, unroll=16)
    total = jnp.zeros((8, 128), F32)
    sides = lax.broadcasted_iota(jnp.int32, (8, 128), 0)
    for f0 in range(0, faces, 128):
        contrib = jnp.zeros((128, 128), F32)
        for i in range(nv):
            value = jnp.sum(picked[i * faces + f0 : i * faces + f0 + 128, :], axis=1, keepdims=True)
            contrib = contrib + value * design_ref[i, f0 : f0 + 128, :]
        table = (side_ref[f0 // 128 : f0 // 128 + 1, :] == sides).astype(F32)
        total = total + jnp.dot(table, contrib, precision=HIGH, preferred_element_type=F32)
    lower_ref[...] = total[0:1, :]
    upper_ref[...] = total[1:2, :]


def halo_part(adj, halos, off, pre, edges, faces=None):
    nt, nv, nq, na = adj.shape
    one = (1, nv, 1, nv, nq, na)
    layer = (nv, 1, nv, nq, na)
    in_specs = [_whole(adj.shape)] + [_whole(h.shape) for h in halos]
    in_specs += [
        pl.BlockSpec(one, lambda s: (0, 0, 0, 0, 0, 0)),
        pl.BlockSpec(one, lambda s: (1, 0, nt - 1, 0, 0, 0)),
        pl.BlockSpec(layer, lambda s: (0, 0, 0, 0, 0)),
        pl.BlockSpec(layer, lambda s: (0, nt - 1, 0, 0, 0)),
    ]
    in_specs += [_whole(e.shape) for e in edges]
    args = [adj, *halos, off, off, pre, pre, *edges]
    params = pltpu.CompilerParams(vmem_limit_bytes=24 << 20)
    cost = pl.CostEstimate(flops=4_000_000, bytes_accessed=5_000_000, transcendentals=0)
    if faces is None:
        out_shape = [jax.ShapeDtypeStruct(adj.shape, F32)]
        out_shape += [jax.ShapeDtypeStruct(h.shape, F32) for h in halos]
        return pl.pallas_call(
            halo_kernel, grid=(1,), in_specs=in_specs,
            out_specs=[_whole(o.shape) for o in out_shape], out_shape=out_shape,
            compiler_params=params, cost_estimate=cost, name="halo_first",
        )(*args)
    cell, side, design = faces
    ndv = design.shape[2]
    out_shape = [jax.ShapeDtypeStruct(adj.shape, F32)] + [jax.ShapeDtypeStruct((1, ndv), F32)] * 2
    return pl.pallas_call(
        final_kernel, grid=(1,),
        in_specs=in_specs + [_smem(), _whole(side.shape), _whole(design.shape)],
        out_specs=[_whole(o.shape) for o in out_shape], out_shape=out_shape,
        scratch_shapes=[
            pltpu.VMEM((nt * nq * na // 128 * 8, 128), F32),
            pltpu.VMEM((8 * design.shape[1], 128), F32),
        ],
        compiler_params=params, cost_estimate=cost, name="halo_last",
    )(*args, cell, side, design)


def swap_halos(even, odd, near, far):
    nc = lax.axis_size("circ")
    nr = lax.axis_size("radax")
    odd = lax.ppermute(odd, "circ", [(i, (i + 1) % nc if i % 2 else (i - 1) % nc) for i in range(nc)])
    far = lax.ppermute(far, "radax", [(i, nr - 1 - i) for i in range(nr)])
    even = lax.ppermute(even, "circ", [(i, i ^ 1) for i in range(nc)])
    near = lax.ppermute(near, "radax", [(i, i ^ 1) for i in range(nr)])
    return even, odd, near, far


def body(objective_grad, adjoint_start, jac_off, jac_diag, precond, face_cell, face_side, design_grad):
    g = objective_grad.transpose(0, 2, 1, 3)
    adj = adjoint_start.transpose(0, 2, 1, 3)
    off = jac_off.transpose(0, 1, 2, 4, 3, 5)
    diag = jac_diag.transpose(0, 1, 3, 2, 4)
    pre = precond.transpose(0, 1, 3, 2, 4)
    design = design_grad.transpose(1, 0, 2)
    nt, nv, nq, na = adj.shape
    ring = jax.ShapeDtypeStruct((nv, nq, na), F32)
    rows = jax.ShapeDtypeStruct((nv, nt, na), F32)
    sends = pl.pallas_call(
        faces_kernel, in_specs=[_vmem()], out_specs=[_vmem()] * 4,
        out_shape=[ring, ring, rows, rows], name="faces",
    )(adj)
    halos = swap_halos(*sends)
    part, *edges = local_part(adj, g, off, diag, pre, True)
    adj, *sends = halo_part(part, halos, off, pre, edges)
    halos = swap_halos(*sends)
    (part,) = local_part(adj, g, off, diag, pre, False)
    side = face_side.reshape(-1, 128)
    adj, lower, upper = halo_part(part, halos, off, pre, edges, (face_cell, side, design))
    nc = lax.axis_size("circ")
    nr = lax.axis_size("radax")
    total = lower + lax.ppermute(upper, "circ", [(i, (i + 1) % nc) for i in range(nc)])
    total = total + lax.ppermute(total, "radax", [(i, i ^ 1) for i in range(nr)])
    total = total + lax.ppermute(total, "radax", [(i, i ^ 2) for i in range(nr)])
    owned = total.shape[1] // nr
    sensitivity = lax.dynamic_slice_in_dim(total, lax.axis_index("radax") * owned, owned, 1)
    return adj.transpose(0, 2, 1, 3), sensitivity


def solution(mesh):
    in_specs = (
        P("circ", "radax", None, None),
        P("circ", "radax", None, None),
        P(None, None, "circ", "radax", None, None),
        P(None, "circ", "radax", None, None),
        P(None, "circ", "radax", None, None),
        P(("circ", "radax")),
        P(("circ", "radax")),
        P(("circ", "radax"), None, None),
    )
    out_specs = (P("circ", "radax", None, None), P("circ", "radax"))
    return jax.shard_map(body, mesh=mesh, in_specs=in_specs, out_specs=out_specs, check_vma=False)
```

time: 725 us -> 62.2 us (0.09); the launches traced: 715 us -> 61.7 us
  other arithmetic: 356 us -> 0.01 us
  local copies, waits for them, and re-layouts: 320 us -> 11.2 us
  Pallas kernels: 0 us -> 20.5 us
  waiting for transfers between devices: 0.02 us -> 11.4 us
  starting transfers between devices: 27.2 us -> 17.8 us
    slice x17 -> x0, local copies, waits for them, and re-layouts: 265 us -> none  [the longest x3 213 us: block_apply(): summed = blocks[0].astype(jnp.float32) * vector[:, :, 0:1, :]]
    slice x4 -> x0, other arithmetic: 255 us -> none  [block_apply(): summed = blocks[0].astype(jnp.float32) * vector[:, :, 0:1, :]]
    add x3, other arithmetic: 75.1 us -> 0.01 us  [the longest x1 0.01 us: body(): lower + lax.ppermute(upper, 'circ', [(i, (i + 1) % nc) for i in range(nc)])]
    sub x2 -> x0, other arithmetic: 22.9 us -> none  [body(): residual = objective_grad - applied]
    pallas_call x0 -> x5, Pallas kernels: none -> 20.5 us  [the longest x2 11.5 us: local_part(): pl.pallas_call(functools.partial(local_kernel, keep_edges), grid=(nt,), i...]
    unnamed x45 -> x24, local copies, waits for them, and re-layouts: 28.4 us -> 10.7 us
    ppermute x9 -> x11, waiting for transfers between devices: 0.02 us -> 11.4 us  [the longest x1 6.64 us: body(): lax.ppermute(upper, 'circ', [(i, (i + 1) % nc) for i in range(nc)])]
    ppermute x9 -> x11, starting transfers between devices: 27.2 us -> 17.8 us  [the longest x2 6.41 us: swap_halos(): lax.ppermute(odd, 'circ', [(i, (i + 1) % nc if i % 2 else (i - 1) % nc) f...]
  transfers between devices with their start and end apart: 9 -> 11, of which waited for: 0 -> 3; matrix products, arithmetic and copies ran while one was open for 39% -> 0% of each run, Pallas kernels for 0% -> 19%
where the time goes in v1:
time: 62.2 us; the launch traced here: 61.7 us
  Pallas kernels  20.5 us (33%)
  starting transfers between devices  17.8 us (29%)
  waiting for transfers between devices  11.4 us (18%)
  local copies, waits for them, and re-layouts  11.2 us (18%)
  between operations  0.81 us (1%)
    pallas_call x2, Pallas kernels, local_part(): pl.pallas_call(functools.partial(local_kernel, keep_edges), grid=(nt,), i...  11.5 us
    unnamed x24, local copies, waits for them, and re-layouts  10.7 us
    pallas_call x1, Pallas kernels, halo_part(): pl.pallas_call(final_kernel, grid=(1,), in_specs=in_specs + [_smem(), _wh...  6.64 us
    ppermute x1, waiting for transfers between devices, body(): lax.ppermute(upper, 'circ', [(i, (i + 1) % nc) for i in range(nc)])  6.64 us
    ppermute x2, starting transfers between devices, swap_halos(): lax.ppermute(odd, 'circ', [(i, (i + 1) % nc if i % 2 else (i - 1) % nc) f...  6.41 us
    ppermute x2, starting transfers between devices, swap_halos(): far = lax.ppermute(far, 'radax', [(i, nr - 1 - i) for i in range(nr)])  3.96 us
    ppermute x1, waiting for transfers between devices, body(): lax.ppermute(total, 'radax', [(i, i ^ 2) for i in range(nr)])  3.88 us
    ppermute x1, starting transfers between devices, body(): lax.ppermute(total, 'radax', [(i, i ^ 1) for i in range(nr)])  2.87 us
  transfers between devices with their start and end apart: 11, of which 3 were waited for; matrix products, arithmetic and copies ran while one was open for 0% of the time, Pallas kernels for 19%

profile of v1, /device:TPU:1, one launch (start us, length us, event | category | flops | bytes accessed | tf_op | source)
XLA Modules:
  0.0 61.7 jit_solution(10351284383624663487)
XLA Ops:
  0.6 1.9 %faces.1 = (f32[6,16,256]{2,1,0:T(8,128)}, f32[6,16,256]{2,1,0:T(8,128)}, f32[6,8,256]{2,1,0:T(8,128)}, f32[6,8,256]{2,1,0:T(8,128)}) custom-call(f32[8,6,16,256]{3,2,1,0:T(8,128)} %bitcast.22), custom_call_target="tpu_custom_call" | custom-call | tf_op jit(solution)/shard_map/faces/pallas_call | solution.py:269
  2.5 2.1 %collective-permute-start = (f32[6,16,256]{2,1,0:T(8,128)}, f32[6,16,256]{2,1,0:T(8,128)S(1)}, u32[]{:S(2)}, u32[]{:S(2)}) collective-permute-start(f32[6,16,256]{2,1,0:T(8,128)} %get-tuple-element.20), channel_id=1, source_target_pairs={{0,4},{4,0},{8,12},{12,8},{16,20},{20,16},{24,28},{28,24},{32,36},... | collective-permute-start | bytes 294920 | tf_op jit(solution)/shard_map/ppermute | solution.py:254
  4.6 6.3 %collective-permute-start.1 = (f32[6,16,256]{2,1,0:T(8,128)}, f32[6,16,256]{2,1,0:T(8,128)S(1)}, u32[]{:S(2)}, u32[]{:S(2)}) collective-permute-start(f32[6,16,256]{2,1,0:T(8,128)} %get-tuple-element.21), channel_id=1, source_target_pairs={{0,124},{4,8},{8,4},{12,16},{16,12},{20,24},{24,20},{28,32},{32,28... | collective-permute-start | bytes 294920 | tf_op jit(solution)/shard_map/ppermute | solution.py:252
  10.9 1.2 %collective-permute-start.2 = (f32[6,8,256]{2,1,0:T(8,128)}, f32[6,8,256]{2,1,0:T(8,128)S(1)}, u32[]{:S(2)}, u32[]{:S(2)}) collective-permute-start(f32[6,8,256]{2,1,0:T(8,128)} %get-tuple-element.22), channel_id=1, source_target_pairs={{0,1},{1,0},{2,3},{3,2},{4,5},{5,4},{6,7},{7,6},{8,9},{9,8},{10,11... | collective-permute-start | bytes 147464 | tf_op jit(solution)/shard_map/ppermute | solution.py:255
  12.2 2.3 %collective-permute-start.3 = (f32[6,8,256]{2,1,0:T(8,128)}, f32[6,8,256]{2,1,0:T(8,128)S(1)}, u32[]{:S(2)}, u32[]{:S(2)}) collective-permute-start(f32[6,8,256]{2,1,0:T(8,128)} %get-tuple-element.23), channel_id=1, source_target_pairs={{0,3},{1,2},{2,1},{3,0},{4,7},{5,6},{6,5},{7,4},{8,11},{9,10},{10,... | collective-permute-start | bytes 147464 | tf_op jit(solution)/shard_map/ppermute | solution.py:253
  14.5 0.0 copy-start
  14.5 5.0 %copy-done = bf16[6,6,8,16,6,256]{5,3,4,2,1,0:T(8,128)(2,1)S(1)} copy-done((bf16[6,6,8,16,6,256]{5,3,4,2,1,0:T(8,128)(2,1)S(1)}, bf16[6,6,8,16,6,256]{5,3,4,2,1,0:T(8,128)(2,1)}, u32[]{:S(2)}) %copy-start) | copy-done | bytes 14155800
  19.5 0.0 copy-start.2
  19.5 1.7 %copy-done.2 = bf16[6,8,16,6,256]{4,2,3,1,0:T(8,128)(2,1)S(1)} copy-done((bf16[6,8,16,6,256]{4,2,3,1,0:T(8,128)(2,1)S(1)}, bf16[6,8,16,6,256]{4,2,3,1,0:T(8,128)(2,1)}, u32[]{:S(2)}) %copy-start.2) | copy-done | bytes 2359320
  21.2 0.0 copy-start.4
  21.2 1.7 %copy-done.4 = bf16[6,8,16,6,256]{4,2,3,1,0:T(8,128)(2,1)S(1)} copy-done((bf16[6,8,16,6,256]{4,2,3,1,0:T(8,128)(2,1)S(1)}, bf16[6,8,16,6,256]{4,2,3,1,0:T(8,128)(2,1)}, u32[]{:S(2)}) %copy-start.4) | copy-done | bytes 2359320
  22.9 0.0 copy-start.6
  22.9 1.1 %copy-done.6 = f32[8,16,6,256]{3,1,2,0:T(8,128)S(1)} copy-done((f32[8,16,6,256]{3,1,2,0:T(8,128)S(1)}, f32[8,16,6,256]{3,1,2,0:T(8,128)}, u32[]{:S(2)}) %copy-start.6) | copy-done | bytes 786456
  24.0 0.0 copy-start.7
  24.0 1.1 %copy-done.7 = f32[8,16,6,256]{3,1,2,0:T(8,128)S(1)} copy-done((f32[8,16,6,256]{3,1,2,0:T(8,128)S(1)}, f32[8,16,6,256]{3,1,2,0:T(8,128)}, u32[]{:S(2)}) %copy-start.7) | copy-done | bytes 786456
  25.1 0.0 copy-start.1
  25.1 0.0 copy-start.3
  25.1 6.0 %local_first.1 = (f32[8,6,16,256]{3,2,1,0:T(8,128)S(1)}, f32[6,6,8,256]{3,2,1,0:T(8,128)S(1)}, f32[6,6,8,256]{3,2,1,0:T(8,128)S(1)}, f32[6,6,8,256]{3,2,1,0:T(8,128)S(1)}, f32[6,6,8,256]{3,2,1,0:T(8,128)S(1)}) custom-call(f32[8,6,16,256]{3,2,1,0:T(8,128)S(1)} %bitcast.23, f32[8,6,16,256]{3,2,1,0:T(8,128)S(1)} %bitcast.24, ...), custom_call_target="tpu_custom_call" | custom-call | flops 40000000 | bytes 24000000 | tf_op jit(solution)/shard_map/local_first/pallas_call | solution.py:110
  31.2 0.0 collective-permute-done.2.near
  31.2 0.0 collective-permute-done.3.far
  31.2 0.0 collective-permute-done.even
  31.2 0.0 collective-permute-done.1.odd
  31.2 0.0 copy-done.1
  31.2 0.0 copy-done.3
  31.3 0.0 copy-start.5
  31.3 0.0 copy-start.8
  31.3 0.5 halo_first.1
  31.8 0.1 collective-permute-start.4
  31.9 0.1 collective-permute-start.5
  32.0 1.1 %collective-permute-start.6 = (f32[6,8,256]{2,1,0:T(8,128)S(1)}, f32[6,8,256]{2,1,0:T(8,128)S(1)}, u32[]{:S(2)}, u32[]{:S(2)}) collective-permute-start(f32[6,8,256]{2,1,0:T(8,128)S(1)} %get-tuple-element.31), channel_id=1, source_target_pairs={{0,1},{1,0},{2,3},{3,2},{4,5},{5,4},{6,7},{7,6},{8,9},{9,8},{10,11... | collective-permute-start | bytes 147464 | tf_op jit(solution)/shard_map/ppermute | solution.py:255
  33.1 1.6 %collective-permute-start.7 = (f32[6,8,256]{2,1,0:T(8,128)S(1)}, f32[6,8,256]{2,1,0:T(8,128)S(1)}, u32[]{:S(2)}, u32[]{:S(2)}) collective-permute-start(f32[6,8,256]{2,1,0:T(8,128)S(1)} %get-tuple-element.32), channel_id=1, source_target_pairs={{0,3},{1,2},{2,1},{3,0},{4,7},{5,6},{6,5},{7,4},{8,11},{9,10},{10,... | collective-permute-start | bytes 147464 | tf_op jit(solution)/shard_map/ppermute | solution.py:253
  34.7 0.0 copy-done.5
  34.7 0.0 copy-done.8
  34.7 0.0 copy-start.9
  34.7 0.0 copy-start.10
  34.7 0.0 copy-start.11
  34.7 5.4 %local_second.1.adj_ref = f32[8,6,16,256]{3,2,1,0:T(8,128)S(1)} custom-call(f32[8,6,16,256]{3,2,1,0:T(8,128)S(1)} %get-tuple-element.28.adj_ref, f32[8,6,16,256]{3,2,1,0:T(8,128)S(1)} %bitcast.25, bf16[6,6,8,6,16,256]{5,4,3,2,1,0:T(8,128)(2,1)S(1)} %bitcast.11, bf16[6,8,6,16,256]{4,3,2,1,0:T(8,128)(2,1)S(1)} %bitcast.21, bf16[6,8,6,16,256]{4,3,2,1,0:T(8,128)(2,1)S(1)} %bitcast.17), custom_call_target="tpu_custom_call" | custom-call | flops 40000000 | bytes 24000000 | tf_op jit(solution)/shard_map/local_second/pallas_call | solution.py:110
  40.2 0.0 collective-permute-done.6.near
  40.2 0.0 collective-permute-done.7.far
  40.2 0.0 collective-permute-done.4.even
  40.2 0.0 collective-permute-done.5.odd
  40.2 0.0 copy-done.9
  40.2 0.0 copy-done.10
  40.2 0.0 copy-done.11
  40.2 6.6 %halo_last.1 = (f32[8,6,16,256]{3,2,1,0:T(8,128)}, f32[1,128]{1,0:T(1,128)S(1)}, f32[1,128]{1,0:T(1,128)S(1)}) custom-call(f32[8,6,16,256]{3,2,1,0:T(8,128)S(1)} %local_second.1.adj_ref, f32[6,16,256]{2,1,0:T(8,128)S(1)} %collective-permute-done.4.even, f32[6,16,256]{2,1,0:T(8,128)S(1)} %collective-permute-done.5.odd, ...), custom_call_target="tpu_custom_call" | custom-call | flops 4000000 | bytes 5000000 | tf_op jit(solution)/shard_map/halo_last/pallas_call | solution.py:237
  46.9 0.0 collective-permute-start.8
  46.9 6.6 %collective-permute-done.8 = f32[1,128]{1,0:T(1,128)S(1)} collective-permute-done((f32[1,128]{1,0:T(1,128)S(1)}, f32[1,128]{1,0:T(1,128)S(1)}, u32[]{:S(2)}, u32[]{:S(2)}) %collective-permute-start.8) | collective-permute-done | bytes 544 | tf_op jit(solution)/shard_map/ppermute | solution.py:282
  53.5 2.9 %collective-permute-start.9 = (f32[1,128]{1,0:T(1,128)S(1)}, f32[1,128]{1,0:T(1,128)S(1)}, u32[]{:S(2)}, u32[]{:S(2)}) collective-permute-start(f32[1,128]{1,0:T(1,128)S(1)} %add.12), channel_id=1, source_target_pairs={{0,1},{1,0},{2,3},{3,2},{4,5},{5,4},{6,7},{7,6},{8,9},{9,8},{10,11... | collective-permute-start | bytes 1544 | tf_op jit(solution)/shard_map/ppermute | solution.py:283
  56.4 0.8 %collective-permute-done.9 = f32[1,128]{1,0:T(1,128)S(1)} collective-permute-done((f32[1,128]{1,0:T(1,128)S(1)}, f32[1,128]{1,0:T(1,128)S(1)}, u32[]{:S(2)}, u32[]{:S(2)}) %collective-permute-start.9) | collective-permute-done | bytes 544 | tf_op jit(solution)/shard_map/ppermute | solution.py:283
  57.2 0.0 collective-permute-start.10
  57.3 3.9 %collective-permute-done.10 = f32[1,128]{1,0:T(1,128)S(1)} collective-permute-done((f32[1,128]{1,0:T(1,128)S(1)}, f32[1,128]{1,0:T(1,128)S(1)}, u32[]{:S(2)}, u32[]{:S(2)}) %collective-permute-start.10) | collective-permute-done | bytes 544 | tf_op jit(solution)/shard_map/ppermute | solution.py:284
  61.1 0.6 constant_dynamic-slice_fusion
  (3 shorter events, 0.0 us)
Async XLA Ops:
  2.5 28.7 %collective-permute-start = (f32[6,16,256]{2,1,0:T(8,128)}, f32[6,16,256]{2,1,0:T(8,128)S(1)}, u32[]{:S(2)}, u32[]{:S(2)}) collective-permute-start(f32[6,16,256]{2,1,0:T(8,128)} %get-tuple-element.20), channel_id=1, source_target_pairs={{0,4},{4,0},{8,12},{12,8},{16,20},{20,16},{24,28},{28,24},{32,36},... | collective-permute-start | bytes 294920 | tf_op jit(solution)/shard_map/ppermute | solution.py:254
  4.6 26.6 %collective-permute-start.1 = (f32[6,16,256]{2,1,0:T(8,128)}, f32[6,16,256]{2,1,0:T(8,128)S(1)}, u32[]{:S(2)}, u32[]{:S(2)}) collective-permute-start(f32[6,16,256]{2,1,0:T(8,128)} %get-tuple-element.21), channel_id=1, source_target_pairs={{0,124},{4,8},{8,4},{12,16},{16,12},{20,24},{24,20},{28,32},{32,28... | collective-permute-start | bytes 294920 | tf_op jit(solution)/shard_map/ppermute | solution.py:252
  10.9 20.2 %collective-permute-start.2 = (f32[6,8,256]{2,1,0:T(8,128)}, f32[6,8,256]{2,1,0:T(8,128)S(1)}, u32[]{:S(2)}, u32[]{:S(2)}) collective-permute-start(f32[6,8,256]{2,1,0:T(8,128)} %get-tuple-element.22), channel_id=1, source_target_pairs={{0,1},{1,0},{2,3},{3,2},{4,5},{5,4},{6,7},{7,6},{8,9},{9,8},{10,11... | collective-permute-start | bytes 147464 | tf_op jit(solution)/shard_map/ppermute | solution.py:255
  12.2 19.0 %collective-permute-start.3 = (f32[6,8,256]{2,1,0:T(8,128)}, f32[6,8,256]{2,1,0:T(8,128)S(1)}, u32[]{:S(2)}, u32[]{:S(2)}) collective-permute-start(f32[6,8,256]{2,1,0:T(8,128)} %get-tuple-element.23), channel_id=1, source_target_pairs={{0,3},{1,2},{2,1},{3,0},{4,7},{5,6},{6,5},{7,4},{8,11},{9,10},{10,... | collective-permute-start | bytes 147464 | tf_op jit(solution)/shard_map/ppermute | solution.py:253
  14.5 5.0 %copy-start = (bf16[6,6,8,16,6,256]{5,3,4,2,1,0:T(8,128)(2,1)S(1)}, bf16[6,6,8,16,6,256]{5,3,4,2,1,0:T(8,128)(2,1)}, u32[]{:S(2)}) copy-start(bf16[6,6,8,16,6,256]{5,3,4,2,1,0:T(8,128)(2,1)} %param.10) | copy-start | bytes 42467332
  19.5 1.7 %copy-start.2 = (bf16[6,8,16,6,256]{4,2,3,1,0:T(8,128)(2,1)S(1)}, bf16[6,8,16,6,256]{4,2,3,1,0:T(8,128)(2,1)}, u32[]{:S(2)}) copy-start(bf16[6,8,16,6,256]{4,2,3,1,0:T(8,128)(2,1)} %param.12) | copy-start | bytes 7077892
  21.2 1.7 %copy-start.4 = (bf16[6,8,16,6,256]{4,2,3,1,0:T(8,128)(2,1)S(1)}, bf16[6,8,16,6,256]{4,2,3,1,0:T(8,128)(2,1)}, u32[]{:S(2)}) copy-start(bf16[6,8,16,6,256]{4,2,3,1,0:T(8,128)(2,1)} %param.11) | copy-start | bytes 7077892
  22.9 1.1 %copy-start.6 = (f32[8,16,6,256]{3,1,2,0:T(8,128)S(1)}, f32[8,16,6,256]{3,1,2,0:T(8,128)}, u32[]{:S(2)}) copy-start(f32[8,16,6,256]{3,1,2,0:T(8,128)} %param.9) | copy-start | bytes 2359300
  24.0 1.1 %copy-start.7 = (f32[8,16,6,256]{3,1,2,0:T(8,128)S(1)}, f32[8,16,6,256]{3,1,2,0:T(8,128)}, u32[]{:S(2)}) copy-start(f32[8,16,6,256]{3,1,2,0:T(8,128)} %param.8) | copy-start | bytes 2359300
  25.1 6.1 %copy-start.1 = (bf16[6,6,8,16,6,256]{5,3,4,2,1,0:T(8,128)(2,1)S(1)}, bf16[6,6,8,16,6,256]{5,3,4,2,1,0:T(8,128)(2,1)}, u32[]{:S(2)}) copy-start(bf16[6,6,8,16,6,256]{5,3,4,2,1,0:T(8,128)(2,1)} %param.10) | copy-start | bytes 42467332
  25.1 6.1 %copy-start.3 = (bf16[6,8,16,6,256]{4,2,3,1,0:T(8,128)(2,1)S(1)}, bf16[6,8,16,6,256]{4,2,3,1,0:T(8,128)(2,1)}, u32[]{:S(2)}) copy-start(bf16[6,8,16,6,256]{4,2,3,1,0:T(8,128)(2,1)} %param.12) | copy-start | bytes 7077892
  31.3 3.4 %copy-start.5 = (bf16[6,8,16,6,256]{4,2,3,1,0:T(8,128)(2,1)S(1)}, bf16[6,8,16,6,256]{4,2,3,1,0:T(8,128)(2,1)}, u32[]{:S(2)}) copy-start(bf16[6,8,16,6,256]{4,2,3,1,0:T(8,128)(2,1)} %param.11) | copy-start | bytes 7077892
  31.3 3.4 %copy-start.8 = (f32[8,16,6,256]{3,1,2,0:T(8,128)S(1)}, f32[8,16,6,256]{3,1,2,0:T(8,128)}, u32[]{:S(2)}) copy-start(f32[8,16,6,256]{3,1,2,0:T(8,128)} %param.8) | copy-start | bytes 2359300
  31.8 8.4 %collective-permute-start.4 = (f32[6,16,256]{2,1,0:T(8,128)S(1)}, f32[6,16,256]{2,1,0:T(8,128)S(1)}, u32[]{:S(2)}, u32[]{:S(2)}) collective-permute-start(f32[6,16,256]{2,1,0:T(8,128)S(1)} %get-tuple-element.29), channel_id=1, source_target_pairs={{0,4},{4,0},{8,12},{12,8},{16,20},{20,16},{24,28},{28,24},{32,36},... | collective-permute-start | bytes 294920 | tf_op jit(solution)/shard_map/ppermute | solution.py:254
  31.9 8.3 %collective-permute-start.5 = (f32[6,16,256]{2,1,0:T(8,128)S(1)}, f32[6,16,256]{2,1,0:T(8,128)S(1)}, u32[]{:S(2)}, u32[]{:S(2)}) collective-permute-start(f32[6,16,256]{2,1,0:T(8,128)S(1)} %get-tuple-element.30), channel_id=1, source_target_pairs={{0,124},{4,8},{8,4},{12,16},{16,12},{20,24},{24,20},{28,32},{32,28... | collective-permute-start | bytes 294920 | tf_op jit(solution)/shard_map/ppermute | solution.py:252
  32.0 8.1 %collective-permute-start.6 = (f32[6,8,256]{2,1,0:T(8,128)S(1)}, f32[6,8,256]{2,1,0:T(8,128)S(1)}, u32[]{:S(2)}, u32[]{:S(2)}) collective-permute-start(f32[6,8,256]{2,1,0:T(8,128)S(1)} %get-tuple-element.31), channel_id=1, source_target_pairs={{0,1},{1,0},{2,3},{3,2},{4,5},{5,4},{6,7},{7,6},{8,9},{9,8},{10,11... | collective-permute-start | bytes 147464 | tf_op jit(solution)/shard_map/ppermute | solution.py:255
  33.1 7.1 %collective-permute-start.7 = (f32[6,8,256]{2,1,0:T(8,128)S(1)}, f32[6,8,256]{2,1,0:T(8,128)S(1)}, u32[]{:S(2)}, u32[]{:S(2)}) collective-permute-start(f32[6,8,256]{2,1,0:T(8,128)S(1)} %get-tuple-element.32), channel_id=1, source_target_pairs={{0,3},{1,2},{2,1},{3,0},{4,7},{5,6},{6,5},{7,4},{8,11},{9,10},{10,... | collective-permute-start | bytes 147464 | tf_op jit(solution)/shard_map/ppermute | solution.py:253
  34.7 5.5 %copy-start.9 = (f32[512,6,128]{2,0,1:T(8,128)S(1)}, f32[512,6,128]{2,0,1:T(8,128)}, u32[]{:S(2)}) copy-start(f32[512,6,128]{2,0,1:T(8,128)} %param.15) | copy-start | bytes 4718596
  34.7 5.5 %copy-start.10 = (s32[512]{0:T(512)S(1)}, s32[512]{0:T(512)}, u32[]{:S(2)}) copy-start(s32[512]{0:T(512)} %cell_ref.1) | copy-start | bytes 6148
  34.7 5.5 %copy-start.11 = (s32[512]{0:T(512)S(1)}, s32[512]{0:T(512)}, u32[]{:S(2)}) copy-start(s32[512]{0:T(512)} %param.14) | copy-start | bytes 6148
  46.9 6.6 %collective-permute-start.8 = (f32[1,128]{1,0:T(1,128)S(1)}, f32[1,128]{1,0:T(1,128)S(1)}, u32[]{:S(2)}, u32[]{:S(2)}) collective-permute-start(f32[1,128]{1,0:T(1,128)S(1)} %get-tuple-element.35), channel_id=1, source_target_pairs={{0,4},{4,8},{8,12},{12,16},{16,20},{20,24},{24,28},{28,32},{32,36}... | collective-permute-start | bytes 1544 | tf_op jit(solution)/shard_map/ppermute | solution.py:282
  53.5 3.7 %collective-permute-start.9 = (f32[1,128]{1,0:T(1,128)S(1)}, f32[1,128]{1,0:T(1,128)S(1)}, u32[]{:S(2)}, u32[]{:S(2)}) collective-permute-start(f32[1,128]{1,0:T(1,128)S(1)} %add.12), channel_id=1, source_target_pairs={{0,1},{1,0},{2,3},{3,2},{4,5},{5,4},{6,7},{7,6},{8,9},{9,8},{10,11... | collective-permute-start | bytes 1544 | tf_op jit(solution)/shard_map/ppermute | solution.py:283
  57.2 3.9 %collective-permute-start.10 = (f32[1,128]{1,0:T(1,128)S(1)}, f32[1,128]{1,0:T(1,128)S(1)}, u32[]{:S(2)}, u32[]{:S(2)}) collective-permute-start(f32[1,128]{1,0:T(1,128)S(1)} %add.13), channel_id=1, source_target_pairs={{0,2},{1,3},{2,0},{3,1},{4,6},{5,7},{6,4},{7,5},{8,10},{9,11},{10,... | collective-permute-start | bytes 1544 | tf_op jit(solution)/shard_map/ppermute | solution.py:284

commit v2 on v1

v2 whole, which is shorter than its diff:
```python
import functools

import jax
import jax.numpy as jnp
from jax import lax
from jax.experimental import pallas as pl
from jax.experimental.pallas import tpu as pltpu
from jax.sharding import PartitionSpec as P

F32 = jnp.float32
PARAMS = pltpu.CompilerParams(vmem_limit_bytes=28 << 20)


def _vmem():
    return pl.BlockSpec(memory_space=pltpu.VMEM)


def _smem():
    return pl.BlockSpec(memory_space=pltpu.SMEM)


def send_faces(adj, even_ref, odd_ref, near_ref, far_ref):
    nt, nv, nq, _ = adj.shape
    c = lax.axis_index("circ")
    r = lax.axis_index("radax")
    t_even = jnp.where(c % 2 == 0, nt - 1, 0)
    even_ref[...] = adj[t_even]
    odd_ref[...] = adj[nt - 1 - t_even]
    up = r % 2 == 0
    for t in range(nt):
        for i in range(nv):
            low = adj[t, i, 0:1, :]
            high = adj[t, i, nq - 1 : nq, :]
            near_ref[i, t : t + 1, :] = jnp.where(up, high, low)
            far_ref[i, t : t + 1, :] = jnp.where(up, low, high)


def faces_kernel(adj_ref, even_ref, odd_ref, near_ref, far_ref):
    send_faces(adj_ref, even_ref, odd_ref, near_ref, far_ref)


def shift_lanes(plane, step):
    width = plane.shape[1]
    lane = lax.broadcasted_iota(jnp.int32, plane.shape, 1)
    edge = 0 if step == 1 else width - 1
    return jnp.where(lane == edge, 0.0, pltpu.roll(plane, step % width, 1))


def shift_rows(plane, step):
    rows = plane.shape[0]
    row = lax.broadcasted_iota(jnp.int32, plane.shape, 0)
    edge = 0 if step == 1 else rows - 1
    return jnp.where(row == edge, 0.0, pltpu.roll(plane, step % rows, 0))


def local_layer(t, adj_ref, g_ref, off_ref, diag_ref, pre_ref, out_ref, edge_refs=()):
    nt, nv, nq, _ = adj_ref.shape
    below = jnp.maximum(t - 1, 0)
    above = jnp.minimum(t + 1, nt - 1)
    has_below = (t > 0).astype(F32)
    has_above = (t < nt - 1).astype(F32)
    acc = [g_ref[t, i] for i in range(nv)]
    for j in range(nv):
        here = adj_ref[t, j]
        fields = [
            adj_ref[below, j] * has_below,
            adj_ref[above, j] * has_above,
            shift_rows(here, 1),
            shift_rows(here, -1),
            shift_lanes(here, 1),
            shift_lanes(here, -1),
        ]
        for i in range(nv):
            acc[i] = acc[i] - diag_ref[j, t, i].astype(F32) * here
        for k in range(6):
            for i in range(nv):
                block = off_ref[k, j, t, i].astype(F32)
                acc[i] = acc[i] - block * fields[k]
                if edge_refs and k == 2:
                    edge_refs[0][j, i, pl.ds(t, 1), :] = block[0:1, :]
                if edge_refs and k == 3:
                    edge_refs[1][j, i, pl.ds(t, 1), :] = block[nq - 1 : nq, :]
    new = [adj_ref[t, i] for i in range(nv)]
    for j in range(nv):
        for i in range(nv):
            block = pre_ref[j, t, i].astype(F32)
            new[i] = new[i] + block * acc[j]
            if edge_refs:
                edge_refs[2][j, i, pl.ds(t, 1), :] = block[0:1, :]
                edge_refs[3][j, i, pl.ds(t, 1), :] = block[nq - 1 : nq, :]
    for i in range(nv):
        out_ref[t, i] = new[i]


def first_kernel(adj_hbm, g_hbm, off_hbm, diag_hbm, pre_hbm,
                 out_ref, e0, e1, e2, e3, g_ref, off_ref, diag_ref, pre_ref, adj_ref, sems):
    nt = adj_ref.shape[0]

    def copies(t):
        return [
            pltpu.make_async_copy(off_hbm.at[:, :, t], off_ref.at[:, :, t], sems.at[0, t]),
            pltpu.make_async_copy(diag_hbm.at[:, t], diag_ref.at[:, t], sems.at[1, t]),
            pltpu.make_async_copy(pre_hbm.at[:, t], pre_ref.at[:, t], sems.at[2, t]),
            pltpu.make_async_copy(g_hbm.at[t], g_ref.at[t], sems.at[3, t]),
        ]

    whole = pltpu.make_async_copy(adj_hbm, adj_ref, sems.at[4, 0])
    whole.start()
    for t in range(nt):
        for copy in copies(t):
            copy.start()
    whole.wait()

    def layer(t, carry):
        for copy in copies(t):
            copy.wait()
        local_layer(t, adj_ref, g_ref, off_ref, diag_ref, pre_ref, out_ref, (e0, e1, e2, e3))
        return carry

    lax.fori_loop(0, nt, layer, 0)


def second_kernel(adj_ref, g_ref, off_ref, diag_ref, pre_ref, out_ref):
    def layer(t, carry):
        local_layer(t, adj_ref, g_ref, off_ref, diag_ref, pre_ref, out_ref)
        return carry

    lax.fori_loop(0, adj_ref.shape[0], layer, 0)


COST = pl.CostEstimate(flops=40_000_000, bytes_accessed=24_000_000, transcendentals=0)


def first_part(adj, g, off, diag, pre):
    nt, nv, nq, na = adj.shape
    out_shape = [jax.ShapeDtypeStruct(adj.shape, F32)]
    out_shape += [jax.ShapeDtypeStruct((nv, nv, nt, na), F32)] * 4
    out_shape += [pltpu.VMEM(x.shape, x.dtype) for x in (g, off, diag, pre)]
    return pl.pallas_call(
        first_kernel,
        in_specs=[pl.BlockSpec(memory_space=pltpu.HBM)] * 5,
        out_specs=[_vmem()] * len(out_shape),
        out_shape=out_shape,
        scratch_shapes=[pltpu.VMEM(adj.shape, F32), pltpu.SemaphoreType.DMA((5, nt))],
        compiler_params=PARAMS,
        cost_estimate=COST,
        name="local_first",
    )(adj, g, off, diag, pre)


def second_part(adj, g, off, diag, pre):
    return pl.pallas_call(
        second_kernel,
        in_specs=[_vmem()] * 5,
        out_specs=_vmem(),
        out_shape=jax.ShapeDtypeStruct(adj.shape, F32),
        compiler_params=PARAMS,
        cost_estimate=COST,
        name="local_second",
    )(adj, g, off, diag, pre)


def apply_blocks(load, vectors):
    nv = len(vectors)
    out = []
    for i in range(nv):
        total = load(0, i) * vectors[0]
        for j in range(1, nv):
            total = total + load(j, i) * vectors[j]
        out.append(total)
    return out


def add_halos(adj_ref, even, odd, near, far, off_ref, pre_ref, edges, out_ref):
    nt, nv, nq, _ = adj_ref.shape
    c = lax.axis_index("circ")
    r = lax.axis_index("radax")
    c_even = c % 2 == 0
    r_even = r % 2 == 0
    out_ref[...] = adj_ref[...]
    for t, low in ((0, True), (nt - 1, False)):
        k = 0 if low else 1
        pick = jnp.logical_not(c_even) if low else c_even
        halo = [jnp.where(pick, even[j], odd[j]) for j in range(nv)]
        extra = apply_blocks(lambda j, i: off_ref[k, j, t, i].astype(F32), halo)
        change = apply_blocks(lambda j, i: pre_ref[j, t, i].astype(F32), extra)
        for i in range(nv):
            out_ref[t, i] = out_ref[t, i] - change[i]
    last = lax.axis_size("radax") - 1
    for q, low in ((0, True), (nq - 1, False)):
        off, pre = (edges[0], edges[2]) if low else (edges[1], edges[3])
        pick = jnp.logical_not(r_even) if low else r_even
        inside = (r > 0) if low else (r < last)
        halo = [jnp.where(inside, jnp.where(pick, near[j], far[j]), 0.0) for j in range(nv)]
        extra = apply_blocks(lambda j, i: off[j, i], halo)
        change = apply_blocks(lambda j, i: pre[j, i], extra)
        for t in range(nt):
            for i in range(nv):
                out_ref[t, i, q : q + 1, :] = out_ref[t, i, q : q + 1, :] - change[i][t : t + 1, :]


def halo_kernel(adj_ref, even, odd, near, far, off_ref, pre_ref, e0, e1, e2, e3,
                out_ref, even_out, odd_out, near_out, far_out):
    add_halos(adj_ref, even, odd, near, far, off_ref, pre_ref, (e0, e1, e2, e3), out_ref)
    send_faces(out_ref, even_out, odd_out, near_out, far_out)


def final_kernel(adj_ref, even, odd, near, far, off_ref, pre_ref, e0, e1, e2, e3,
                 side_ref, design_ref, cell_ref, out_ref, sums_ref, by_cell, picked):
    add_halos(adj_ref, even, odd, near, far, off_ref, pre_ref, (e0, e1, e2, e3), out_ref)
    nt, nv, nq, na = adj_ref.shape
    halves = na // 128
    for t in range(nt):
        for i in range(nv):
            for qt in range(nq // 8):
                for h in range(halves):
                    first = ((t * nq + qt * 8) * halves + h) * 8 + i
                    by_cell[pl.ds(first, 8, stride=8 * halves), :] = out_ref[
                        t, i, qt * 8 : qt * 8 + 8, h * 128 : h * 128 + 128
                    ]
    faces = design_ref.shape[1]
    lane = lax.broadcasted_iota(jnp.int32, (8, 128), 1)

    def pick(f, carry):
        cell = cell_ref[f]
        row = pl.multiple_of(lax.shift_right_logical(cell, 7) * 8, 8)
        tile = by_cell[pl.ds(row, 8), :]
        kept = jnp.where(lane == (cell & 127), tile, 0.0)
        picked[pl.ds(f, 8, stride=faces), :] = kept
        return carry

    lax.fori_loop(0, faces, pick, 0, unroll=32)
    every = jnp.zeros((8, 128), F32)
    upper = jnp.zeros((8, 128), F32)
    for f0 in range(0, faces, 128):
        on_upper = jnp.transpose(jnp.broadcast_to(side_ref[f0 // 128 : f0 // 128 + 1, :].astype(F32), (128, 128)))
        contrib = jnp.zeros((128, 128), F32)
        for i in range(nv):
            value = jnp.sum(picked[i * faces + f0 : i * faces + f0 + 128, :], axis=1, keepdims=True)
            contrib = contrib + value * design_ref[i, f0 : f0 + 128, :]
        every = every + jnp.sum(contrib.reshape(16, 8, 128), axis=0)
        upper = upper + jnp.sum((contrib * on_upper).reshape(16, 8, 128), axis=0)
    upper = jnp.sum(upper, axis=0, keepdims=True)
    sums_ref[0:1, :] = jnp.sum(every, axis=0, keepdims=True) - upper
    sums_ref[1:2, :] = upper


def halo_part(adj, halos, off, pre, edges, faces=None):
    nt, nv, nq, na = adj.shape
    args = [adj, *halos, off, pre, *edges]
    cost = pl.CostEstimate(flops=4_000_000, bytes_accessed=5_000_000, transcendentals=0)
    out_shape = [jax.ShapeDtypeStruct(adj.shape, F32)]
    if faces is None:
        out_shape += [jax.ShapeDtypeStruct(h.shape, F32) for h in halos]
        return pl.pallas_call(
            halo_kernel, in_specs=[_vmem()] * len(args), out_specs=[_vmem()] * 5, out_shape=out_shape,
            compiler_params=PARAMS, cost_estimate=cost, name="halo_first",
        )(*args)
    cell, side, design = faces
    out_shape += [jax.ShapeDtypeStruct((2, design.shape[2]), F32)]
    return pl.pallas_call(
        final_kernel, in_specs=[_vmem()] * (len(args) + 2) + [_smem()], out_specs=[_vmem()] * 2, out_shape=out_shape,
        scratch_shapes=[
            pltpu.VMEM((nt * nq * na // 128 * 8, 128), F32),
            pltpu.VMEM((8 * design.shape[1], 128), F32),
        ],
        compiler_params=PARAMS, cost_estimate=cost, name="halo_last",
    )(*args, side, design, cell)


def swap_halos(even, odd, near, far):
    nc = lax.axis_size("circ")
    nr = lax.axis_size("radax")
    odd = lax.ppermute(odd, "circ", [(i, (i + 1) % nc if i % 2 else (i - 1) % nc) for i in range(nc)])
    far = lax.ppermute(far, "radax", [(i, nr - 1 - i) for i in range(nr)])
    even = lax.ppermute(even, "circ", [(i, i ^ 1) for i in range(nc)])
    near = lax.ppermute(near, "radax", [(i, i ^ 1) for i in range(nr)])
    return even, odd, near, far


def combine(sums):
    nc = lax.axis_size("circ")
    nr = lax.axis_size("radax")
    near = [(i, i ^ 1) for i in range(nr)]
    both = sums + lax.ppermute(sums, "radax", near)
    lower, upper = both[0:1], both[1:2]
    ring = [(c * nr + r, (c + 1) % nc * nr + (r ^ 2 if r % 2 == 0 else r)) for c in range(nc) for r in range(nr)]
    arrived = lax.ppermute(upper, ("circ", "radax"), ring)
    other = lax.ppermute(lower, "radax", [(i, i ^ 2) for i in range(nr)])
    first = lax.axis_index("radax") % 2 == 0
    mine = arrived + jnp.where(first, lower + other, 0.0)
    return mine + lax.ppermute(mine, "radax", near)


def body(objective_grad, adjoint_start, jac_off, jac_diag, precond, face_cell, face_side, design_grad):
    g = objective_grad.transpose(0, 2, 1, 3)
    adj = adjoint_start.transpose(0, 2, 1, 3)
    off = jac_off.transpose(0, 1, 2, 4, 3, 5)
    diag = jac_diag.transpose(0, 1, 3, 2, 4)
    pre = precond.transpose(0, 1, 3, 2, 4)
    design = design_grad.transpose(1, 0, 2)
    nt, nv, nq, na = adj.shape
    ring = jax.ShapeDtypeStruct((nv, nq, na), F32)
    rows = jax.ShapeDtypeStruct((nv, nt, na), F32)
    sends = pl.pallas_call(
        faces_kernel, in_specs=[_vmem()], out_specs=[_vmem()] * 4,
        out_shape=[ring, ring, rows, rows], name="faces",
        compiler_params=PARAMS,
    )(adj)
    halos = swap_halos(*sends)
    hbm = [pltpu.with_memory_space_constraint(x, pltpu.HBM) for x in (adj, g, off, diag, pre)]
    part, *edges, g, off, diag, pre = first_part(*hbm)
    g, off, diag, pre = [pltpu.with_memory_space_constraint(x, pltpu.VMEM) for x in (g, off, diag, pre)]
    adj, *sends = halo_part(part, halos, off, pre, edges)
    halos = swap_halos(*sends)
    part = second_part(adj, g, off, diag, pre)
    side = face_side.reshape(-1, 128)
    adj, sums = halo_part(part, halos, off, pre, edges, (face_cell, side, design))
    total = combine(sums)
    nr = lax.axis_size("radax")
    owned = total.shape[1] // nr
    sensitivity = lax.dynamic_slice_in_dim(total, lax.axis_index("radax") * owned, owned, 1)
    return adj.transpose(0, 2, 1, 3), sensitivity


def solution(mesh):
    in_specs = (
        P("circ", "radax", None, None),
        P("circ", "radax", None, None),
        P(None, None, "circ", "radax", None, None),
        P(None, "circ", "radax", None, None),
        P(None, "circ", "radax", None, None),
        P(("circ", "radax")),
        P(("circ", "radax")),
        P(("circ", "radax"), None, None),
    )
    out_specs = (P("circ", "radax", None, None), P("circ", "radax"))
    return jax.shard_map(body, mesh=mesh, in_specs=in_specs, out_specs=out_specs, check_vma=False)
```

time: 62.2 us -> 48.4 us (0.78)
  local copies, waits for them, and re-layouts: 11.2 us -> 1.73 us
  Pallas kernels: 20.5 us -> 16.6 us
  starting transfers between devices: 17.8 us -> 19.8 us
  waiting for transfers between devices: 11.4 us -> 9.41 us
    unnamed x24 -> x8, local copies, waits for them, and re-layouts: 10.7 us -> 1.14 us
    ppermute x3 -> x4, waiting for transfers between devices: 11.3 us -> 8.25 us  [the longest x1 3.83 us: combine(): other = lax.ppermute(lower, 'radax', [(i, i ^ 2) for i in range(nr)])]
    pallas_call x4, Pallas kernels: 18.6 us -> 16.5 us  [the longest x1 7.8 us: first_part(): pl.pallas_call(first_kernel, in_specs=[pl.BlockSpec(memory_space=pltpu.HB...]
    ppermute x3 -> x4, starting transfers between devices: 2.92 us -> 4.87 us  [the longest x1 2.9 us: combine(): return mine + lax.ppermute(mine, 'radax', near)]
    pallas_call x1, Pallas kernels: 1.9 us -> 0.07 us  [body(): pl.pallas_call(faces_kernel, in_specs=[_vmem()], out_specs=[_vmem()] * 4,...]
    ppermute x2, waiting for transfers between devices: 0.01 us -> 1.15 us  [swap_halos(): lax.ppermute(odd, 'circ', [(i, (i + 1) % nc if i % 2 else (i - 1) % nc) f...]
  transfers between devices with their start and end apart: 11 -> 12, of which waited for: 3 -> 5; matrix products, arithmetic and copies ran while one was open for 0% -> 0% of each run, Pallas kernels for 19% -> 25%
where the time goes in v2:
time: 48.4 us; the launch traced here: 48.3 us
  starting transfers between devices  19.8 us (41%)
  Pallas kernels  16.6 us (34%)
  waiting for transfers between devices  9.41 us (19%)
  local copies, waits for them, and re-layouts  1.73 us (4%)
  between operations  0.77 us (2%)
    pallas_call x1, Pallas kernels, first_part(): pl.pallas_call(first_kernel, in_specs=[pl.BlockSpec(memory_space=pltpu.HB...  7.8 us
    ppermute x2, starting transfers between devices, swap_halos(): lax.ppermute(odd, 'circ', [(i, (i + 1) % nc if i % 2 else (i - 1) % nc) f...  6.41 us
    pallas_call x1, Pallas kernels, second_part(): pl.pallas_call(second_kernel, in_specs=[_vmem()] * 5, out_specs=_vmem(),...  4.16 us
    pallas_call x1, Pallas kernels, halo_part(): pl.pallas_call(final_kernel, in_specs=[_vmem()] * (len(args) + 2) + [_sme...  4.04 us
    ppermute x2, starting transfers between devices, swap_halos(): far = lax.ppermute(far, 'radax', [(i, nr - 1 - i) for i in range(nr)])  3.96 us
    ppermute x1, waiting for transfers between devices, combine(): other = lax.ppermute(lower, 'radax', [(i, i ^ 2) for i in range(nr)])  3.83 us
    ppermute x1, starting transfers between devices, combine(): return mine + lax.ppermute(mine, 'radax', near)  2.9 us
    ppermute x1, waiting for transfers between devices, combine(): arrived = lax.ppermute(upper, ('circ', 'radax'), ring)  2.79 us
  transfers between devices with their start and end apart: 12, of which 5 were waited for; matrix products, arithmetic and copies ran while one was open for 0% of the time, Pallas kernels for 25%

profile of v2, /device:TPU:1, one launch (start us, length us, event | category | flops | bytes accessed | tf_op | source)
XLA Modules:
  0.0 48.3 jit_solution(13154162662650798569)
XLA Ops:
  0.6 0.0 copy-start
  0.6 1.1 %copy-done = f32[8,16,6,256]{3,1,2,0:T(8,128)S(1)} copy-done((f32[8,16,6,256]{3,1,2,0:T(8,128)S(1)}, f32[8,16,6,256]{3,1,2,0:T(8,128)}, u32[]{:S(2)}) %copy-start) | copy-done | bytes 786456
  1.8 0.1 faces.1
  1.8 2.2 %collective-permute-start = (f32[6,16,256]{2,1,0:T(8,128)S(1)}, f32[6,16,256]{2,1,0:T(8,128)S(1)}, u32[]{:S(2)}, u32[]{:S(2)}) collective-permute-start(f32[6,16,256]{2,1,0:T(8,128)S(1)} %get-tuple-element.23), channel_id=1, source_target_pairs={{0,4},{4,0},{8,12},{12,8},{16,20},{20,16},{24,28},{28,24},{32,36},... | collective-permute-start | bytes 294920 | tf_op jit(solution)/shard_map/ppermute | solution.py:276
  4.0 6.3 %collective-permute-start.1 = (f32[6,16,256]{2,1,0:T(8,128)S(1)}, f32[6,16,256]{2,1,0:T(8,128)S(1)}, u32[]{:S(2)}, u32[]{:S(2)}) collective-permute-start(f32[6,16,256]{2,1,0:T(8,128)S(1)} %get-tuple-element.24), channel_id=1, source_target_pairs={{0,124},{4,8},{8,4},{12,16},{16,12},{20,24},{24,20},{28,32},{32,28... | collective-permute-start | bytes 294920 | tf_op jit(solution)/shard_map/ppermute | solution.py:274
  10.3 1.2 %collective-permute-start.2 = (f32[6,8,256]{2,1,0:T(8,128)S(1)}, f32[6,8,256]{2,1,0:T(8,128)S(1)}, u32[]{:S(2)}, u32[]{:S(2)}) collective-permute-start(f32[6,8,256]{2,1,0:T(8,128)S(1)} %get-tuple-element.25), channel_id=1, source_target_pairs={{0,1},{1,0},{2,3},{3,2},{4,5},{5,4},{6,7},{7,6},{8,9},{9,8},{10,11... | collective-permute-start | bytes 147464 | tf_op jit(solution)/shard_map/ppermute | solution.py:277
  11.6 2.3 %collective-permute-start.3 = (f32[6,8,256]{2,1,0:T(8,128)S(1)}, f32[6,8,256]{2,1,0:T(8,128)S(1)}, u32[]{:S(2)}, u32[]{:S(2)}) collective-permute-start(f32[6,8,256]{2,1,0:T(8,128)S(1)} %get-tuple-element.26), channel_id=1, source_target_pairs={{0,3},{1,2},{2,1},{3,0},{4,7},{5,6},{6,5},{7,4},{8,11},{9,10},{10,... | collective-permute-start | bytes 147464 | tf_op jit(solution)/shard_map/ppermute | solution.py:275
  13.9 7.8 %local_first.1 = (f32[8,6,16,256]{3,2,1,0:T(8,128)S(1)}, f32[6,6,8,256]{3,2,1,0:T(8,128)S(1)}, f32[6,6,8,256]{3,2,1,0:T(8,128)S(1)}, f32[6,6,8,256]{3,2,1,0:T(8,...) custom-call(f32[8,6,16,256]{3,2,1,0:T(8,128)} %bitcast.8, ...), custom_call_target="tpu_custom_call" | custom-call | flops 40000000 | bytes 24000000 | tf_op jit(solution)/shard_map/local_first/pallas_call | solution.py:139
  21.7 0.0 collective-permute-done.2.near
  21.7 0.0 collective-permute-done.3.far
  21.7 0.0 collective-permute-done.even
  21.8 0.0 collective-permute-done.1.odd
  21.8 0.5 %halo_first.1 = (f32[8,6,16,256]{3,2,1,0:T(8,128)S(1)}, f32[6,16,256]{2,1,0:T(8,128)S(1)}, f32[6,16,256]{2,1,0:T(8,128)S(1)}, f32[6,8,256]{2,1,0:T(8,128)S(1)}, f32[6,8,256]{2,1,0:T(8,128)S(1)}) custom-call(f32[8,6,16,256]{3,2,1,0:T(8,128)S(1)} %get-tuple-element.22.adj_ref, f32[6,16,256]{2,1,0:T(8,128)S(1)} %collective-permute-done.even, ...), custom_call_target="tpu_custom_call" | custom-call | flops 4000000 | bytes 5000000 | tf_op jit(solution)/shard_map/halo_first/pallas_call | solution.py:255
  22.3 0.1 collective-permute-start.4
  22.4 0.1 collective-permute-start.5
  22.5 1.1 %collective-permute-start.6 = (f32[6,8,256]{2,1,0:T(8,128)S(1)}, f32[6,8,256]{2,1,0:T(8,128)S(1)}, u32[]{:S(2)}, u32[]{:S(2)}) collective-permute-start(f32[6,8,256]{2,1,0:T(8,128)S(1)} %get-tuple-element.38), channel_id=1, source_target_pairs={{0,1},{1,0},{2,3},{3,2},{4,5},{5,4},{6,7},{7,6},{8,9},{9,8},{10,11... | collective-permute-start | bytes 147464 | tf_op jit(solution)/shard_map/ppermute | solution.py:277
  23.5 1.6 %collective-permute-start.7 = (f32[6,8,256]{2,1,0:T(8,128)S(1)}, f32[6,8,256]{2,1,0:T(8,128)S(1)}, u32[]{:S(2)}, u32[]{:S(2)}) collective-permute-start(f32[6,8,256]{2,1,0:T(8,128)S(1)} %get-tuple-element.39), channel_id=1, source_target_pairs={{0,3},{1,2},{2,1},{3,0},{4,7},{5,6},{6,5},{7,4},{8,11},{9,10},{10,... | collective-permute-start | bytes 147464 | tf_op jit(solution)/shard_map/ppermute | solution.py:275
  25.1 0.0 copy-start.1
  25.1 0.0 copy-start.2
  25.1 0.0 copy-start.3
  25.1 4.2 %local_second.1.adj_ref = f32[8,6,16,256]{3,2,1,0:T(8,128)S(1)} custom-call(f32[8,6,16,256]{3,2,1,0:T(8,128)S(1)} %get-tuple-element.33.adj_ref, f32[8,6,16,256]{3,2,1,0:T(8,128)S(1)} %get-tuple-element.34.g_ref, bf16[6,6,8,6,16,256]{5,4,3,2,1,0:T(8,128)(2,1)S(1)} %get-tuple-element.27.off_ref, bf16[6,8,6,16,256]{4,3,2,1,0:T(8,128)(2,1)S(1)} %get-tuple-element.35.diag_ref, ...), custom_call_target="tpu_custom_call" | custom-call | flops 40000000 | bytes 24000000 | tf_op jit(solution)/shard_map/local_second/pallas_call | solution.py:152
  29.3 0.0 collective-permute-done.6.near
  29.3 0.0 collective-permute-done.7.far
  29.3 0.0 collective-permute-done.4.even
  29.4 1.1 %collective-permute-done.5.odd = f32[6,16,256]{2,1,0:T(8,128)S(1)} collective-permute-done((f32[6,16,256]{2,1,0:T(8,128)S(1)}, f32[6,16,256]{2,1,0:T(8,128)S(1)}, u32[]{:S(2)}, u32[]{:S(2)}) %collective-permute-start.5) | collective-permute-done | bytes 98336 | tf_op jit(solution)/shard_map/ppermute | solution.py:274
  30.5 0.0 copy-done.1
  30.5 0.0 copy-done.2
  30.5 0.0 copy-done.3
  30.5 4.0 %halo_last.1 = (f32[8,6,16,256]{3,2,1,0:T(8,128)}, f32[2,128]{1,0:T(2,128)S(1)}) custom-call(f32[8,6,16,256]{3,2,1,0:T(8,128)S(1)} %local_second.1.adj_ref, f32[6,16,256]{2,1,0:T(8,128)S(1)} %collective-permute-done.4.even, f32[6,16,256]{2,1,0:T(8,128)S(1)} %collective-permute-done.5.odd, f32[6,8,256]{2,1,0:T(8,128)S(1)} %collective-permute-done.6.near, ...), custom_call_target="tpu_custom_call" | custom-call | flops 4000000 | bytes 5000000 | tf_op jit(solution)/shard_map/halo_last/pallas_call | solution.py:261
  34.5 1.9 %collective-permute-start.8 = (f32[2,128]{1,0:T(2,128)S(1)}, f32[2,128]{1,0:T(2,128)S(1)}, u32[]{:S(2)}, u32[]{:S(2)}) collective-permute-start(f32[2,128]{1,0:T(2,128)S(1)} %get-tuple-element.41), channel_id=1, source_target_pairs={{0,1},{1,0},{2,3},{3,2},{4,5},{5,4},{6,7},{7,6},{8,9},{9,8},{10,11... | collective-permute-start | bytes 3080 | tf_op jit(solution)/shard_map/ppermute | solution.py:285
  36.4 0.8 %collective-permute-done.8 = f32[2,128]{1,0:T(2,128)S(1)} collective-permute-done((f32[2,128]{1,0:T(2,128)S(1)}, f32[2,128]{1,0:T(2,128)S(1)}, u32[]{:S(2)}, u32[]{:S(2)}) %collective-permute-start.8) | collective-permute-done | bytes 1056 | tf_op jit(solution)/shard_map/ppermute | solution.py:285
  37.3 0.0 collective-permute-start.10
  37.3 0.1 collective-permute-start.9
  37.4 3.8 %collective-permute-done.10 = f32[1,128]{1,0:T(1,128)S(1)} collective-permute-done((f32[1,128]{1,0:T(1,128)S(1)}, f32[1,128]{1,0:T(1,128)S(1)}, u32[]{:S(2)}, u32[]{:S(2)}) %collective-permute-start.10) | collective-permute-done | bytes 544 | tf_op jit(solution)/shard_map/ppermute | solution.py:289
  41.2 2.8 %collective-permute-done.9 = f32[1,128]{1,0:T(1,128)S(1)} collective-permute-done((f32[1,128]{1,0:T(1,128)S(1)}, f32[1,128]{1,0:T(1,128)S(1)}, u32[]{:S(2)}, u32[]{:S(2)}) %collective-permute-start.9) | collective-permute-done | bytes 544 | tf_op jit(solution)/shard_map/ppermute | solution.py:288
  44.0 2.9 %collective-permute-start.11 = (f32[1,128]{1,0:T(1,128)S(1)}, f32[1,128]{1,0:T(1,128)S(1)}, u32[]{:S(2)}, u32[]{:S(2)}) collective-permute-start(f32[1,128]{1,0:T(1,128)S(1)} %fusion), channel_id=1, source_target_pairs={{0,1},{1,0},{2,3},{3,2},{4,5},{5,4},{6,7},{7,6},{8,9},{9,8},{10,11... | collective-permute-start | bytes 1544 | tf_op jit(solution)/shard_map/ppermute | solution.py:292
  46.9 0.8 %collective-permute-done.11 = f32[1,128]{1,0:T(1,128)S(1)} collective-permute-done((f32[1,128]{1,0:T(1,128)S(1)}, f32[1,128]{1,0:T(1,128)S(1)}, u32[]{:S(2)}, u32[]{:S(2)}) %collective-permute-start.11) | collective-permute-done | bytes 544 | tf_op jit(solution)/shard_map/ppermute | solution.py:292
  47.7 0.6 %constant_dynamic-slice_fusion = f32[1,32]{1,0:T(1,128)} fusion(f32[1,128]{1,0:T(1,128)S(1)} %add.23, s32[]{:T(128)S(6)} %select_n.21), kind=kLoop, calls=%fused_computation.2 | loop fusion | bytes 260 | tf_op jit(solution)/shard_map/dynamic_slice | solution.py:322
  (4 shorter events, 0.0 us)
Async XLA Ops:
  0.6 1.1 %copy-start = (f32[8,16,6,256]{3,1,2,0:T(8,128)S(1)}, f32[8,16,6,256]{3,1,2,0:T(8,128)}, u32[]{:S(2)}) copy-start(f32[8,16,6,256]{3,1,2,0:T(8,128)} %param.9) | copy-start | bytes 2359300
  1.8 19.9 %collective-permute-start = (f32[6,16,256]{2,1,0:T(8,128)S(1)}, f32[6,16,256]{2,1,0:T(8,128)S(1)}, u32[]{:S(2)}, u32[]{:S(2)}) collective-permute-start(f32[6,16,256]{2,1,0:T(8,128)S(1)} %get-tuple-element.23), channel_id=1, source_target_pairs={{0,4},{4,0},{8,12},{12,8},{16,20},{20,16},{24,28},{28,24},{32,36},... | collective-permute-start | bytes 294920 | tf_op jit(solution)/shard_map/ppermute | solution.py:276
  4.0 17.7 %collective-permute-start.1 = (f32[6,16,256]{2,1,0:T(8,128)S(1)}, f32[6,16,256]{2,1,0:T(8,128)S(1)}, u32[]{:S(2)}, u32[]{:S(2)}) collective-permute-start(f32[6,16,256]{2,1,0:T(8,128)S(1)} %get-tuple-element.24), channel_id=1, source_target_pairs={{0,124},{4,8},{8,4},{12,16},{16,12},{20,24},{24,20},{28,32},{32,28... | collective-permute-start | bytes 294920 | tf_op jit(solution)/shard_map/ppermute | solution.py:274
  10.3 11.4 %collective-permute-start.2 = (f32[6,8,256]{2,1,0:T(8,128)S(1)}, f32[6,8,256]{2,1,0:T(8,128)S(1)}, u32[]{:S(2)}, u32[]{:S(2)}) collective-permute-start(f32[6,8,256]{2,1,0:T(8,128)S(1)} %get-tuple-element.25), channel_id=1, source_target_pairs={{0,1},{1,0},{2,3},{3,2},{4,5},{5,4},{6,7},{7,6},{8,9},{9,8},{10,11... | collective-permute-start | bytes 147464 | tf_op jit(solution)/shard_map/ppermute | solution.py:277
  11.6 10.2 %collective-permute-start.3 = (f32[6,8,256]{2,1,0:T(8,128)S(1)}, f32[6,8,256]{2,1,0:T(8,128)S(1)}, u32[]{:S(2)}, u32[]{:S(2)}) collective-permute-start(f32[6,8,256]{2,1,0:T(8,128)S(1)} %get-tuple-element.26), channel_id=1, source_target_pairs={{0,3},{1,2},{2,1},{3,0},{4,7},{5,6},{6,5},{7,4},{8,11},{9,10},{10,... | collective-permute-start | bytes 147464 | tf_op jit(solution)/shard_map/ppermute | solution.py:275
  22.3 7.1 %collective-permute-start.4 = (f32[6,16,256]{2,1,0:T(8,128)S(1)}, f32[6,16,256]{2,1,0:T(8,128)S(1)}, u32[]{:S(2)}, u32[]{:S(2)}) collective-permute-start(f32[6,16,256]{2,1,0:T(8,128)S(1)} %get-tuple-element.36), channel_id=1, source_target_pairs={{0,4},{4,0},{8,12},{12,8},{16,20},{20,16},{24,28},{28,24},{32,36},... | collective-permute-start | bytes 294920 | tf_op jit(solution)/shard_map/ppermute | solution.py:276
  22.4 8.1 %collective-permute-start.5 = (f32[6,16,256]{2,1,0:T(8,128)S(1)}, f32[6,16,256]{2,1,0:T(8,128)S(1)}, u32[]{:S(2)}, u32[]{:S(2)}) collective-permute-start(f32[6,16,256]{2,1,0:T(8,128)S(1)} %get-tuple-element.37), channel_id=1, source_target_pairs={{0,124},{4,8},{8,4},{12,16},{16,12},{20,24},{24,20},{28,32},{32,28... | collective-permute-start | bytes 294920 | tf_op jit(solution)/shard_map/ppermute | solution.py:274
  22.5 6.9 %collective-permute-start.6 = (f32[6,8,256]{2,1,0:T(8,128)S(1)}, f32[6,8,256]{2,1,0:T(8,128)S(1)}, u32[]{:S(2)}, u32[]{:S(2)}) collective-permute-start(f32[6,8,256]{2,1,0:T(8,128)S(1)} %get-tuple-element.38), channel_id=1, source_target_pairs={{0,1},{1,0},{2,3},{3,2},{4,5},{5,4},{6,7},{7,6},{8,9},{9,8},{10,11... | collective-permute-start | bytes 147464 | tf_op jit(solution)/shard_map/ppermute | solution.py:277
  23.5 5.8 %collective-permute-start.7 = (f32[6,8,256]{2,1,0:T(8,128)S(1)}, f32[6,8,256]{2,1,0:T(8,128)S(1)}, u32[]{:S(2)}, u32[]{:S(2)}) collective-permute-start(f32[6,8,256]{2,1,0:T(8,128)S(1)} %get-tuple-element.39), channel_id=1, source_target_pairs={{0,3},{1,2},{2,1},{3,0},{4,7},{5,6},{6,5},{7,4},{8,11},{9,10},{10,... | collective-permute-start | bytes 147464 | tf_op jit(solution)/shard_map/ppermute | solution.py:275
  25.1 5.4 %copy-start.1 = (f32[512,6,128]{2,0,1:T(8,128)S(1)}, f32[512,6,128]{2,0,1:T(8,128)}, u32[]{:S(2)}) copy-start(f32[512,6,128]{2,0,1:T(8,128)} %param.15) | copy-start | bytes 4718596
  25.1 5.4 %copy-start.2 = (s32[512]{0:T(512)S(1)}, s32[512]{0:T(512)}, u32[]{:S(2)}) copy-start(s32[512]{0:T(512)} %param.14) | copy-start | bytes 6148
  25.1 5.4 %copy-start.3 = (s32[512]{0:T(512)S(1)}, s32[512]{0:T(512)}, u32[]{:S(2)}) copy-start(s32[512]{0:T(512)} %cell_ref.1) | copy-start | bytes 6148
  34.5 2.7 %collective-permute-start.8 = (f32[2,128]{1,0:T(2,128)S(1)}, f32[2,128]{1,0:T(2,128)S(1)}, u32[]{:S(2)}, u32[]{:S(2)}) collective-permute-start(f32[2,128]{1,0:T(2,128)S(1)} %get-tuple-element.41), channel_id=1, source_target_pairs={{0,1},{1,0},{2,3},{3,2},{4,5},{5,4},{6,7},{7,6},{8,9},{9,8},{10,11... | collective-permute-start | bytes 3080 | tf_op jit(solution)/shard_map/ppermute | solution.py:285
  37.3 3.9 %collective-permute-start.10 = (f32[1,128]{1,0:T(1,128)S(1)}, f32[1,128]{1,0:T(1,128)S(1)}, u32[]{:S(2)}, u32[]{:S(2)}) collective-permute-start(f32[1,128]{1,0:T(1,128)S(1)} %get-tuple-element.42), channel_id=1, source_target_pairs={{0,2},{1,3},{2,0},{3,1},{4,6},{5,7},{6,4},{7,5},{8,10},{9,11},{10,... | collective-permute-start | bytes 1544 | tf_op jit(solution)/shard_map/ppermute | solution.py:289
  37.3 6.7 %collective-permute-start.9 = (f32[1,128]{1,0:T(1,128)S(1)}, f32[1,128]{1,0:T(1,128)S(1)}, u32[]{:S(2)}, u32[]{:S(2)}) collective-permute-start(f32[1,128]{1,0:T(1,128)S(1)} %get-tuple-element.43), channel_id=1, source_target_pairs={{0,6},{1,5},{2,4},{3,7},{4,10},{5,9},{6,8},{7,11},{8,14},{9,13},{1... | collective-permute-start | bytes 1544 | tf_op jit(solution)/shard_map/ppermute | solution.py:288
  44.0 3.7 %collective-permute-start.11 = (f32[1,128]{1,0:T(1,128)S(1)}, f32[1,128]{1,0:T(1,128)S(1)}, u32[]{:S(2)}, u32[]{:S(2)}) collective-permute-start(f32[1,128]{1,0:T(1,128)S(1)} %fusion), channel_id=1, source_target_pairs={{0,1},{1,0},{2,3},{3,2},{4,5},{5,4},{6,7},{7,6},{8,9},{9,8},{10,11... | collective-permute-start | bytes 1544 | tf_op jit(solution)/shard_map/ppermute | solution.py:292

commit v3 on v2

--- a/solution.py
+++ b/solution.py
@@ -1,5 +1,3 @@
-import functools
-
 import jax
 import jax.numpy as jnp
 from jax import lax
@@ -7,16 +5,13 @@
 from jax.experimental.pallas import tpu as pltpu
 from jax.sharding import PartitionSpec as P
 
+
 F32 = jnp.float32
 PARAMS = pltpu.CompilerParams(vmem_limit_bytes=28 << 20)
 
 
 def _vmem():
     return pl.BlockSpec(memory_space=pltpu.VMEM)
-
-
-def _smem():
-    return pl.BlockSpec(memory_space=pltpu.SMEM)
 
 
 def send_faces(adj, even_ref, odd_ref, near_ref, far_ref):
@@ -35,7 +30,10 @@
             far_ref[i, t : t + 1, :] = jnp.where(up, low, high)
 
 
-def faces_kernel(adj_ref, even_ref, odd_ref, near_ref, far_ref):
+def faces_kernel(adj_hbm, adj_ref, even_ref, odd_ref, near_ref, far_ref, sem):
+    copy = pltpu.make_async_copy(adj_hbm, adj_ref, sem)
+    copy.start()
+    copy.wait()
     send_faces(adj_ref, even_ref, odd_ref, near_ref, far_ref)
 
 
@@ -53,13 +51,13 @@
     return jnp.where(row == edge, 0.0, pltpu.roll(plane, step % rows, 0))
 
 
-def local_layer(t, adj_ref, g_ref, off_ref, diag_ref, pre_ref, out_ref, edge_refs=()):
+def local_layer(t, adj_ref, g_ref, off_ref, diag_ref, pre_ref, out_ref, edge_refs=(), wait=None):
     nt, nv, nq, _ = adj_ref.shape
     below = jnp.maximum(t - 1, 0)
     above = jnp.minimum(t + 1, nt - 1)
     has_below = (t > 0).astype(F32)
     has_above = (t < nt - 1).astype(F32)
-    acc = [g_ref[t, i] for i in range(nv)]
+    acc = [jnp.zeros(adj_ref.shape[2:], F32)] * nv
     for j in range(nv):
         here = adj_ref[t, j]
         fields = [
@@ -70,16 +68,21 @@
             shift_lanes(here, 1),
             shift_lanes(here, -1),
         ]
-        for i in range(nv):
-            acc[i] = acc[i] - diag_ref[j, t, i].astype(F32) * here
         for k in range(6):
             for i in range(nv):
                 block = off_ref[k, j, t, i].astype(F32)
-                acc[i] = acc[i] - block * fields[k]
+                acc[i] = acc[i] + block * fields[k]
                 if edge_refs and k == 2:
                     edge_refs[0][j, i, pl.ds(t, 1), :] = block[0:1, :]
                 if edge_refs and k == 3:
                     edge_refs[1][j, i, pl.ds(t, 1), :] = block[nq - 1 : nq, :]
+    if wait is not None:
+        wait()
+    for j in range(nv):
+        here = adj_ref[t, j]
+        for i in range(nv):
+            acc[i] = acc[i] + diag_ref[j, t, i].astype(F32) * here
+    acc = [g_ref[t, i] - acc[i] for i in range(nv)]
     new = [adj_ref[t, i] for i in range(nv)]
     for j in range(nv):
         for i in range(nv):
@@ -92,29 +95,27 @@
         out_ref[t, i] = new[i]
 
 
-def first_kernel(adj_hbm, g_hbm, off_hbm, diag_hbm, pre_hbm,
-                 out_ref, e0, e1, e2, e3, g_ref, off_ref, diag_ref, pre_ref, adj_ref, sems):
+def first_kernel(adj_ref, off_ref, g_hbm, diag_hbm, pre_hbm,
+                 out_ref, e0, e1, e2, e3, g_ref, diag_ref, pre_ref, sems):
     nt = adj_ref.shape[0]
 
     def copies(t):
         return [
-            pltpu.make_async_copy(off_hbm.at[:, :, t], off_ref.at[:, :, t], sems.at[0, t]),
+            pltpu.make_async_copy(g_hbm.at[t], g_ref.at[t], sems.at[0, t]),
             pltpu.make_async_copy(diag_hbm.at[:, t], diag_ref.at[:, t], sems.at[1, t]),
             pltpu.make_async_copy(pre_hbm.at[:, t], pre_ref.at[:, t], sems.at[2, t]),
-            pltpu.make_async_copy(g_hbm.at[t], g_ref.at[t], sems.at[3, t]),
         ]
 
-    whole = pltpu.make_async_copy(adj_hbm, adj_ref, sems.at[4, 0])
-    whole.start()
     for t in range(nt):
         for copy in copies(t):
             copy.start()
-    whole.wait()
 
     def layer(t, carry):
-        for copy in copies(t):
-            copy.wait()
-        local_layer(t, adj_ref, g_ref, off_ref, diag_ref, pre_ref, out_ref, (e0, e1, e2, e3))
+        def wait():
+            for copy in copies(t):
+                copy.wait()
+
+        local_layer(t, adj_ref, g_ref, off_ref, diag_ref, pre_ref, out_ref, (e0, e1, e2, e3), wait)
         return carry
 
     lax.fori_loop(0, nt, layer, 0)
@@ -131,21 +132,21 @@
 COST = pl.CostEstimate(flops=40_000_000, bytes_accessed=24_000_000, transcendentals=0)
 
 
-def first_part(adj, g, off, diag, pre):
-    nt, nv, nq, na = adj.shape
+def first_part(adj, off, g, diag, pre):
+    nt, nv, _, na = adj.shape
     out_shape = [jax.ShapeDtypeStruct(adj.shape, F32)]
     out_shape += [jax.ShapeDtypeStruct((nv, nv, nt, na), F32)] * 4
-    out_shape += [pltpu.VMEM(x.shape, x.dtype) for x in (g, off, diag, pre)]
+    out_shape += [pltpu.VMEM(x.shape, x.dtype) for x in (g, diag, pre)]
     return pl.pallas_call(
         first_kernel,
-        in_specs=[pl.BlockSpec(memory_space=pltpu.HBM)] * 5,
+        in_specs=[_vmem()] * 2 + [pl.BlockSpec(memory_space=pltpu.HBM)] * 3,
         out_specs=[_vmem()] * len(out_shape),
         out_shape=out_shape,
-        scratch_shapes=[pltpu.VMEM(adj.shape, F32), pltpu.SemaphoreType.DMA((5, nt))],
+        scratch_shapes=[pltpu.SemaphoreType.DMA((3, nt))],
         compiler_params=PARAMS,
         cost_estimate=COST,
         name="local_first",
-    )(adj, g, off, diag, pre)
+    )(adj, off, g, diag, pre)
 
 
 def second_part(adj, g, off, diag, pre):
@@ -206,47 +207,57 @@
 
 
 def final_kernel(adj_ref, even, odd, near, far, off_ref, pre_ref, e0, e1, e2, e3,
-                 side_ref, design_ref, cell_ref, out_ref, sums_ref, by_cell, picked):
+                 side_ref, design_ref, cell_ref, out_hbm, sums_ref, out_ref, by_cell, places, table, sems):
+    nt, nv, nq, na = adj_ref.shape
+    chunks = cell_ref.shape[0]
+    cell = cell_ref[...]
+    lane = lax.broadcasted_iota(jnp.int32, cell.shape, 1)
+    places[0:chunks, :] = (cell >> 7) * 8 + (cell >> (na.bit_length() - 1))
+    places[chunks : 2 * chunks, :] = (lane - cell) & 127
+    look_up = pltpu.make_async_copy(places, table, sems.at[0])
+    look_up.start()
     add_halos(adj_ref, even, odd, near, far, off_ref, pre_ref, (e0, e1, e2, e3), out_ref)
-    nt, nv, nq, na = adj_ref.shape
+    result = pltpu.make_async_copy(out_ref, out_hbm, sems.at[1])
+    result.start()
     halves = na // 128
+    pitch = 8 * halves + 1
     for t in range(nt):
         for i in range(nv):
             for qt in range(nq // 8):
                 for h in range(halves):
-                    first = ((t * nq + qt * 8) * halves + h) * 8 + i
-                    by_cell[pl.ds(first, 8, stride=8 * halves), :] = out_ref[
+                    first = (t * nq + qt * 8) * pitch + h * 8 + i
+                    by_cell[pl.ds(first, 8, stride=pitch), :] = out_ref[
                         t, i, qt * 8 : qt * 8 + 8, h * 128 : h * 128 + 128
                     ]
-    faces = design_ref.shape[1]
     lane = lax.broadcasted_iota(jnp.int32, (8, 128), 1)
-
-    def pick(f, carry):
-        cell = cell_ref[f]
-        row = pl.multiple_of(lax.shift_right_logical(cell, 7) * 8, 8)
-        tile = by_cell[pl.ds(row, 8), :]
-        kept = jnp.where(lane == (cell & 127), tile, 0.0)
-        picked[pl.ds(f, 8, stride=faces), :] = kept
-        return carry
-
-    lax.fori_loop(0, faces, pick, 0, unroll=32)
-    every = jnp.zeros((8, 128), F32)
-    upper = jnp.zeros((8, 128), F32)
-    for f0 in range(0, faces, 128):
-        on_upper = jnp.transpose(jnp.broadcast_to(side_ref[f0 // 128 : f0 // 128 + 1, :].astype(F32), (128, 128)))
+    field = lax.broadcasted_iota(jnp.int32, (8, 128), 0)
+    look_up.wait()
+
+    def chunk(k, carry):
+        every, upper = carry
+        side = jnp.broadcast_to(side_ref[pl.ds(k, 1), :].astype(F32), (8, 128))
+        picked = jnp.zeros((8, 128), F32)
+        for f in range(128):
+            tile = by_cell[pl.ds(table[k, f], 8), :]
+            picked = jnp.where(lane == f, pltpu.roll(tile, table[k + chunks, f], 1), picked)
+        by_face = jnp.transpose(jnp.where(field == 6, side, picked))
         contrib = jnp.zeros((128, 128), F32)
         for i in range(nv):
-            value = jnp.sum(picked[i * faces + f0 : i * faces + f0 + 128, :], axis=1, keepdims=True)
-            contrib = contrib + value * design_ref[i, f0 : f0 + 128, :]
+            contrib = contrib + by_face[:, i : i + 1] * design_ref[i, pl.ds(pl.multiple_of(k * 128, 128), 128), :]
         every = every + jnp.sum(contrib.reshape(16, 8, 128), axis=0)
-        upper = upper + jnp.sum((contrib * on_upper).reshape(16, 8, 128), axis=0)
+        upper = upper + jnp.sum((contrib * by_face[:, 6:7]).reshape(16, 8, 128), axis=0)
+        return every, upper
+
+    zero = jnp.zeros((8, 128), F32)
+    every, upper = lax.fori_loop(0, chunks, chunk, (zero, zero))
     upper = jnp.sum(upper, axis=0, keepdims=True)
     sums_ref[0:1, :] = jnp.sum(every, axis=0, keepdims=True) - upper
     sums_ref[1:2, :] = upper
+    result.wait()
 
 
 def halo_part(adj, halos, off, pre, edges, faces=None):
-    nt, nv, nq, na = adj.shape
+    nt, _, nq, na = adj.shape
     args = [adj, *halos, off, pre, *edges]
     cost = pl.CostEstimate(flops=4_000_000, bytes_accessed=5_000_000, transcendentals=0)
     out_shape = [jax.ShapeDtypeStruct(adj.shape, F32)]
@@ -259,10 +270,14 @@
     cell, side, design = faces
     out_shape += [jax.ShapeDtypeStruct((2, design.shape[2]), F32)]
     return pl.pallas_call(
-        final_kernel, in_specs=[_vmem()] * (len(args) + 2) + [_smem()], out_specs=[_vmem()] * 2, out_shape=out_shape,
+        final_kernel, in_specs=[_vmem()] * (len(args) + 3),
+        out_specs=[pl.BlockSpec(memory_space=pltpu.HBM), _vmem()], out_shape=out_shape,
         scratch_shapes=[
-            pltpu.VMEM((nt * nq * na // 128 * 8, 128), F32),
-            pltpu.VMEM((8 * design.shape[1], 128), F32),
+            pltpu.VMEM(adj.shape, F32),
+            pltpu.VMEM((nt * nq * (na // 16 + 1), 128), F32),
+            pltpu.VMEM((2 * cell.shape[0], 128), jnp.int32),
+            pltpu.SMEM((2 * cell.shape[0], 128), jnp.int32),
+            pltpu.SemaphoreType.DMA((2,)),
         ],
         compiler_params=PARAMS, cost_estimate=cost, name="halo_last",
     )(*args, side, design, cell)
@@ -281,15 +296,16 @@
 def combine(sums):
     nc = lax.axis_size("circ")
     nr = lax.axis_size("radax")
-    near = [(i, i ^ 1) for i in range(nr)]
-    both = sums + lax.ppermute(sums, "radax", near)
-    lower, upper = both[0:1], both[1:2]
-    ring = [(c * nr + r, (c + 1) % nc * nr + (r ^ 2 if r % 2 == 0 else r)) for c in range(nc) for r in range(nr)]
-    arrived = lax.ppermute(upper, ("circ", "radax"), ring)
+    lower, upper = sums[0:1], sums[1:2]
+
+    def ring(flip):
+        return [(c * nr + r, (c + 1) % nc * nr + (r ^ flip)) for c in range(nc) for r in range(nr)]
+
+    crossed = lax.ppermute(upper, ("circ", "radax"), ring(2))
+    straight = lax.ppermute(upper, ("circ", "radax"), ring(0))
     other = lax.ppermute(lower, "radax", [(i, i ^ 2) for i in range(nr)])
-    first = lax.axis_index("radax") % 2 == 0
-    mine = arrived + jnp.where(first, lower + other, 0.0)
-    return mine + lax.ppermute(mine, "radax", near)
+    mine = (lower + other) + (straight + crossed)
+    return mine + lax.ppermute(mine, "radax", [(i, i ^ 1) for i in range(nr)])
 
 
 def body(objective_grad, adjoint_start, jac_off, jac_diag, precond, face_cell, face_side, design_grad):
@@ -302,20 +318,24 @@
     nt, nv, nq, na = adj.shape
     ring = jax.ShapeDtypeStruct((nv, nq, na), F32)
     rows = jax.ShapeDtypeStruct((nv, nt, na), F32)
-    sends = pl.pallas_call(
-        faces_kernel, in_specs=[_vmem()], out_specs=[_vmem()] * 4,
-        out_shape=[ring, ring, rows, rows], name="faces",
-        compiler_params=PARAMS,
-    )(adj)
+    adj, *sends = pl.pallas_call(
+        faces_kernel, in_specs=[pl.BlockSpec(memory_space=pltpu.HBM)], out_specs=[_vmem()] * 5,
+        out_shape=[pltpu.VMEM(adj.shape, F32), ring, ring, rows, rows], name="faces",
+        scratch_shapes=[pltpu.SemaphoreType.DMA],
+        compiler_params=pltpu.CompilerParams(vmem_limit_bytes=4 << 20),
+        cost_estimate=pl.CostEstimate(flops=4_000_000_000, bytes_accessed=200_000_000, transcendentals=0),
+    )(pltpu.with_memory_space_constraint(adj, pltpu.HBM))
+    adj = pltpu.with_memory_space_constraint(adj, pltpu.VMEM)
     halos = swap_halos(*sends)
-    hbm = [pltpu.with_memory_space_constraint(x, pltpu.HBM) for x in (adj, g, off, diag, pre)]
-    part, *edges, g, off, diag, pre = first_part(*hbm)
-    g, off, diag, pre = [pltpu.with_memory_space_constraint(x, pltpu.VMEM) for x in (g, off, diag, pre)]
+    hbm = [pltpu.with_memory_space_constraint(x, pltpu.HBM) for x in (g, diag, pre)]
+    part, *edges, g, diag, pre = first_part(adj, off, *hbm)
+    g, diag, pre = [pltpu.with_memory_space_constraint(x, pltpu.VMEM) for x in (g, diag, pre)]
     adj, *sends = halo_part(part, halos, off, pre, edges)
     halos = swap_halos(*sends)
     part = second_part(adj, g, off, diag, pre)
+    cell = face_cell.reshape(-1, 128)
     side = face_side.reshape(-1, 128)
-    adj, sums = halo_part(part, halos, off, pre, edges, (face_cell, side, design))
+    adj, sums = halo_part(part, halos, off, pre, edges, (cell, side, design))
     total = combine(sums)
     nr = lax.axis_size("radax")
     owned = total.shape[1] // nr

time: 48.4 us -> 44.8 us (0.926)
  waiting for transfers between devices: 9.41 us -> 5.86 us
  starting transfers between devices: 19.8 us -> 22.9 us
  Pallas kernels: 16.6 us -> 14.6 us
  local copies, waits for them, and re-layouts: 1.73 us -> 0.6 us
    ppermute x1, waiting for transfers between devices: 3.83 us -> 0.01 us  [combine(): other = lax.ppermute(lower, 'radax', [(i, i ^ 2) for i in range(nr)])]
    pallas_call x3, Pallas kernels: 11.9 us -> 9.96 us  [the longest x1 5.66 us: first_part(): pl.pallas_call(first_kernel, in_specs=[_vmem()] * 2 + [pl.BlockSpec(memor...]
    ppermute x3, waiting for transfers between devices: 4.43 us -> 5.71 us  [the longest x1 4.28 us: combine(): crossed = lax.ppermute(upper, ('circ', 'radax'), ring(2))]
    ppermute x3, starting transfers between devices: 4.87 us -> 6.04 us  [the longest x1 3.29 us: combine(): return mine + lax.ppermute(mine, 'radax', [(i, i ^ 1) for i in range(nr)])]
    unnamed x8, local copies, waits for them, and re-layouts: 1.14 us -> 0.02 us
    ppermute x2, waiting for transfers between devices: 1.15 us -> 0.13 us  [swap_halos(): lax.ppermute(odd, 'circ', [(i, (i + 1) % nc if i % 2 else (i - 1) % nc) f...]
    ppermute x1, starting transfers between devices: 0.01 us -> 0.89 us  [combine(): other = lax.ppermute(lower, 'radax', [(i, i ^ 2) for i in range(nr)])]
    ppermute x2, starting transfers between devices: 3.96 us -> 4.68 us  [swap_halos(): far = lax.ppermute(far, 'radax', [(i, nr - 1 - i) for i in range(nr)])]
  transfers between devices with their start and end apart: 12 -> 12, of which waited for: 5 -> 4; matrix products, arithmetic and copies ran while one was open for 0% -> 0% of each run, Pallas kernels for 25% -> 22%
where the time goes in v3:
time: 44.8 us; the launch traced here: 44.7 us
  starting transfers between devices  22.9 us (51%)
  Pallas kernels  14.6 us (33%)
  waiting for transfers between devices  5.86 us (13%)
  between operations  0.76 us (2%)
  local copies, waits for them, and re-layouts  0.6 us (1%)
    ppermute x2, starting transfers between devices, swap_halos(): lax.ppermute(odd, 'circ', [(i, (i + 1) % nc if i % 2 else (i - 1) % nc) f...  6.51 us
    pallas_call x1, Pallas kernels, first_part(): pl.pallas_call(first_kernel, in_specs=[_vmem()] * 2 + [pl.BlockSpec(memor...  5.66 us
    ppermute x2, starting transfers between devices, swap_halos(): far = lax.ppermute(far, 'radax', [(i, nr - 1 - i) for i in range(nr)])  4.68 us
    ppermute x1, waiting for transfers between devices, combine(): crossed = lax.ppermute(upper, ('circ', 'radax'), ring(2))  4.28 us
    pallas_call x1, Pallas kernels, second_part(): pl.pallas_call(second_kernel, in_specs=[_vmem()] * 5, out_specs=_vmem(),...  4.19 us
    ppermute x1, starting transfers between devices, combine(): return mine + lax.ppermute(mine, 'radax', [(i, i ^ 1) for i in range(nr)])  3.29 us
    pallas_call x1, Pallas kernels, halo_part(): pl.pallas_call(final_kernel, in_specs=[_vmem()] * (len(args) + 3), out_sp...  2.94 us
    ppermute x2, starting transfers between devices, swap_halos(): near = lax.ppermute(near, 'radax', [(i, i ^ 1) for i in range(nr)])  2.47 us
  transfers between devices with their start and end apart: 12, of which 4 were waited for; matrix products, arithmetic and copies ran while one was open for 0% of the time, Pallas kernels for 22%

profile of v3, /device:TPU:1, one launch (start us, length us, event | category | flops | bytes accessed | tf_op | source)
XLA Modules:
  0.0 44.7 jit_solution(9001483163887039778)
XLA Ops:
  0.6 0.0 copy-start
  0.6 1.4 %faces.1 = (f32[8,6,16,256]{3,2,1,0:T(8,128)S(1)}, f32[6,16,256]{2,1,0:T(8,128)S(1)}, f32[6,16,256]{2,1,0:T(8,128)S(1)}, f32[6,8,256]{2,1,0:T(8,128)S(1)}, f32[6,8,256]{2,1,0:T(8,128)S(1)}) custom-call(f32[8,6,16,256]{3,2,1,0:T(8,128)} %bitcast.19), custom_call_target="tpu_custom_call" | custom-call | flops 4000000000 | bytes 200000000 | tf_op jit(solution)/shard_map/faces/pallas_call | solution.py:321
  2.0 2.2 %collective-permute-start = (f32[6,16,256]{2,1,0:T(8,128)S(1)}, f32[6,16,256]{2,1,0:T(8,128)S(1)}, u32[]{:S(2)}, u32[]{:S(2)}) collective-permute-start(f32[6,16,256]{2,1,0:T(8,128)S(1)} %get-tuple-element.24), channel_id=1, source_target_pairs={{0,4},{4,0},{8,12},{12,8},{16,20},{20,16},{24,28},{28,24},{32,36},... | collective-permute-start | bytes 294920 | tf_op jit(solution)/shard_map/ppermute | solution.py:291
  4.2 6.3 %collective-permute-start.1 = (f32[6,16,256]{2,1,0:T(8,128)S(1)}, f32[6,16,256]{2,1,0:T(8,128)S(1)}, u32[]{:S(2)}, u32[]{:S(2)}) collective-permute-start(f32[6,16,256]{2,1,0:T(8,128)S(1)} %get-tuple-element.25), channel_id=1, source_target_pairs={{0,124},{4,8},{8,4},{12,16},{16,12},{20,24},{24,20},{28,32},{32,28... | collective-permute-start | bytes 294920 | tf_op jit(solution)/shard_map/ppermute | solution.py:289
  10.5 1.2 %collective-permute-start.2 = (f32[6,8,256]{2,1,0:T(8,128)S(1)}, f32[6,8,256]{2,1,0:T(8,128)S(1)}, u32[]{:S(2)}, u32[]{:S(2)}) collective-permute-start(f32[6,8,256]{2,1,0:T(8,128)S(1)} %get-tuple-element.26), channel_id=1, source_target_pairs={{0,1},{1,0},{2,3},{3,2},{4,5},{5,4},{6,7},{7,6},{8,9},{9,8},{10,11... | collective-permute-start | bytes 147464 | tf_op jit(solution)/shard_map/ppermute | solution.py:292
  11.7 2.3 %collective-permute-start.3 = (f32[6,8,256]{2,1,0:T(8,128)S(1)}, f32[6,8,256]{2,1,0:T(8,128)S(1)}, u32[]{:S(2)}, u32[]{:S(2)}) collective-permute-start(f32[6,8,256]{2,1,0:T(8,128)S(1)} %get-tuple-element.27), channel_id=1, source_target_pairs={{0,3},{1,2},{2,1},{3,0},{4,7},{5,6},{6,5},{7,4},{8,11},{9,10},{10,... | collective-permute-start | bytes 147464 | tf_op jit(solution)/shard_map/ppermute | solution.py:290
  14.1 0.0 copy-done
  14.1 5.7 %local_first.1 = (f32[8,6,16,256]{3,2,1,0:T(8,128)S(1)}, f32[6,6,8,256]{3,2,1,0:T(8,128)S(1)}, f32[6,6,8,256]{3,2,1,0:T(8,128)S(1)}, f32[6,6,8,256]{3,2,1,0:T(8,...) custom-call(f32[8,6,16,256]{3,2,1,0:T(8,128)S(1)} %get-tuple-element, ...), custom_call_target="tpu_custom_call" | custom-call | flops 40000000 | bytes 24000000 | tf_op jit(solution)/shard_map/local_first/pallas_call | solution.py:140
  19.8 0.0 collective-permute-done.2.near
  19.8 0.0 collective-permute-done.3.far
  19.8 0.0 collective-permute-done.even
  19.8 0.0 collective-permute-done.1.odd
  19.8 0.5 %halo_first.1 = (f32[8,6,16,256]{3,2,1,0:T(8,128)S(1)}, f32[6,16,256]{2,1,0:T(8,128)S(1)}, f32[6,16,256]{2,1,0:T(8,128)S(1)}, f32[6,8,256]{2,1,0:T(8,128)S(1)}, f32[6,8,256]{2,1,0:T(8,128)S(1)}) custom-call(f32[8,6,16,256]{3,2,1,0:T(8,128)S(1)} %get-tuple-element.23.adj_ref, f32[6,16,256]{2,1,0:T(8,128)S(1)} %collective-permute-done.even, ...), custom_call_target="tpu_custom_call" | custom-call | flops 4000000 | bytes 5000000 | tf_op jit(solution)/shard_map/halo_first/pallas_call | solution.py:266
  20.3 0.1 collective-permute-start.4
  20.4 0.2 collective-permute-start.5
  20.6 1.2 %collective-permute-start.6 = (f32[6,8,256]{2,1,0:T(8,128)S(1)}, f32[6,8,256]{2,1,0:T(8,128)S(1)}, u32[]{:S(2)}, u32[]{:S(2)}) collective-permute-start(f32[6,8,256]{2,1,0:T(8,128)S(1)} %get-tuple-element.38), channel_id=1, source_target_pairs={{0,1},{1,0},{2,3},{3,2},{4,5},{5,4},{6,7},{7,6},{8,9},{9,8},{10,11... | collective-permute-start | bytes 147464 | tf_op jit(solution)/shard_map/ppermute | solution.py:292
  21.8 2.3 %collective-permute-start.7 = (f32[6,8,256]{2,1,0:T(8,128)S(1)}, f32[6,8,256]{2,1,0:T(8,128)S(1)}, u32[]{:S(2)}, u32[]{:S(2)}) collective-permute-start(f32[6,8,256]{2,1,0:T(8,128)S(1)} %get-tuple-element.39), channel_id=1, source_target_pairs={{0,3},{1,2},{2,1},{3,0},{4,7},{5,6},{6,5},{7,4},{8,11},{9,10},{10,... | collective-permute-start | bytes 147464 | tf_op jit(solution)/shard_map/ppermute | solution.py:290
  24.2 0.0 copy-start.1
  24.2 0.0 copy-start.2
  24.2 0.0 copy-start.3
  24.2 4.2 %local_second.1.adj_ref = f32[8,6,16,256]{3,2,1,0:T(8,128)S(1)} custom-call(f32[8,6,16,256]{3,2,1,0:T(8,128)S(1)} %get-tuple-element.33.adj_ref, f32[8,6,16,256]{3,2,1,0:T(8,128)S(1)} %get-tuple-element.34.g_ref, bf16[6,6,8,6,16,256]{5,4,3,2,1,0:T(8,128)(2,1)S(1)} %bitcast.11, bf16[6,8,6,16,256]{4,3,2,1,0:T(8,128)(2,1)S(1)} %get-tuple-element.35.diag_ref, ...), custom_call_target="tpu_custom_call" | custom-call | flops 40000000 | bytes 24000000 | tf_op jit(solution)/shard_map/local_second/pallas_call | solution.py:153
  28.4 0.0 collective-permute-done.6.near
  28.4 0.0 collective-permute-done.7.far
  28.4 0.0 collective-permute-done.4.even
  28.4 0.1 collective-permute-done.5.odd
  28.5 0.0 copy-done.1
  28.5 0.0 copy-done.2
  28.5 0.0 copy-done.3
  28.5 2.9 %halo_last.1 = (f32[8,6,16,256]{3,2,1,0:T(8,128)}, f32[2,128]{1,0:T(2,128)S(1)}) custom-call(f32[8,6,16,256]{3,2,1,0:T(8,128)S(1)} %local_second.1.adj_ref, f32[6,16,256]{2,1,0:T(8,128)S(1)} %collective-permute-done.4.even, f32[6,16,256]{2,1,0:T(8,128)S(1)} %collective-permute-done.5.odd, f32[6,8,256]{2,1,0:T(8,128)S(1)} %collective-permute-done.6.near, ...), custom_call_target="tpu_custom_call" | custom-call | flops 4000000 | bytes 5000000 | tf_op jit(solution)/shard_map/halo_last/pallas_call | solution.py:272
  31.5 1.0 %collective-permute-start.10 = (f32[1,128]{1,0:T(1,128)S(1)}, f32[1,128]{1,0:T(1,128)S(1)}, u32[]{:S(2)}, u32[]{:S(2)}) collective-permute-start(f32[1,128]{1,0:T(1,128)S(1)} %get-tuple-element.43), channel_id=1, source_target_pairs={{0,6},{1,7},{2,4},{3,5},{4,10},{5,11},{6,8},{7,9},{8,14},{9,15},{1... | collective-permute-start | bytes 1544 | tf_op jit(solution)/shard_map/ppermute | solution.py:304
  32.5 0.9 %collective-permute-start.8 = (f32[1,128]{1,0:T(1,128)S(1)}, f32[1,128]{1,0:T(1,128)S(1)}, u32[]{:S(2)}, u32[]{:S(2)}) collective-permute-start(f32[1,128]{1,0:T(1,128)S(1)} %get-tuple-element.42), channel_id=1, source_target_pairs={{0,2},{1,3},{2,0},{3,1},{4,6},{5,7},{6,4},{7,5},{8,10},{9,11},{10,... | collective-permute-start | bytes 1544 | tf_op jit(solution)/shard_map/ppermute | solution.py:306
  33.4 1.7 %collective-permute-start.9 = (f32[1,128]{1,0:T(1,128)S(1)}, f32[1,128]{1,0:T(1,128)S(1)}, u32[]{:S(2)}, u32[]{:S(2)}) collective-permute-start(f32[1,128]{1,0:T(1,128)S(1)} %get-tuple-element.43), channel_id=1, source_target_pairs={{0,4},{1,5},{2,6},{3,7},{4,8},{5,9},{6,10},{7,11},{8,12},{9,13},{1... | collective-permute-start | bytes 1544 | tf_op jit(solution)/shard_map/ppermute | solution.py:305
  35.1 4.3 %collective-permute-done.10 = f32[1,128]{1,0:T(1,128)S(1)} collective-permute-done((f32[1,128]{1,0:T(1,128)S(1)}, f32[1,128]{1,0:T(1,128)S(1)}, u32[]{:S(2)}, u32[]{:S(2)}) %collective-permute-start.10) | collective-permute-done | bytes 544 | tf_op jit(solution)/shard_map/ppermute | solution.py:304
  39.4 0.0 collective-permute-done.8
  39.4 0.6 %collective-permute-done.9 = f32[1,128]{1,0:T(1,128)S(1)} collective-permute-done((f32[1,128]{1,0:T(1,128)S(1)}, f32[1,128]{1,0:T(1,128)S(1)}, u32[]{:S(2)}, u32[]{:S(2)}) %collective-permute-start.9) | collective-permute-done | bytes 544 | tf_op jit(solution)/shard_map/ppermute | solution.py:305
  40.0 3.3 %collective-permute-start.11 = (f32[1,128]{1,0:T(1,128)S(1)}, f32[1,128]{1,0:T(1,128)S(1)}, u32[]{:S(2)}, u32[]{:S(2)}) collective-permute-start(f32[1,128]{1,0:T(1,128)S(1)} %add_add_fusion), channel_id=1, source_target_pairs={{0,1},{1,0},{2,3},{3,2},{4,5},{5,4},{6,7},{7,6},{8,9},{9,8},{10,11... | collective-permute-start | bytes 1544 | tf_op jit(solution)/shard_map/ppermute | solution.py:308
  43.3 0.8 %collective-permute-done.11 = f32[1,128]{1,0:T(1,128)S(1)} collective-permute-done((f32[1,128]{1,0:T(1,128)S(1)}, f32[1,128]{1,0:T(1,128)S(1)}, u32[]{:S(2)}, u32[]{:S(2)}) %collective-permute-start.11) | collective-permute-done | bytes 544 | tf_op jit(solution)/shard_map/ppermute | solution.py:308
  44.2 0.6 %constant_dynamic-slice_fusion = f32[1,32]{1,0:T(1,128)} fusion(f32[1,128]{1,0:T(1,128)S(1)} %add.18, s32[]{:T(128)S(6)} %select_n.3), kind=kLoop, calls=%fused_computation.1 | loop fusion | bytes 260 | tf_op jit(solution)/shard_map/dynamic_slice | solution.py:342
  (3 shorter events, 0.0 us)
Async XLA Ops:
  0.6 13.5 %copy-start = (bf16[6,6,8,16,6,256]{5,3,4,2,1,0:T(8,128)(2,1)S(1)}, bf16[6,6,8,16,6,256]{5,3,4,2,1,0:T(8,128)(2,1)}, u32[]{:S(2)}) copy-start(bf16[6,6,8,16,6,256]{5,3,4,2,1,0:T(8,128)(2,1)} %param.10) | copy-start | bytes 42467332
  2.0 17.8 %collective-permute-start = (f32[6,16,256]{2,1,0:T(8,128)S(1)}, f32[6,16,256]{2,1,0:T(8,128)S(1)}, u32[]{:S(2)}, u32[]{:S(2)}) collective-permute-start(f32[6,16,256]{2,1,0:T(8,128)S(1)} %get-tuple-element.24), channel_id=1, source_target_pairs={{0,4},{4,0},{8,12},{12,8},{16,20},{20,16},{24,28},{28,24},{32,36},... | collective-permute-start | bytes 294920 | tf_op jit(solution)/shard_map/ppermute | solution.py:291
  4.2 15.6 %collective-permute-start.1 = (f32[6,16,256]{2,1,0:T(8,128)S(1)}, f32[6,16,256]{2,1,0:T(8,128)S(1)}, u32[]{:S(2)}, u32[]{:S(2)}) collective-permute-start(f32[6,16,256]{2,1,0:T(8,128)S(1)} %get-tuple-element.25), channel_id=1, source_target_pairs={{0,124},{4,8},{8,4},{12,16},{16,12},{20,24},{24,20},{28,32},{32,28... | collective-permute-start | bytes 294920 | tf_op jit(solution)/shard_map/ppermute | solution.py:289
  10.5 9.2 %collective-permute-start.2 = (f32[6,8,256]{2,1,0:T(8,128)S(1)}, f32[6,8,256]{2,1,0:T(8,128)S(1)}, u32[]{:S(2)}, u32[]{:S(2)}) collective-permute-start(f32[6,8,256]{2,1,0:T(8,128)S(1)} %get-tuple-element.26), channel_id=1, source_target_pairs={{0,1},{1,0},{2,3},{3,2},{4,5},{5,4},{6,7},{7,6},{8,9},{9,8},{10,11... | collective-permute-start | bytes 147464 | tf_op jit(solution)/shard_map/ppermute | solution.py:292
  11.7 8.0 %collective-permute-start.3 = (f32[6,8,256]{2,1,0:T(8,128)S(1)}, f32[6,8,256]{2,1,0:T(8,128)S(1)}, u32[]{:S(2)}, u32[]{:S(2)}) collective-permute-start(f32[6,8,256]{2,1,0:T(8,128)S(1)} %get-tuple-element.27), channel_id=1, source_target_pairs={{0,3},{1,2},{2,1},{3,0},{4,7},{5,6},{6,5},{7,4},{8,11},{9,10},{10,... | collective-permute-start | bytes 147464 | tf_op jit(solution)/shard_map/ppermute | solution.py:290
  20.3 8.1 %collective-permute-start.4 = (f32[6,16,256]{2,1,0:T(8,128)S(1)}, f32[6,16,256]{2,1,0:T(8,128)S(1)}, u32[]{:S(2)}, u32[]{:S(2)}) collective-permute-start(f32[6,16,256]{2,1,0:T(8,128)S(1)} %get-tuple-element.36), channel_id=1, source_target_pairs={{0,4},{4,0},{8,12},{12,8},{16,20},{20,16},{24,28},{28,24},{32,36},... | collective-permute-start | bytes 294920 | tf_op jit(solution)/shard_map/ppermute | solution.py:291
  20.4 8.1 %collective-permute-start.5 = (f32[6,16,256]{2,1,0:T(8,128)S(1)}, f32[6,16,256]{2,1,0:T(8,128)S(1)}, u32[]{:S(2)}, u32[]{:S(2)}) collective-permute-start(f32[6,16,256]{2,1,0:T(8,128)S(1)} %get-tuple-element.37), channel_id=1, source_target_pairs={{0,124},{4,8},{8,4},{12,16},{16,12},{20,24},{24,20},{28,32},{32,28... | collective-permute-start | bytes 294920 | tf_op jit(solution)/shard_map/ppermute | solution.py:289
  20.6 7.8 %collective-permute-start.6 = (f32[6,8,256]{2,1,0:T(8,128)S(1)}, f32[6,8,256]{2,1,0:T(8,128)S(1)}, u32[]{:S(2)}, u32[]{:S(2)}) collective-permute-start(f32[6,8,256]{2,1,0:T(8,128)S(1)} %get-tuple-element.38), channel_id=1, source_target_pairs={{0,1},{1,0},{2,3},{3,2},{4,5},{5,4},{6,7},{7,6},{8,9},{9,8},{10,11... | collective-permute-start | bytes 147464 | tf_op jit(solution)/shard_map/ppermute | solution.py:292
  21.8 6.6 %collective-permute-start.7 = (f32[6,8,256]{2,1,0:T(8,128)S(1)}, f32[6,8,256]{2,1,0:T(8,128)S(1)}, u32[]{:S(2)}, u32[]{:S(2)}) collective-permute-start(f32[6,8,256]{2,1,0:T(8,128)S(1)} %get-tuple-element.39), channel_id=1, source_target_pairs={{0,3},{1,2},{2,1},{3,0},{4,7},{5,6},{6,5},{7,4},{8,11},{9,10},{10,... | collective-permute-start | bytes 147464 | tf_op jit(solution)/shard_map/ppermute | solution.py:290
  24.2 4.4 %copy-start.1 = (f32[512,6,128]{2,0,1:T(8,128)S(1)}, f32[512,6,128]{2,0,1:T(8,128)}, u32[]{:S(2)}) copy-start(f32[512,6,128]{2,0,1:T(8,128)} %param.15) | copy-start | bytes 4718596
  24.2 4.4 %copy-start.2 = (s32[512]{0:T(512)S(1)}, s32[512]{0:T(512)}, u32[]{:S(2)}) copy-start(s32[512]{0:T(512)} %param.14) | copy-start | bytes 6148
  24.2 4.4 %copy-start.3 = (s32[512]{0:T(512)S(1)}, s32[512]{0:T(512)}, u32[]{:S(2)}) copy-start(s32[512]{0:T(512)} %param.13) | copy-start | bytes 6148
  31.5 7.9 %collective-permute-start.10 = (f32[1,128]{1,0:T(1,128)S(1)}, f32[1,128]{1,0:T(1,128)S(1)}, u32[]{:S(2)}, u32[]{:S(2)}) collective-permute-start(f32[1,128]{1,0:T(1,128)S(1)} %get-tuple-element.43), channel_id=1, source_target_pairs={{0,6},{1,7},{2,4},{3,5},{4,10},{5,11},{6,8},{7,9},{8,14},{9,15},{1... | collective-permute-start | bytes 1544 | tf_op jit(solution)/shard_map/ppermute | solution.py:304
  32.5 6.9 %collective-permute-start.8 = (f32[1,128]{1,0:T(1,128)S(1)}, f32[1,128]{1,0:T(1,128)S(1)}, u32[]{:S(2)}, u32[]{:S(2)}) collective-permute-start(f32[1,128]{1,0:T(1,128)S(1)} %get-tuple-element.42), channel_id=1, source_target_pairs={{0,2},{1,3},{2,0},{3,1},{4,6},{5,7},{6,4},{7,5},{8,10},{9,11},{10,... | collective-permute-start | bytes 1544 | tf_op jit(solution)/shard_map/ppermute | solution.py:306
  33.4 6.6 %collective-permute-start.9 = (f32[1,128]{1,0:T(1,128)S(1)}, f32[1,128]{1,0:T(1,128)S(1)}, u32[]{:S(2)}, u32[]{:S(2)}) collective-permute-start(f32[1,128]{1,0:T(1,128)S(1)} %get-tuple-element.43), channel_id=1, source_target_pairs={{0,4},{1,5},{2,6},{3,7},{4,8},{5,9},{6,10},{7,11},{8,12},{9,13},{1... | collective-permute-start | bytes 1544 | tf_op jit(solution)/shard_map/ppermute | solution.py:305
  40.0 4.1 %collective-permute-start.11 = (f32[1,128]{1,0:T(1,128)S(1)}, f32[1,128]{1,0:T(1,128)S(1)}, u32[]{:S(2)}, u32[]{:S(2)}) collective-permute-start(f32[1,128]{1,0:T(1,128)S(1)} %add_add_fusion), channel_id=1, source_target_pairs={{0,1},{1,0},{2,3},{3,2},{4,5},{5,4},{6,7},{7,6},{8,9},{9,8},{10,11... | collective-permute-start | bytes 1544 | tf_op jit(solution)/shard_map/ppermute | solution.py:308

commit v4 on v3

--- a/solution.py
+++ b/solution.py
@@ -49,6 +49,11 @@
     row = lax.broadcasted_iota(jnp.int32, plane.shape, 0)
     edge = 0 if step == 1 else rows - 1
     return jnp.where(row == edge, 0.0, pltpu.roll(plane, step % rows, 0))
+
+
+def keep_row(rows_ref, t, plane, q):
+    here = lax.broadcasted_iota(jnp.int32, rows_ref.shape, 0) == t
+    pltpu.store(rows_ref, jnp.broadcast_to(plane[q : q + 1, :], rows_ref.shape), mask=here)
 
 
 def local_layer(t, adj_ref, g_ref, off_ref, diag_ref, pre_ref, out_ref, edge_refs=(), wait=None):
@@ -72,10 +77,8 @@
             for i in range(nv):
                 block = off_ref[k, j, t, i].astype(F32)
                 acc[i] = acc[i] + block * fields[k]
-                if edge_refs and k == 2:
-                    edge_refs[0][j, i, pl.ds(t, 1), :] = block[0:1, :]
-                if edge_refs and k == 3:
-                    edge_refs[1][j, i, pl.ds(t, 1), :] = block[nq - 1 : nq, :]
+                if edge_refs and k in (2, 3):
+                    keep_row(edge_refs[k - 2].at[j, i], t, block, 0 if k == 2 else nq - 1)
     if wait is not None:
         wait()
     for j in range(nv):
@@ -89,8 +92,8 @@
             block = pre_ref[j, t, i].astype(F32)
             new[i] = new[i] + block * acc[j]
             if edge_refs:
-                edge_refs[2][j, i, pl.ds(t, 1), :] = block[0:1, :]
-                edge_refs[3][j, i, pl.ds(t, 1), :] = block[nq - 1 : nq, :]
+                keep_row(edge_refs[2].at[j, i], t, block, 0)
+                keep_row(edge_refs[3].at[j, i], t, block, nq - 1)
     for i in range(nv):
         out_ref[t, i] = new[i]
 
@@ -233,9 +236,10 @@
     field = lax.broadcasted_iota(jnp.int32, (8, 128), 0)
     look_up.wait()
 
-    def chunk(k, carry):
-        every, upper = carry
-        side = jnp.broadcast_to(side_ref[pl.ds(k, 1), :].astype(F32), (8, 128))
+    every = jnp.zeros((8, 128), F32)
+    upper = jnp.zeros((8, 128), F32)
+    for k in range(chunks):
+        side = jnp.broadcast_to(side_ref[k : k + 1, :].astype(F32), (8, 128))
         picked = jnp.zeros((8, 128), F32)
         for f in range(128):
             tile = by_cell[pl.ds(table[k, f], 8), :]
@@ -243,13 +247,9 @@
         by_face = jnp.transpose(jnp.where(field == 6, side, picked))
         contrib = jnp.zeros((128, 128), F32)
         for i in range(nv):
-            contrib = contrib + by_face[:, i : i + 1] * design_ref[i, pl.ds(pl.multiple_of(k * 128, 128), 128), :]
+            contrib = contrib + by_face[:, i : i + 1] * design_ref[i, k * 128 : k * 128 + 128, :]
         every = every + jnp.sum(contrib.reshape(16, 8, 128), axis=0)
         upper = upper + jnp.sum((contrib * by_face[:, 6:7]).reshape(16, 8, 128), axis=0)
-        return every, upper
-
-    zero = jnp.zeros((8, 128), F32)
-    every, upper = lax.fori_loop(0, chunks, chunk, (zero, zero))
     upper = jnp.sum(upper, axis=0, keepdims=True)
     sums_ref[0:1, :] = jnp.sum(every, axis=0, keepdims=True) - upper
     sums_ref[1:2, :] = upper

time: 44.8 us -> 44.2 us (0.987)
  Pallas kernels: 14.6 us -> 14 us
  transfers between devices with their start and end apart: 12 -> 12, of which waited for: 4 -> 3; matrix products, arithmetic and copies ran while one was open for 0% -> 0% of each run, Pallas kernels for 22% -> 22%
where the time goes in v4:
time: 44.2 us; the launch traced here: 44.1 us
  starting transfers between devices  22.8 us (52%)
  Pallas kernels  14 us (32%)
  waiting for transfers between devices  5.88 us (13%)
  between operations  0.79 us (2%)
  local copies, waits for them, and re-layouts  0.6 us (1%)
    ppermute x2, starting transfers between devices, swap_halos(): lax.ppermute(odd, 'circ', [(i, (i + 1) % nc if i % 2 else (i - 1) % nc) f...  6.51 us
    pallas_call x1, Pallas kernels, first_part(): pl.pallas_call(first_kernel, in_specs=[_vmem()] * 2 + [pl.BlockSpec(memor...  5.32 us
    ppermute x2, starting transfers between devices, swap_halos(): far = lax.ppermute(far, 'radax', [(i, nr - 1 - i) for i in range(nr)])  4.95 us
    ppermute x1, waiting for transfers between devices, combine(): crossed = lax.ppermute(upper, ('circ', 'radax'), ring(2))  4.46 us
    pallas_call x1, Pallas kernels, second_part(): pl.pallas_call(second_kernel, in_specs=[_vmem()] * 5, out_specs=_vmem(),...  4.19 us
    ppermute x1, starting transfers between devices, combine(): return mine + lax.ppermute(mine, 'radax', [(i, i ^ 1) for i in range(nr)])  3.14 us
    pallas_call x1, Pallas kernels, halo_part(): pl.pallas_call(final_kernel, in_specs=[_vmem()] * (len(args) + 3), out_sp...  2.63 us
    ppermute x2, starting transfers between devices, swap_halos(): near = lax.ppermute(near, 'radax', [(i, i ^ 1) for i in range(nr)])  2.47 us
  transfers between devices with their start and end apart: 12, of which 3 were waited for; matrix products, arithmetic and copies ran while one was open for 0% of the time, Pallas kernels for 22%

profile of v4, /device:TPU:1, one launch (start us, length us, event | category | flops | bytes accessed | tf_op | source)
XLA Modules:
  0.0 44.1 jit_solution(4152013040044511547)
XLA Ops:
  0.6 0.0 copy-start
  0.6 1.4 %faces.1 = (f32[8,6,16,256]{3,2,1,0:T(8,128)S(1)}, f32[6,16,256]{2,1,0:T(8,128)S(1)}, f32[6,16,256]{2,1,0:T(8,128)S(1)}, f32[6,8,256]{2,1,0:T(8,128)S(1)}, f32[6,8,256]{2,1,0:T(8,128)S(1)}) custom-call(f32[8,6,16,256]{3,2,1,0:T(8,128)} %bitcast.19), custom_call_target="tpu_custom_call" | custom-call | flops 4000000000 | bytes 200000000 | tf_op jit(solution)/shard_map/faces/pallas_call | solution.py:321
  2.0 2.2 %collective-permute-start = (f32[6,16,256]{2,1,0:T(8,128)S(1)}, f32[6,16,256]{2,1,0:T(8,128)S(1)}, u32[]{:S(2)}, u32[]{:S(2)}) collective-permute-start(f32[6,16,256]{2,1,0:T(8,128)S(1)} %get-tuple-element.24), channel_id=1, source_target_pairs={{0,4},{4,0},{8,12},{12,8},{16,20},{20,16},{24,28},{28,24},{32,36},... | collective-permute-start | bytes 294920 | tf_op jit(solution)/shard_map/ppermute | solution.py:291
  4.2 6.3 %collective-permute-start.1 = (f32[6,16,256]{2,1,0:T(8,128)S(1)}, f32[6,16,256]{2,1,0:T(8,128)S(1)}, u32[]{:S(2)}, u32[]{:S(2)}) collective-permute-start(f32[6,16,256]{2,1,0:T(8,128)S(1)} %get-tuple-element.25), channel_id=1, source_target_pairs={{0,124},{4,8},{8,4},{12,16},{16,12},{20,24},{24,20},{28,32},{32,28... | collective-permute-start | bytes 294920 | tf_op jit(solution)/shard_map/ppermute | solution.py:289
  10.5 1.2 %collective-permute-start.2 = (f32[6,8,256]{2,1,0:T(8,128)S(1)}, f32[6,8,256]{2,1,0:T(8,128)S(1)}, u32[]{:S(2)}, u32[]{:S(2)}) collective-permute-start(f32[6,8,256]{2,1,0:T(8,128)S(1)} %get-tuple-element.26), channel_id=1, source_target_pairs={{0,1},{1,0},{2,3},{3,2},{4,5},{5,4},{6,7},{7,6},{8,9},{9,8},{10,11... | collective-permute-start | bytes 147464 | tf_op jit(solution)/shard_map/ppermute | solution.py:292
  11.7 2.3 %collective-permute-start.3 = (f32[6,8,256]{2,1,0:T(8,128)S(1)}, f32[6,8,256]{2,1,0:T(8,128)S(1)}, u32[]{:S(2)}, u32[]{:S(2)}) collective-permute-start(f32[6,8,256]{2,1,0:T(8,128)S(1)} %get-tuple-element.27), channel_id=1, source_target_pairs={{0,3},{1,2},{2,1},{3,0},{4,7},{5,6},{6,5},{7,4},{8,11},{9,10},{10,... | collective-permute-start | bytes 147464 | tf_op jit(solution)/shard_map/ppermute | solution.py:290
  14.1 0.0 copy-done
  14.1 5.3 %local_first.1 = (f32[8,6,16,256]{3,2,1,0:T(8,128)S(1)}, f32[6,6,8,256]{3,2,1,0:T(8,128)S(1)}, f32[6,6,8,256]{3,2,1,0:T(8,128)S(1)}, f32[6,6,8,256]{3,2,1,0:T(8,...) custom-call(f32[8,6,16,256]{3,2,1,0:T(8,128)S(1)} %get-tuple-element, ...), custom_call_target="tpu_custom_call" | custom-call | flops 40000000 | bytes 24000000 | tf_op jit(solution)/shard_map/local_first/pallas_call | solution.py:143
  19.4 0.0 collective-permute-done.2.near
  19.4 0.0 collective-permute-done.3.far
  19.4 0.0 collective-permute-done.even
  19.4 0.0 collective-permute-done.1.odd
  19.5 0.5 %halo_first.1 = (f32[8,6,16,256]{3,2,1,0:T(8,128)S(1)}, f32[6,16,256]{2,1,0:T(8,128)S(1)}, f32[6,16,256]{2,1,0:T(8,128)S(1)}, f32[6,8,256]{2,1,0:T(8,128)S(1)}, f32[6,8,256]{2,1,0:T(8,128)S(1)}) custom-call(f32[8,6,16,256]{3,2,1,0:T(8,128)S(1)} %get-tuple-element.23.adj_ref, f32[6,16,256]{2,1,0:T(8,128)S(1)} %collective-permute-done.even, ...), custom_call_target="tpu_custom_call" | custom-call | flops 4000000 | bytes 5000000 | tf_op jit(solution)/shard_map/halo_first/pallas_call | solution.py:266
  19.9 0.1 collective-permute-start.4
  20.0 0.2 collective-permute-start.5
  20.3 1.2 %collective-permute-start.6 = (f32[6,8,256]{2,1,0:T(8,128)S(1)}, f32[6,8,256]{2,1,0:T(8,128)S(1)}, u32[]{:S(2)}, u32[]{:S(2)}) collective-permute-start(f32[6,8,256]{2,1,0:T(8,128)S(1)} %get-tuple-element.38), channel_id=1, source_target_pairs={{0,1},{1,0},{2,3},{3,2},{4,5},{5,4},{6,7},{7,6},{8,9},{9,8},{10,11... | collective-permute-start | bytes 147464 | tf_op jit(solution)/shard_map/ppermute | solution.py:292
  21.5 2.6 %collective-permute-start.7 = (f32[6,8,256]{2,1,0:T(8,128)S(1)}, f32[6,8,256]{2,1,0:T(8,128)S(1)}, u32[]{:S(2)}, u32[]{:S(2)}) collective-permute-start(f32[6,8,256]{2,1,0:T(8,128)S(1)} %get-tuple-element.39), channel_id=1, source_target_pairs={{0,3},{1,2},{2,1},{3,0},{4,7},{5,6},{6,5},{7,4},{8,11},{9,10},{10,... | collective-permute-start | bytes 147464 | tf_op jit(solution)/shard_map/ppermute | solution.py:290
  24.1 0.0 copy-start.1
  24.1 0.0 copy-start.2
  24.1 0.0 copy-start.3
  24.1 4.2 %local_second.1.adj_ref = f32[8,6,16,256]{3,2,1,0:T(8,128)S(1)} custom-call(f32[8,6,16,256]{3,2,1,0:T(8,128)S(1)} %get-tuple-element.33.adj_ref, f32[8,6,16,256]{3,2,1,0:T(8,128)S(1)} %get-tuple-element.34.g_ref, bf16[6,6,8,6,16,256]{5,4,3,2,1,0:T(8,128)(2,1)S(1)} %bitcast.11, bf16[6,8,6,16,256]{4,3,2,1,0:T(8,128)(2,1)S(1)} %get-tuple-element.35.diag_ref, ...), custom_call_target="tpu_custom_call" | custom-call | flops 40000000 | bytes 24000000 | tf_op jit(solution)/shard_map/local_second/pallas_call | solution.py:156
  28.3 0.0 collective-permute-done.6.near
  28.3 0.0 collective-permute-done.7.far
  28.3 0.0 collective-permute-done.4.even
  28.3 0.0 collective-permute-done.5.odd
  28.3 0.0 copy-done.1
  28.4 0.0 copy-done.2
  28.4 0.0 copy-done.3
  28.4 2.6 %halo_last.1 = (f32[8,6,16,256]{3,2,1,0:T(8,128)}, f32[2,128]{1,0:T(2,128)S(1)}) custom-call(f32[8,6,16,256]{3,2,1,0:T(8,128)S(1)} %local_second.1.adj_ref, f32[6,16,256]{2,1,0:T(8,128)S(1)} %collective-permute-done.4.even, f32[6,16,256]{2,1,0:T(8,128)S(1)} %collective-permute-done.5.odd, f32[6,8,256]{2,1,0:T(8,128)S(1)} %collective-permute-done.6.near, ...), custom_call_target="tpu_custom_call" | custom-call | flops 4000000 | bytes 5000000 | tf_op jit(solution)/shard_map/halo_last/pallas_call | solution.py:272
  31.0 0.8 %collective-permute-start.10 = (f32[1,128]{1,0:T(1,128)S(1)}, f32[1,128]{1,0:T(1,128)S(1)}, u32[]{:S(2)}, u32[]{:S(2)}) collective-permute-start(f32[1,128]{1,0:T(1,128)S(1)} %get-tuple-element.43), channel_id=1, source_target_pairs={{0,6},{1,7},{2,4},{3,5},{4,10},{5,11},{6,8},{7,9},{8,14},{9,15},{1... | collective-permute-start | bytes 1544 | tf_op jit(solution)/shard_map/ppermute | solution.py:304
  31.8 0.9 %collective-permute-start.8 = (f32[1,128]{1,0:T(1,128)S(1)}, f32[1,128]{1,0:T(1,128)S(1)}, u32[]{:S(2)}, u32[]{:S(2)}) collective-permute-start(f32[1,128]{1,0:T(1,128)S(1)} %get-tuple-element.42), channel_id=1, source_target_pairs={{0,2},{1,3},{2,0},{3,1},{4,6},{5,7},{6,4},{7,5},{8,10},{9,11},{10,... | collective-permute-start | bytes 1544 | tf_op jit(solution)/shard_map/ppermute | solution.py:306
  32.7 1.7 %collective-permute-start.9 = (f32[1,128]{1,0:T(1,128)S(1)}, f32[1,128]{1,0:T(1,128)S(1)}, u32[]{:S(2)}, u32[]{:S(2)}) collective-permute-start(f32[1,128]{1,0:T(1,128)S(1)} %get-tuple-element.43), channel_id=1, source_target_pairs={{0,4},{1,5},{2,6},{3,7},{4,8},{5,9},{6,10},{7,11},{8,12},{9,13},{1... | collective-permute-start | bytes 1544 | tf_op jit(solution)/shard_map/ppermute | solution.py:305
  34.5 4.5 %collective-permute-done.10 = f32[1,128]{1,0:T(1,128)S(1)} collective-permute-done((f32[1,128]{1,0:T(1,128)S(1)}, f32[1,128]{1,0:T(1,128)S(1)}, u32[]{:S(2)}, u32[]{:S(2)}) %collective-permute-start.10) | collective-permute-done | bytes 544 | tf_op jit(solution)/shard_map/ppermute | solution.py:304
  38.9 0.0 collective-permute-done.8
  38.9 0.6 %collective-permute-done.9 = f32[1,128]{1,0:T(1,128)S(1)} collective-permute-done((f32[1,128]{1,0:T(1,128)S(1)}, f32[1,128]{1,0:T(1,128)S(1)}, u32[]{:S(2)}, u32[]{:S(2)}) %collective-permute-start.9) | collective-permute-done | bytes 544 | tf_op jit(solution)/shard_map/ppermute | solution.py:305
  39.5 3.1 %collective-permute-start.11 = (f32[1,128]{1,0:T(1,128)S(1)}, f32[1,128]{1,0:T(1,128)S(1)}, u32[]{:S(2)}, u32[]{:S(2)}) collective-permute-start(f32[1,128]{1,0:T(1,128)S(1)} %add_add_fusion), channel_id=1, source_target_pairs={{0,1},{1,0},{2,3},{3,2},{4,5},{5,4},{6,7},{7,6},{8,9},{9,8},{10,11... | collective-permute-start | bytes 1544 | tf_op jit(solution)/shard_map/ppermute | solution.py:308
  42.7 0.8 %collective-permute-done.11 = f32[1,128]{1,0:T(1,128)S(1)} collective-permute-done((f32[1,128]{1,0:T(1,128)S(1)}, f32[1,128]{1,0:T(1,128)S(1)}, u32[]{:S(2)}, u32[]{:S(2)}) %collective-permute-start.11) | collective-permute-done | bytes 544 | tf_op jit(solution)/shard_map/ppermute | solution.py:308
  43.5 0.6 %constant_dynamic-slice_fusion = f32[1,32]{1,0:T(1,128)} fusion(f32[1,128]{1,0:T(1,128)S(1)} %add.18, s32[]{:T(128)S(6)} %select_n.3), kind=kLoop, calls=%fused_computation.1 | loop fusion | bytes 260 | tf_op jit(solution)/shard_map/dynamic_slice | solution.py:342
  (3 shorter events, 0.0 us)
Async XLA Ops:
  0.6 13.5 %copy-start = (bf16[6,6,8,16,6,256]{5,3,4,2,1,0:T(8,128)(2,1)S(1)}, bf16[6,6,8,16,6,256]{5,3,4,2,1,0:T(8,128)(2,1)}, u32[]{:S(2)}) copy-start(bf16[6,6,8,16,6,256]{5,3,4,2,1,0:T(8,128)(2,1)} %param.10) | copy-start | bytes 42467332
  2.0 17.4 %collective-permute-start = (f32[6,16,256]{2,1,0:T(8,128)S(1)}, f32[6,16,256]{2,1,0:T(8,128)S(1)}, u32[]{:S(2)}, u32[]{:S(2)}) collective-permute-start(f32[6,16,256]{2,1,0:T(8,128)S(1)} %get-tuple-element.24), channel_id=1, source_target_pairs={{0,4},{4,0},{8,12},{12,8},{16,20},{20,16},{24,28},{28,24},{32,36},... | collective-permute-start | bytes 294920 | tf_op jit(solution)/shard_map/ppermute | solution.py:291
  4.2 15.2 %collective-permute-start.1 = (f32[6,16,256]{2,1,0:T(8,128)S(1)}, f32[6,16,256]{2,1,0:T(8,128)S(1)}, u32[]{:S(2)}, u32[]{:S(2)}) collective-permute-start(f32[6,16,256]{2,1,0:T(8,128)S(1)} %get-tuple-element.25), channel_id=1, source_target_pairs={{0,124},{4,8},{8,4},{12,16},{16,12},{20,24},{24,20},{28,32},{32,28... | collective-permute-start | bytes 294920 | tf_op jit(solution)/shard_map/ppermute | solution.py:289
  10.5 8.9 %collective-permute-start.2 = (f32[6,8,256]{2,1,0:T(8,128)S(1)}, f32[6,8,256]{2,1,0:T(8,128)S(1)}, u32[]{:S(2)}, u32[]{:S(2)}) collective-permute-start(f32[6,8,256]{2,1,0:T(8,128)S(1)} %get-tuple-element.26), channel_id=1, source_target_pairs={{0,1},{1,0},{2,3},{3,2},{4,5},{5,4},{6,7},{7,6},{8,9},{9,8},{10,11... | collective-permute-start | bytes 147464 | tf_op jit(solution)/shard_map/ppermute | solution.py:292
  11.7 7.7 %collective-permute-start.3 = (f32[6,8,256]{2,1,0:T(8,128)S(1)}, f32[6,8,256]{2,1,0:T(8,128)S(1)}, u32[]{:S(2)}, u32[]{:S(2)}) collective-permute-start(f32[6,8,256]{2,1,0:T(8,128)S(1)} %get-tuple-element.27), channel_id=1, source_target_pairs={{0,3},{1,2},{2,1},{3,0},{4,7},{5,6},{6,5},{7,4},{8,11},{9,10},{10,... | collective-permute-start | bytes 147464 | tf_op jit(solution)/shard_map/ppermute | solution.py:290
  19.9 8.4 %collective-permute-start.4 = (f32[6,16,256]{2,1,0:T(8,128)S(1)}, f32[6,16,256]{2,1,0:T(8,128)S(1)}, u32[]{:S(2)}, u32[]{:S(2)}) collective-permute-start(f32[6,16,256]{2,1,0:T(8,128)S(1)} %get-tuple-element.36), channel_id=1, source_target_pairs={{0,4},{4,0},{8,12},{12,8},{16,20},{20,16},{24,28},{28,24},{32,36},... | collective-permute-start | bytes 294920 | tf_op jit(solution)/shard_map/ppermute | solution.py:291
  20.0 8.3 %collective-permute-start.5 = (f32[6,16,256]{2,1,0:T(8,128)S(1)}, f32[6,16,256]{2,1,0:T(8,128)S(1)}, u32[]{:S(2)}, u32[]{:S(2)}) collective-permute-start(f32[6,16,256]{2,1,0:T(8,128)S(1)} %get-tuple-element.37), channel_id=1, source_target_pairs={{0,124},{4,8},{8,4},{12,16},{16,12},{20,24},{24,20},{28,32},{32,28... | collective-permute-start | bytes 294920 | tf_op jit(solution)/shard_map/ppermute | solution.py:289
  20.3 8.1 %collective-permute-start.6 = (f32[6,8,256]{2,1,0:T(8,128)S(1)}, f32[6,8,256]{2,1,0:T(8,128)S(1)}, u32[]{:S(2)}, u32[]{:S(2)}) collective-permute-start(f32[6,8,256]{2,1,0:T(8,128)S(1)} %get-tuple-element.38), channel_id=1, source_target_pairs={{0,1},{1,0},{2,3},{3,2},{4,5},{5,4},{6,7},{7,6},{8,9},{9,8},{10,11... | collective-permute-start | bytes 147464 | tf_op jit(solution)/shard_map/ppermute | solution.py:292
  21.5 6.8 %collective-permute-start.7 = (f32[6,8,256]{2,1,0:T(8,128)S(1)}, f32[6,8,256]{2,1,0:T(8,128)S(1)}, u32[]{:S(2)}, u32[]{:S(2)}) collective-permute-start(f32[6,8,256]{2,1,0:T(8,128)S(1)} %get-tuple-element.39), channel_id=1, source_target_pairs={{0,3},{1,2},{2,1},{3,0},{4,7},{5,6},{6,5},{7,4},{8,11},{9,10},{10,... | collective-permute-start | bytes 147464 | tf_op jit(solution)/shard_map/ppermute | solution.py:290
  24.1 4.2 %copy-start.1 = (f32[512,6,128]{2,0,1:T(8,128)S(1)}, f32[512,6,128]{2,0,1:T(8,128)}, u32[]{:S(2)}) copy-start(f32[512,6,128]{2,0,1:T(8,128)} %param.15) | copy-start | bytes 4718596
  24.1 4.3 %copy-start.2 = (s32[512]{0:T(512)S(1)}, s32[512]{0:T(512)}, u32[]{:S(2)}) copy-start(s32[512]{0:T(512)} %param.14) | copy-start | bytes 6148
  24.1 4.3 %copy-start.3 = (s32[512]{0:T(512)S(1)}, s32[512]{0:T(512)}, u32[]{:S(2)}) copy-start(s32[512]{0:T(512)} %param.13) | copy-start | bytes 6148
  31.0 7.9 %collective-permute-start.10 = (f32[1,128]{1,0:T(1,128)S(1)}, f32[1,128]{1,0:T(1,128)S(1)}, u32[]{:S(2)}, u32[]{:S(2)}) collective-permute-start(f32[1,128]{1,0:T(1,128)S(1)} %get-tuple-element.43), channel_id=1, source_target_pairs={{0,6},{1,7},{2,4},{3,5},{4,10},{5,11},{6,8},{7,9},{8,14},{9,15},{1... | collective-permute-start | bytes 1544 | tf_op jit(solution)/shard_map/ppermute | solution.py:304
  31.8 7.1 %collective-permute-start.8 = (f32[1,128]{1,0:T(1,128)S(1)}, f32[1,128]{1,0:T(1,128)S(1)}, u32[]{:S(2)}, u32[]{:S(2)}) collective-permute-start(f32[1,128]{1,0:T(1,128)S(1)} %get-tuple-element.42), channel_id=1, source_target_pairs={{0,2},{1,3},{2,0},{3,1},{4,6},{5,7},{6,4},{7,5},{8,10},{9,11},{10,... | collective-permute-start | bytes 1544 | tf_op jit(solution)/shard_map/ppermute | solution.py:306
  32.7 6.8 %collective-permute-start.9 = (f32[1,128]{1,0:T(1,128)S(1)}, f32[1,128]{1,0:T(1,128)S(1)}, u32[]{:S(2)}, u32[]{:S(2)}) collective-permute-start(f32[1,128]{1,0:T(1,128)S(1)} %get-tuple-element.43), channel_id=1, source_target_pairs={{0,4},{1,5},{2,6},{3,7},{4,8},{5,9},{6,10},{7,11},{8,12},{9,13},{1... | collective-permute-start | bytes 1544 | tf_op jit(solution)/shard_map/ppermute | solution.py:305
  39.5 4.0 %collective-permute-start.11 = (f32[1,128]{1,0:T(1,128)S(1)}, f32[1,128]{1,0:T(1,128)S(1)}, u32[]{:S(2)}, u32[]{:S(2)}) collective-permute-start(f32[1,128]{1,0:T(1,128)S(1)} %add_add_fusion), channel_id=1, source_target_pairs={{0,1},{1,0},{2,3},{3,2},{4,5},{5,4},{6,7},{7,6},{8,9},{9,8},{10,11... | collective-permute-start | bytes 1544 | tf_op jit(solution)/shard_map/ppermute | solution.py:308

commit v5 on v4

--- a/solution.py
+++ b/solution.py
@@ -236,15 +236,17 @@
     field = lax.broadcasted_iota(jnp.int32, (8, 128), 0)
     look_up.wait()
 
+    picked = [jnp.zeros((8, 128), F32)] * chunks
+    for f in range(128):
+        place = lane == f
+        for k in range(chunks):
+            tile = by_cell[pl.ds(table[k, f], 8), :]
+            picked[k] = jnp.where(place, pltpu.roll(tile, table[k + chunks, f], 1), picked[k])
     every = jnp.zeros((8, 128), F32)
     upper = jnp.zeros((8, 128), F32)
     for k in range(chunks):
         side = jnp.broadcast_to(side_ref[k : k + 1, :].astype(F32), (8, 128))
-        picked = jnp.zeros((8, 128), F32)
-        for f in range(128):
-            tile = by_cell[pl.ds(table[k, f], 8), :]
-            picked = jnp.where(lane == f, pltpu.roll(tile, table[k + chunks, f], 1), picked)
-        by_face = jnp.transpose(jnp.where(field == 6, side, picked))
+        by_face = jnp.transpose(jnp.where(field == 6, side, picked[k]))
         contrib = jnp.zeros((128, 128), F32)
         for i in range(nv):
             contrib = contrib + by_face[:, i : i + 1] * design_ref[i, k * 128 : k * 128 + 128, :]

time: 44.2 us -> 43.6 us (0.986)
  Pallas kernels: 14 us -> 13.4 us
    pallas_call x1, Pallas kernels: 2.63 us -> 2.01 us  [halo_part(): pl.pallas_call(final_kernel, in_specs=[_vmem()] * (len(args) + 3), out_sp...]
where the time goes in v5:
time: 43.6 us; the launch traced here: 43.5 us
  starting transfers between devices  22.8 us (52%)
  Pallas kernels  13.4 us (31%)
  waiting for transfers between devices  5.88 us (13%)
  between operations  0.79 us (2%)
  local copies, waits for them, and re-layouts  0.6 us (1%)
    ppermute x2, starting transfers between devices, swap_halos(): lax.ppermute(odd, 'circ', [(i, (i + 1) % nc if i % 2 else (i - 1) % nc) f...  6.51 us
    pallas_call x1, Pallas kernels, first_part(): pl.pallas_call(first_kernel, in_specs=[_vmem()] * 2 + [pl.BlockSpec(memor...  5.32 us
    ppermute x2, starting transfers between devices, swap_halos(): far = lax.ppermute(far, 'radax', [(i, nr - 1 - i) for i in range(nr)])  4.95 us
    ppermute x1, waiting for transfers between devices, combine(): crossed = lax.ppermute(upper, ('circ', 'radax'), ring(2))  4.46 us
    pallas_call x1, Pallas kernels, second_part(): pl.pallas_call(second_kernel, in_specs=[_vmem()] * 5, out_specs=_vmem(),...  4.19 us
    ppermute x1, starting transfers between devices, combine(): return mine + lax.ppermute(mine, 'radax', [(i, i ^ 1) for i in range(nr)])  3.14 us
    ppermute x2, starting transfers between devices, swap_halos(): near = lax.ppermute(near, 'radax', [(i, i ^ 1) for i in range(nr)])  2.47 us
    ppermute x2, starting transfers between devices, swap_halos(): even = lax.ppermute(even, 'circ', [(i, i ^ 1) for i in range(nc)])  2.28 us
  transfers between devices with their start and end apart: 12, of which 3 were waited for; matrix products, arithmetic and copies ran while one was open for 0% of the time, Pallas kernels for 22%

profile of v5, /device:TPU:1, one launch (start us, length us, event | category | flops | bytes accessed | tf_op | source)
XLA Modules:
  0.0 43.5 jit_solution(7218759096059116332)
XLA Ops:
  0.6 0.0 copy-start
  0.6 1.4 %faces.1 = (f32[8,6,16,256]{3,2,1,0:T(8,128)S(1)}, f32[6,16,256]{2,1,0:T(8,128)S(1)}, f32[6,16,256]{2,1,0:T(8,128)S(1)}, f32[6,8,256]{2,1,0:T(8,128)S(1)}, f32[6,8,256]{2,1,0:T(8,128)S(1)}) custom-call(f32[8,6,16,256]{3,2,1,0:T(8,128)} %bitcast.19), custom_call_target="tpu_custom_call" | custom-call | flops 4000000000 | bytes 200000000 | tf_op jit(solution)/shard_map/faces/pallas_call | solution.py:323
  2.0 2.2 %collective-permute-start = (f32[6,16,256]{2,1,0:T(8,128)S(1)}, f32[6,16,256]{2,1,0:T(8,128)S(1)}, u32[]{:S(2)}, u32[]{:S(2)}) collective-permute-start(f32[6,16,256]{2,1,0:T(8,128)S(1)} %get-tuple-element.24), channel_id=1, source_target_pairs={{0,4},{4,0},{8,12},{12,8},{16,20},{20,16},{24,28},{28,24},{32,36},... | collective-permute-start | bytes 294920 | tf_op jit(solution)/shard_map/ppermute | solution.py:293
  4.2 6.3 %collective-permute-start.1 = (f32[6,16,256]{2,1,0:T(8,128)S(1)}, f32[6,16,256]{2,1,0:T(8,128)S(1)}, u32[]{:S(2)}, u32[]{:S(2)}) collective-permute-start(f32[6,16,256]{2,1,0:T(8,128)S(1)} %get-tuple-element.25), channel_id=1, source_target_pairs={{0,124},{4,8},{8,4},{12,16},{16,12},{20,24},{24,20},{28,32},{32,28... | collective-permute-start | bytes 294920 | tf_op jit(solution)/shard_map/ppermute | solution.py:291
  10.5 1.2 %collective-permute-start.2 = (f32[6,8,256]{2,1,0:T(8,128)S(1)}, f32[6,8,256]{2,1,0:T(8,128)S(1)}, u32[]{:S(2)}, u32[]{:S(2)}) collective-permute-start(f32[6,8,256]{2,1,0:T(8,128)S(1)} %get-tuple-element.26), channel_id=1, source_target_pairs={{0,1},{1,0},{2,3},{3,2},{4,5},{5,4},{6,7},{7,6},{8,9},{9,8},{10,11... | collective-permute-start | bytes 147464 | tf_op jit(solution)/shard_map/ppermute | solution.py:294
  11.7 2.3 %collective-permute-start.3 = (f32[6,8,256]{2,1,0:T(8,128)S(1)}, f32[6,8,256]{2,1,0:T(8,128)S(1)}, u32[]{:S(2)}, u32[]{:S(2)}) collective-permute-start(f32[6,8,256]{2,1,0:T(8,128)S(1)} %get-tuple-element.27), channel_id=1, source_target_pairs={{0,3},{1,2},{2,1},{3,0},{4,7},{5,6},{6,5},{7,4},{8,11},{9,10},{10,... | collective-permute-start | bytes 147464 | tf_op jit(solution)/shard_map/ppermute | solution.py:292
  14.1 0.0 copy-done
  14.1 5.3 %local_first.1 = (f32[8,6,16,256]{3,2,1,0:T(8,128)S(1)}, f32[6,6,8,256]{3,2,1,0:T(8,128)S(1)}, f32[6,6,8,256]{3,2,1,0:T(8,128)S(1)}, f32[6,6,8,256]{3,2,1,0:T(8,...) custom-call(f32[8,6,16,256]{3,2,1,0:T(8,128)S(1)} %get-tuple-element, ...), custom_call_target="tpu_custom_call" | custom-call | flops 40000000 | bytes 24000000 | tf_op jit(solution)/shard_map/local_first/pallas_call | solution.py:143
  19.4 0.0 collective-permute-done.2.near
  19.4 0.0 collective-permute-done.3.far
  19.4 0.0 collective-permute-done.even
  19.4 0.0 collective-permute-done.1.odd
  19.5 0.5 %halo_first.1 = (f32[8,6,16,256]{3,2,1,0:T(8,128)S(1)}, f32[6,16,256]{2,1,0:T(8,128)S(1)}, f32[6,16,256]{2,1,0:T(8,128)S(1)}, f32[6,8,256]{2,1,0:T(8,128)S(1)}, f32[6,8,256]{2,1,0:T(8,128)S(1)}) custom-call(f32[8,6,16,256]{3,2,1,0:T(8,128)S(1)} %get-tuple-element.23.adj_ref, f32[6,16,256]{2,1,0:T(8,128)S(1)} %collective-permute-done.even, ...), custom_call_target="tpu_custom_call" | custom-call | flops 4000000 | bytes 5000000 | tf_op jit(solution)/shard_map/halo_first/pallas_call | solution.py:268
  19.9 0.1 collective-permute-start.4
  20.0 0.2 collective-permute-start.5
  20.3 1.2 %collective-permute-start.6 = (f32[6,8,256]{2,1,0:T(8,128)S(1)}, f32[6,8,256]{2,1,0:T(8,128)S(1)}, u32[]{:S(2)}, u32[]{:S(2)}) collective-permute-start(f32[6,8,256]{2,1,0:T(8,128)S(1)} %get-tuple-element.38), channel_id=1, source_target_pairs={{0,1},{1,0},{2,3},{3,2},{4,5},{5,4},{6,7},{7,6},{8,9},{9,8},{10,11... | collective-permute-start | bytes 147464 | tf_op jit(solution)/shard_map/ppermute | solution.py:294
  21.5 2.6 %collective-permute-start.7 = (f32[6,8,256]{2,1,0:T(8,128)S(1)}, f32[6,8,256]{2,1,0:T(8,128)S(1)}, u32[]{:S(2)}, u32[]{:S(2)}) collective-permute-start(f32[6,8,256]{2,1,0:T(8,128)S(1)} %get-tuple-element.39), channel_id=1, source_target_pairs={{0,3},{1,2},{2,1},{3,0},{4,7},{5,6},{6,5},{7,4},{8,11},{9,10},{10,... | collective-permute-start | bytes 147464 | tf_op jit(solution)/shard_map/ppermute | solution.py:292
  24.1 0.0 copy-start.1
  24.1 0.0 copy-start.2
  24.1 0.0 copy-start.3
  24.1 4.2 %local_second.1.adj_ref = f32[8,6,16,256]{3,2,1,0:T(8,128)S(1)} custom-call(f32[8,6,16,256]{3,2,1,0:T(8,128)S(1)} %get-tuple-element.33.adj_ref, f32[8,6,16,256]{3,2,1,0:T(8,128)S(1)} %get-tuple-element.34.g_ref, bf16[6,6,8,6,16,256]{5,4,3,2,1,0:T(8,128)(2,1)S(1)} %bitcast.11, bf16[6,8,6,16,256]{4,3,2,1,0:T(8,128)(2,1)S(1)} %get-tuple-element.35.diag_ref, ...), custom_call_target="tpu_custom_call" | custom-call | flops 40000000 | bytes 24000000 | tf_op jit(solution)/shard_map/local_second/pallas_call | solution.py:156
  28.3 0.0 collective-permute-done.6.near
  28.3 0.0 collective-permute-done.7.far
  28.3 0.0 collective-permute-done.4.even
  28.3 0.0 collective-permute-done.5.odd
  28.3 0.0 copy-done.1
  28.4 0.0 copy-done.2
  28.4 0.0 copy-done.3
  28.4 2.0 %halo_last.1 = (f32[8,6,16,256]{3,2,1,0:T(8,128)}, f32[2,128]{1,0:T(2,128)S(1)}) custom-call(f32[8,6,16,256]{3,2,1,0:T(8,128)S(1)} %local_second.1.adj_ref, f32[6,16,256]{2,1,0:T(8,128)S(1)} %collective-permute-done.4.even, f32[6,16,256]{2,1,0:T(8,128)S(1)} %collective-permute-done.5.odd, f32[6,8,256]{2,1,0:T(8,128)S(1)} %collective-permute-done.6.near, ...), custom_call_target="tpu_custom_call" | custom-call | flops 4000000 | bytes 5000000 | tf_op jit(solution)/shard_map/halo_last/pallas_call | solution.py:274
  30.4 0.8 %collective-permute-start.10 = (f32[1,128]{1,0:T(1,128)S(1)}, f32[1,128]{1,0:T(1,128)S(1)}, u32[]{:S(2)}, u32[]{:S(2)}) collective-permute-start(f32[1,128]{1,0:T(1,128)S(1)} %get-tuple-element.43), channel_id=1, source_target_pairs={{0,6},{1,7},{2,4},{3,5},{4,10},{5,11},{6,8},{7,9},{8,14},{9,15},{1... | collective-permute-start | bytes 1544 | tf_op jit(solution)/shard_map/ppermute | solution.py:306
  31.2 0.9 %collective-permute-start.8 = (f32[1,128]{1,0:T(1,128)S(1)}, f32[1,128]{1,0:T(1,128)S(1)}, u32[]{:S(2)}, u32[]{:S(2)}) collective-permute-start(f32[1,128]{1,0:T(1,128)S(1)} %get-tuple-element.42), channel_id=1, source_target_pairs={{0,2},{1,3},{2,0},{3,1},{4,6},{5,7},{6,4},{7,5},{8,10},{9,11},{10,... | collective-permute-start | bytes 1544 | tf_op jit(solution)/shard_map/ppermute | solution.py:308
  32.1 1.7 %collective-permute-start.9 = (f32[1,128]{1,0:T(1,128)S(1)}, f32[1,128]{1,0:T(1,128)S(1)}, u32[]{:S(2)}, u32[]{:S(2)}) collective-permute-start(f32[1,128]{1,0:T(1,128)S(1)} %get-tuple-element.43), channel_id=1, source_target_pairs={{0,4},{1,5},{2,6},{3,7},{4,8},{5,9},{6,10},{7,11},{8,12},{9,13},{1... | collective-permute-start | bytes 1544 | tf_op jit(solution)/shard_map/ppermute | solution.py:307
  33.9 4.5 %collective-permute-done.10 = f32[1,128]{1,0:T(1,128)S(1)} collective-permute-done((f32[1,128]{1,0:T(1,128)S(1)}, f32[1,128]{1,0:T(1,128)S(1)}, u32[]{:S(2)}, u32[]{:S(2)}) %collective-permute-start.10) | collective-permute-done | bytes 544 | tf_op jit(solution)/shard_map/ppermute | solution.py:306
  38.3 0.0 collective-permute-done.8
  38.3 0.6 %collective-permute-done.9 = f32[1,128]{1,0:T(1,128)S(1)} collective-permute-done((f32[1,128]{1,0:T(1,128)S(1)}, f32[1,128]{1,0:T(1,128)S(1)}, u32[]{:S(2)}, u32[]{:S(2)}) %collective-permute-start.9) | collective-permute-done | bytes 544 | tf_op jit(solution)/shard_map/ppermute | solution.py:307
  38.9 3.1 %collective-permute-start.11 = (f32[1,128]{1,0:T(1,128)S(1)}, f32[1,128]{1,0:T(1,128)S(1)}, u32[]{:S(2)}, u32[]{:S(2)}) collective-permute-start(f32[1,128]{1,0:T(1,128)S(1)} %add_add_fusion), channel_id=1, source_target_pairs={{0,1},{1,0},{2,3},{3,2},{4,5},{5,4},{6,7},{7,6},{8,9},{9,8},{10,11... | collective-permute-start | bytes 1544 | tf_op jit(solution)/shard_map/ppermute | solution.py:310
  42.0 0.8 %collective-permute-done.11 = f32[1,128]{1,0:T(1,128)S(1)} collective-permute-done((f32[1,128]{1,0:T(1,128)S(1)}, f32[1,128]{1,0:T(1,128)S(1)}, u32[]{:S(2)}, u32[]{:S(2)}) %collective-permute-start.11) | collective-permute-done | bytes 544 | tf_op jit(solution)/shard_map/ppermute | solution.py:310
  42.9 0.6 %constant_dynamic-slice_fusion = f32[1,32]{1,0:T(1,128)} fusion(f32[1,128]{1,0:T(1,128)S(1)} %add.18, s32[]{:T(128)S(6)} %select_n.3), kind=kLoop, calls=%fused_computation.1 | loop fusion | bytes 260 | tf_op jit(solution)/shard_map/dynamic_slice | solution.py:344
  (3 shorter events, 0.0 us)
Async XLA Ops:
  0.6 13.5 %copy-start = (bf16[6,6,8,16,6,256]{5,3,4,2,1,0:T(8,128)(2,1)S(1)}, bf16[6,6,8,16,6,256]{5,3,4,2,1,0:T(8,128)(2,1)}, u32[]{:S(2)}) copy-start(bf16[6,6,8,16,6,256]{5,3,4,2,1,0:T(8,128)(2,1)} %param.10) | copy-start | bytes 42467332
  2.0 17.4 %collective-permute-start = (f32[6,16,256]{2,1,0:T(8,128)S(1)}, f32[6,16,256]{2,1,0:T(8,128)S(1)}, u32[]{:S(2)}, u32[]{:S(2)}) collective-permute-start(f32[6,16,256]{2,1,0:T(8,128)S(1)} %get-tuple-element.24), channel_id=1, source_target_pairs={{0,4},{4,0},{8,12},{12,8},{16,20},{20,16},{24,28},{28,24},{32,36},... | collective-permute-start | bytes 294920 | tf_op jit(solution)/shard_map/ppermute | solution.py:293
  4.2 15.2 %collective-permute-start.1 = (f32[6,16,256]{2,1,0:T(8,128)S(1)}, f32[6,16,256]{2,1,0:T(8,128)S(1)}, u32[]{:S(2)}, u32[]{:S(2)}) collective-permute-start(f32[6,16,256]{2,1,0:T(8,128)S(1)} %get-tuple-element.25), channel_id=1, source_target_pairs={{0,124},{4,8},{8,4},{12,16},{16,12},{20,24},{24,20},{28,32},{32,28... | collective-permute-start | bytes 294920 | tf_op jit(solution)/shard_map/ppermute | solution.py:291
  10.5 8.9 %collective-permute-start.2 = (f32[6,8,256]{2,1,0:T(8,128)S(1)}, f32[6,8,256]{2,1,0:T(8,128)S(1)}, u32[]{:S(2)}, u32[]{:S(2)}) collective-permute-start(f32[6,8,256]{2,1,0:T(8,128)S(1)} %get-tuple-element.26), channel_id=1, source_target_pairs={{0,1},{1,0},{2,3},{3,2},{4,5},{5,4},{6,7},{7,6},{8,9},{9,8},{10,11... | collective-permute-start | bytes 147464 | tf_op jit(solution)/shard_map/ppermute | solution.py:294
  11.7 7.7 %collective-permute-start.3 = (f32[6,8,256]{2,1,0:T(8,128)S(1)}, f32[6,8,256]{2,1,0:T(8,128)S(1)}, u32[]{:S(2)}, u32[]{:S(2)}) collective-permute-start(f32[6,8,256]{2,1,0:T(8,128)S(1)} %get-tuple-element.27), channel_id=1, source_target_pairs={{0,3},{1,2},{2,1},{3,0},{4,7},{5,6},{6,5},{7,4},{8,11},{9,10},{10,... | collective-permute-start | bytes 147464 | tf_op jit(solution)/shard_map/ppermute | solution.py:292
  19.9 8.4 %collective-permute-start.4 = (f32[6,16,256]{2,1,0:T(8,128)S(1)}, f32[6,16,256]{2,1,0:T(8,128)S(1)}, u32[]{:S(2)}, u32[]{:S(2)}) collective-permute-start(f32[6,16,256]{2,1,0:T(8,128)S(1)} %get-tuple-element.36), channel_id=1, source_target_pairs={{0,4},{4,0},{8,12},{12,8},{16,20},{20,16},{24,28},{28,24},{32,36},... | collective-permute-start | bytes 294920 | tf_op jit(solution)/shard_map/ppermute | solution.py:293
  20.0 8.3 %collective-permute-start.5 = (f32[6,16,256]{2,1,0:T(8,128)S(1)}, f32[6,16,256]{2,1,0:T(8,128)S(1)}, u32[]{:S(2)}, u32[]{:S(2)}) collective-permute-start(f32[6,16,256]{2,1,0:T(8,128)S(1)} %get-tuple-element.37), channel_id=1, source_target_pairs={{0,124},{4,8},{8,4},{12,16},{16,12},{20,24},{24,20},{28,32},{32,28... | collective-permute-start | bytes 294920 | tf_op jit(solution)/shard_map/ppermute | solution.py:291
  20.3 8.1 %collective-permute-start.6 = (f32[6,8,256]{2,1,0:T(8,128)S(1)}, f32[6,8,256]{2,1,0:T(8,128)S(1)}, u32[]{:S(2)}, u32[]{:S(2)}) collective-permute-start(f32[6,8,256]{2,1,0:T(8,128)S(1)} %get-tuple-element.38), channel_id=1, source_target_pairs={{0,1},{1,0},{2,3},{3,2},{4,5},{5,4},{6,7},{7,6},{8,9},{9,8},{10,11... | collective-permute-start | bytes 147464 | tf_op jit(solution)/shard_map/ppermute | solution.py:294
  21.5 6.8 %collective-permute-start.7 = (f32[6,8,256]{2,1,0:T(8,128)S(1)}, f32[6,8,256]{2,1,0:T(8,128)S(1)}, u32[]{:S(2)}, u32[]{:S(2)}) collective-permute-start(f32[6,8,256]{2,1,0:T(8,128)S(1)} %get-tuple-element.39), channel_id=1, source_target_pairs={{0,3},{1,2},{2,1},{3,0},{4,7},{5,6},{6,5},{7,4},{8,11},{9,10},{10,... | collective-permute-start | bytes 147464 | tf_op jit(solution)/shard_map/ppermute | solution.py:292
  24.1 4.2 %copy-start.1 = (f32[512,6,128]{2,0,1:T(8,128)S(1)}, f32[512,6,128]{2,0,1:T(8,128)}, u32[]{:S(2)}) copy-start(f32[512,6,128]{2,0,1:T(8,128)} %param.15) | copy-start | bytes 4718596
  24.1 4.3 %copy-start.2 = (s32[512]{0:T(512)S(1)}, s32[512]{0:T(512)}, u32[]{:S(2)}) copy-start(s32[512]{0:T(512)} %param.14) | copy-start | bytes 6148
  24.1 4.3 %copy-start.3 = (s32[512]{0:T(512)S(1)}, s32[512]{0:T(512)}, u32[]{:S(2)}) copy-start(s32[512]{0:T(512)} %param.13) | copy-start | bytes 6148
  30.4 7.9 %collective-permute-start.10 = (f32[1,128]{1,0:T(1,128)S(1)}, f32[1,128]{1,0:T(1,128)S(1)}, u32[]{:S(2)}, u32[]{:S(2)}) collective-permute-start(f32[1,128]{1,0:T(1,128)S(1)} %get-tuple-element.43), channel_id=1, source_target_pairs={{0,6},{1,7},{2,4},{3,5},{4,10},{5,11},{6,8},{7,9},{8,14},{9,15},{1... | collective-permute-start | bytes 1544 | tf_op jit(solution)/shard_map/ppermute | solution.py:306
  31.2 7.1 %collective-permute-start.8 = (f32[1,128]{1,0:T(1,128)S(1)}, f32[1,128]{1,0:T(1,128)S(1)}, u32[]{:S(2)}, u32[]{:S(2)}) collective-permute-start(f32[1,128]{1,0:T(1,128)S(1)} %get-tuple-element.42), channel_id=1, source_target_pairs={{0,2},{1,3},{2,0},{3,1},{4,6},{5,7},{6,4},{7,5},{8,10},{9,11},{10,... | collective-permute-start | bytes 1544 | tf_op jit(solution)/shard_map/ppermute | solution.py:308
  32.1 6.8 %collective-permute-start.9 = (f32[1,128]{1,0:T(1,128)S(1)}, f32[1,128]{1,0:T(1,128)S(1)}, u32[]{:S(2)}, u32[]{:S(2)}) collective-permute-start(f32[1,128]{1,0:T(1,128)S(1)} %get-tuple-element.43), channel_id=1, source_target_pairs={{0,4},{1,5},{2,6},{3,7},{4,8},{5,9},{6,10},{7,11},{8,12},{9,13},{1... | collective-permute-start | bytes 1544 | tf_op jit(solution)/shard_map/ppermute | solution.py:307
  38.9 4.0 %collective-permute-start.11 = (f32[1,128]{1,0:T(1,128)S(1)}, f32[1,128]{1,0:T(1,128)S(1)}, u32[]{:S(2)}, u32[]{:S(2)}) collective-permute-start(f32[1,128]{1,0:T(1,128)S(1)} %add_add_fusion), channel_id=1, source_target_pairs={{0,1},{1,0},{2,3},{3,2},{4,5},{5,4},{6,7},{7,6},{8,9},{9,8},{10,11... | collective-permute-start | bytes 1544 | tf_op jit(solution)/shard_map/ppermute | solution.py:310

commit v6 on v5

--- a/solution.py
+++ b/solution.py
@@ -62,7 +62,7 @@
     above = jnp.minimum(t + 1, nt - 1)
     has_below = (t > 0).astype(F32)
     has_above = (t < nt - 1).astype(F32)
-    acc = [jnp.zeros(adj_ref.shape[2:], F32)] * nv
+    acc = [None] * nv
     for j in range(nv):
         here = adj_ref[t, j]
         fields = [
@@ -76,7 +76,8 @@
         for k in range(6):
             for i in range(nv):
                 block = off_ref[k, j, t, i].astype(F32)
-                acc[i] = acc[i] + block * fields[k]
+                term = block * fields[k]
+                acc[i] = term if acc[i] is None else acc[i] + term
                 if edge_refs and k in (2, 3):
                     keep_row(edge_refs[k - 2].at[j, i], t, block, 0 if k == 2 else nq - 1)
     if wait is not None:
@@ -276,7 +277,7 @@
         out_specs=[pl.BlockSpec(memory_space=pltpu.HBM), _vmem()], out_shape=out_shape,
         scratch_shapes=[
             pltpu.VMEM(adj.shape, F32),
-            pltpu.VMEM((nt * nq * (na // 16 + 1), 128), F32),
+            pltpu.VMEM(((nt * nq + 8) * (na // 16 + 1), 128), F32),
             pltpu.VMEM((2 * cell.shape[0], 128), jnp.int32),
             pltpu.SMEM((2 * cell.shape[0], 128), jnp.int32),
             pltpu.SemaphoreType.DMA((2,)),

time: 43.6 us -> 43.6 us (level)
  no operation moved by 1% of the time
where the time goes in v6:
time: 43.6 us; the launch traced here: 43.5 us
  starting transfers between devices  22.8 us (52%)
  Pallas kernels  13.4 us (31%)
  waiting for transfers between devices  5.88 us (13%)
  between operations  0.79 us (2%)
  local copies, waits for them, and re-layouts  0.6 us (1%)
    ppermute x2, starting transfers between devices, swap_halos(): lax.ppermute(odd, 'circ', [(i, (i + 1) % nc if i % 2 else (i - 1) % nc) f...  6.51 us
    pallas_call x1, Pallas kernels, first_part(): pl.pallas_call(first_kernel, in_specs=[_vmem()] * 2 + [pl.BlockSpec(memor...  5.32 us
    ppermute x2, starting transfers between devices, swap_halos(): far = lax.ppermute(far, 'radax', [(i, nr - 1 - i) for i in range(nr)])  4.95 us
    ppermute x1, waiting for transfers between devices, combine(): crossed = lax.ppermute(upper, ('circ', 'radax'), ring(2))  4.46 us
    pallas_call x1, Pallas kernels, second_part(): pl.pallas_call(second_kernel, in_specs=[_vmem()] * 5, out_specs=_vmem(),...  4.19 us
    ppermute x1, starting transfers between devices, combine(): return mine + lax.ppermute(mine, 'radax', [(i, i ^ 1) for i in range(nr)])  3.14 us
    ppermute x2, starting transfers between devices, swap_halos(): near = lax.ppermute(near, 'radax', [(i, i ^ 1) for i in range(nr)])  2.47 us
    ppermute x2, starting transfers between devices, swap_halos(): even = lax.ppermute(even, 'circ', [(i, i ^ 1) for i in range(nc)])  2.28 us
  transfers between devices with their start and end apart: 12, of which 3 were waited for; matrix products, arithmetic and copies ran while one was open for 0% of the time, Pallas kernels for 22%

profile of v6, /device:TPU:1, one launch (start us, length us, event | category | flops | bytes accessed | tf_op | source)
XLA Modules:
  0.0 43.5 jit_solution(12587289363433203010)
XLA Ops:
  0.6 0.0 copy-start
  0.6 1.4 %faces.1 = (f32[8,6,16,256]{3,2,1,0:T(8,128)S(1)}, f32[6,16,256]{2,1,0:T(8,128)S(1)}, f32[6,16,256]{2,1,0:T(8,128)S(1)}, f32[6,8,256]{2,1,0:T(8,128)S(1)}, f32[6,8,256]{2,1,0:T(8,128)S(1)}) custom-call(f32[8,6,16,256]{3,2,1,0:T(8,128)} %bitcast.19), custom_call_target="tpu_custom_call" | custom-call | flops 4000000000 | bytes 200000000 | tf_op jit(solution)/shard_map/faces/pallas_call | solution.py:324
  2.0 2.2 %collective-permute-start = (f32[6,16,256]{2,1,0:T(8,128)S(1)}, f32[6,16,256]{2,1,0:T(8,128)S(1)}, u32[]{:S(2)}, u32[]{:S(2)}) collective-permute-start(f32[6,16,256]{2,1,0:T(8,128)S(1)} %get-tuple-element.24), channel_id=1, source_target_pairs={{0,4},{4,0},{8,12},{12,8},{16,20},{20,16},{24,28},{28,24},{32,36},... | collective-permute-start | bytes 294920 | tf_op jit(solution)/shard_map/ppermute | solution.py:294
  4.2 6.3 %collective-permute-start.1 = (f32[6,16,256]{2,1,0:T(8,128)S(1)}, f32[6,16,256]{2,1,0:T(8,128)S(1)}, u32[]{:S(2)}, u32[]{:S(2)}) collective-permute-start(f32[6,16,256]{2,1,0:T(8,128)S(1)} %get-tuple-element.25), channel_id=1, source_target_pairs={{0,124},{4,8},{8,4},{12,16},{16,12},{20,24},{24,20},{28,32},{32,28... | collective-permute-start | bytes 294920 | tf_op jit(solution)/shard_map/ppermute | solution.py:292
  10.5 1.2 %collective-permute-start.2 = (f32[6,8,256]{2,1,0:T(8,128)S(1)}, f32[6,8,256]{2,1,0:T(8,128)S(1)}, u32[]{:S(2)}, u32[]{:S(2)}) collective-permute-start(f32[6,8,256]{2,1,0:T(8,128)S(1)} %get-tuple-element.26), channel_id=1, source_target_pairs={{0,1},{1,0},{2,3},{3,2},{4,5},{5,4},{6,7},{7,6},{8,9},{9,8},{10,11... | collective-permute-start | bytes 147464 | tf_op jit(solution)/shard_map/ppermute | solution.py:295
  11.7 2.3 %collective-permute-start.3 = (f32[6,8,256]{2,1,0:T(8,128)S(1)}, f32[6,8,256]{2,1,0:T(8,128)S(1)}, u32[]{:S(2)}, u32[]{:S(2)}) collective-permute-start(f32[6,8,256]{2,1,0:T(8,128)S(1)} %get-tuple-element.27), channel_id=1, source_target_pairs={{0,3},{1,2},{2,1},{3,0},{4,7},{5,6},{6,5},{7,4},{8,11},{9,10},{10,... | collective-permute-start | bytes 147464 | tf_op jit(solution)/shard_map/ppermute | solution.py:293
  14.1 0.0 copy-done
  14.1 5.3 %local_first.1 = (f32[8,6,16,256]{3,2,1,0:T(8,128)S(1)}, f32[6,6,8,256]{3,2,1,0:T(8,128)S(1)}, f32[6,6,8,256]{3,2,1,0:T(8,128)S(1)}, f32[6,6,8,256]{3,2,1,0:T(8,...) custom-call(f32[8,6,16,256]{3,2,1,0:T(8,128)S(1)} %get-tuple-element, ...), custom_call_target="tpu_custom_call" | custom-call | flops 40000000 | bytes 24000000 | tf_op jit(solution)/shard_map/local_first/pallas_call | solution.py:144
  19.4 0.0 collective-permute-done.2.near
  19.4 0.0 collective-permute-done.3.far
  19.4 0.0 collective-permute-done.even
  19.4 0.0 collective-permute-done.1.odd
  19.5 0.5 %halo_first.1 = (f32[8,6,16,256]{3,2,1,0:T(8,128)S(1)}, f32[6,16,256]{2,1,0:T(8,128)S(1)}, f32[6,16,256]{2,1,0:T(8,128)S(1)}, f32[6,8,256]{2,1,0:T(8,128)S(1)}, f32[6,8,256]{2,1,0:T(8,128)S(1)}) custom-call(f32[8,6,16,256]{3,2,1,0:T(8,128)S(1)} %get-tuple-element.23.adj_ref, f32[6,16,256]{2,1,0:T(8,128)S(1)} %collective-permute-done.even, ...), custom_call_target="tpu_custom_call" | custom-call | flops 4000000 | bytes 5000000 | tf_op jit(solution)/shard_map/halo_first/pallas_call | solution.py:269
  19.9 0.1 collective-permute-start.4
  20.0 0.2 collective-permute-start.5
  20.3 1.2 %collective-permute-start.6 = (f32[6,8,256]{2,1,0:T(8,128)S(1)}, f32[6,8,256]{2,1,0:T(8,128)S(1)}, u32[]{:S(2)}, u32[]{:S(2)}) collective-permute-start(f32[6,8,256]{2,1,0:T(8,128)S(1)} %get-tuple-element.38), channel_id=1, source_target_pairs={{0,1},{1,0},{2,3},{3,2},{4,5},{5,4},{6,7},{7,6},{8,9},{9,8},{10,11... | collective-permute-start | bytes 147464 | tf_op jit(solution)/shard_map/ppermute | solution.py:295
  21.5 2.6 %collective-permute-start.7 = (f32[6,8,256]{2,1,0:T(8,128)S(1)}, f32[6,8,256]{2,1,0:T(8,128)S(1)}, u32[]{:S(2)}, u32[]{:S(2)}) collective-permute-start(f32[6,8,256]{2,1,0:T(8,128)S(1)} %get-tuple-element.39), channel_id=1, source_target_pairs={{0,3},{1,2},{2,1},{3,0},{4,7},{5,6},{6,5},{7,4},{8,11},{9,10},{10,... | collective-permute-start | bytes 147464 | tf_op jit(solution)/shard_map/ppermute | solution.py:293
  24.1 0.0 copy-start.1
  24.1 0.0 copy-start.2
  24.1 0.0 copy-start.3
  24.1 4.2 %local_second.1.adj_ref = f32[8,6,16,256]{3,2,1,0:T(8,128)S(1)} custom-call(f32[8,6,16,256]{3,2,1,0:T(8,128)S(1)} %get-tuple-element.33.adj_ref, f32[8,6,16,256]{3,2,1,0:T(8,128)S(1)} %get-tuple-element.34.g_ref, bf16[6,6,8,6,16,256]{5,4,3,2,1,0:T(8,128)(2,1)S(1)} %bitcast.11, bf16[6,8,6,16,256]{4,3,2,1,0:T(8,128)(2,1)S(1)} %get-tuple-element.35.diag_ref, ...), custom_call_target="tpu_custom_call" | custom-call | flops 40000000 | bytes 24000000 | tf_op jit(solution)/shard_map/local_second/pallas_call | solution.py:157
  28.3 0.0 collective-permute-done.6.near
  28.3 0.0 collective-permute-done.7.far
  28.3 0.0 collective-permute-done.4.even
  28.3 0.0 collective-permute-done.5.odd
  28.3 0.0 copy-done.1
  28.4 0.0 copy-done.2
  28.4 0.0 copy-done.3
  28.4 2.0 %halo_last.1 = (f32[8,6,16,256]{3,2,1,0:T(8,128)}, f32[2,128]{1,0:T(2,128)S(1)}) custom-call(f32[8,6,16,256]{3,2,1,0:T(8,128)S(1)} %local_second.1.adj_ref, f32[6,16,256]{2,1,0:T(8,128)S(1)} %collective-permute-done.4.even, f32[6,16,256]{2,1,0:T(8,128)S(1)} %collective-permute-done.5.odd, f32[6,8,256]{2,1,0:T(8,128)S(1)} %collective-permute-done.6.near, ...), custom_call_target="tpu_custom_call" | custom-call | flops 4000000 | bytes 5000000 | tf_op jit(solution)/shard_map/halo_last/pallas_call | solution.py:275
  30.4 0.8 %collective-permute-start.10 = (f32[1,128]{1,0:T(1,128)S(1)}, f32[1,128]{1,0:T(1,128)S(1)}, u32[]{:S(2)}, u32[]{:S(2)}) collective-permute-start(f32[1,128]{1,0:T(1,128)S(1)} %get-tuple-element.43), channel_id=1, source_target_pairs={{0,6},{1,7},{2,4},{3,5},{4,10},{5,11},{6,8},{7,9},{8,14},{9,15},{1... | collective-permute-start | bytes 1544 | tf_op jit(solution)/shard_map/ppermute | solution.py:307
  31.2 0.9 %collective-permute-start.8 = (f32[1,128]{1,0:T(1,128)S(1)}, f32[1,128]{1,0:T(1,128)S(1)}, u32[]{:S(2)}, u32[]{:S(2)}) collective-permute-start(f32[1,128]{1,0:T(1,128)S(1)} %get-tuple-element.42), channel_id=1, source_target_pairs={{0,2},{1,3},{2,0},{3,1},{4,6},{5,7},{6,4},{7,5},{8,10},{9,11},{10,... | collective-permute-start | bytes 1544 | tf_op jit(solution)/shard_map/ppermute | solution.py:309
  32.1 1.7 %collective-permute-start.9 = (f32[1,128]{1,0:T(1,128)S(1)}, f32[1,128]{1,0:T(1,128)S(1)}, u32[]{:S(2)}, u32[]{:S(2)}) collective-permute-start(f32[1,128]{1,0:T(1,128)S(1)} %get-tuple-element.43), channel_id=1, source_target_pairs={{0,4},{1,5},{2,6},{3,7},{4,8},{5,9},{6,10},{7,11},{8,12},{9,13},{1... | collective-permute-start | bytes 1544 | tf_op jit(solution)/shard_map/ppermute | solution.py:308
  33.9 4.5 %collective-permute-done.10 = f32[1,128]{1,0:T(1,128)S(1)} collective-permute-done((f32[1,128]{1,0:T(1,128)S(1)}, f32[1,128]{1,0:T(1,128)S(1)}, u32[]{:S(2)}, u32[]{:S(2)}) %collective-permute-start.10) | collective-permute-done | bytes 544 | tf_op jit(solution)/shard_map/ppermute | solution.py:307
  38.3 0.0 collective-permute-done.8
  38.3 0.6 %collective-permute-done.9 = f32[1,128]{1,0:T(1,128)S(1)} collective-permute-done((f32[1,128]{1,0:T(1,128)S(1)}, f32[1,128]{1,0:T(1,128)S(1)}, u32[]{:S(2)}, u32[]{:S(2)}) %collective-permute-start.9) | collective-permute-done | bytes 544 | tf_op jit(solution)/shard_map/ppermute | solution.py:308
  38.9 3.1 %collective-permute-start.11 = (f32[1,128]{1,0:T(1,128)S(1)}, f32[1,128]{1,0:T(1,128)S(1)}, u32[]{:S(2)}, u32[]{:S(2)}) collective-permute-start(f32[1,128]{1,0:T(1,128)S(1)} %add_add_fusion), channel_id=1, source_target_pairs={{0,1},{1,0},{2,3},{3,2},{4,5},{5,4},{6,7},{7,6},{8,9},{9,8},{10,11... | collective-permute-start | bytes 1544 | tf_op jit(solution)/shard_map/ppermute | solution.py:311
  42.0 0.8 %collective-permute-done.11 = f32[1,128]{1,0:T(1,128)S(1)} collective-permute-done((f32[1,128]{1,0:T(1,128)S(1)}, f32[1,128]{1,0:T(1,128)S(1)}, u32[]{:S(2)}, u32[]{:S(2)}) %collective-permute-start.11) | collective-permute-done | bytes 544 | tf_op jit(solution)/shard_map/ppermute | solution.py:311
  42.9 0.6 %constant_dynamic-slice_fusion = f32[1,32]{1,0:T(1,128)} fusion(f32[1,128]{1,0:T(1,128)S(1)} %add.18, s32[]{:T(128)S(6)} %select_n.3), kind=kLoop, calls=%fused_computation.1 | loop fusion | bytes 260 | tf_op jit(solution)/shard_map/dynamic_slice | solution.py:345
  (3 shorter events, 0.0 us)
Async XLA Ops:
  0.6 13.5 %copy-start = (bf16[6,6,8,16,6,256]{5,3,4,2,1,0:T(8,128)(2,1)S(1)}, bf16[6,6,8,16,6,256]{5,3,4,2,1,0:T(8,128)(2,1)}, u32[]{:S(2)}) copy-start(bf16[6,6,8,16,6,256]{5,3,4,2,1,0:T(8,128)(2,1)} %param.10) | copy-start | bytes 42467332
  2.0 17.4 %collective-permute-start = (f32[6,16,256]{2,1,0:T(8,128)S(1)}, f32[6,16,256]{2,1,0:T(8,128)S(1)}, u32[]{:S(2)}, u32[]{:S(2)}) collective-permute-start(f32[6,16,256]{2,1,0:T(8,128)S(1)} %get-tuple-element.24), channel_id=1, source_target_pairs={{0,4},{4,0},{8,12},{12,8},{16,20},{20,16},{24,28},{28,24},{32,36},... | collective-permute-start | bytes 294920 | tf_op jit(solution)/shard_map/ppermute | solution.py:294
  4.2 15.2 %collective-permute-start.1 = (f32[6,16,256]{2,1,0:T(8,128)S(1)}, f32[6,16,256]{2,1,0:T(8,128)S(1)}, u32[]{:S(2)}, u32[]{:S(2)}) collective-permute-start(f32[6,16,256]{2,1,0:T(8,128)S(1)} %get-tuple-element.25), channel_id=1, source_target_pairs={{0,124},{4,8},{8,4},{12,16},{16,12},{20,24},{24,20},{28,32},{32,28... | collective-permute-start | bytes 294920 | tf_op jit(solution)/shard_map/ppermute | solution.py:292
  10.5 8.9 %collective-permute-start.2 = (f32[6,8,256]{2,1,0:T(8,128)S(1)}, f32[6,8,256]{2,1,0:T(8,128)S(1)}, u32[]{:S(2)}, u32[]{:S(2)}) collective-permute-start(f32[6,8,256]{2,1,0:T(8,128)S(1)} %get-tuple-element.26), channel_id=1, source_target_pairs={{0,1},{1,0},{2,3},{3,2},{4,5},{5,4},{6,7},{7,6},{8,9},{9,8},{10,11... | collective-permute-start | bytes 147464 | tf_op jit(solution)/shard_map/ppermute | solution.py:295
  11.7 7.7 %collective-permute-start.3 = (f32[6,8,256]{2,1,0:T(8,128)S(1)}, f32[6,8,256]{2,1,0:T(8,128)S(1)}, u32[]{:S(2)}, u32[]{:S(2)}) collective-permute-start(f32[6,8,256]{2,1,0:T(8,128)S(1)} %get-tuple-element.27), channel_id=1, source_target_pairs={{0,3},{1,2},{2,1},{3,0},{4,7},{5,6},{6,5},{7,4},{8,11},{9,10},{10,... | collective-permute-start | bytes 147464 | tf_op jit(solution)/shard_map/ppermute | solution.py:293
  19.9 8.4 %collective-permute-start.4 = (f32[6,16,256]{2,1,0:T(8,128)S(1)}, f32[6,16,256]{2,1,0:T(8,128)S(1)}, u32[]{:S(2)}, u32[]{:S(2)}) collective-permute-start(f32[6,16,256]{2,1,0:T(8,128)S(1)} %get-tuple-element.36), channel_id=1, source_target_pairs={{0,4},{4,0},{8,12},{12,8},{16,20},{20,16},{24,28},{28,24},{32,36},... | collective-permute-start | bytes 294920 | tf_op jit(solution)/shard_map/ppermute | solution.py:294
  20.0 8.3 %collective-permute-start.5 = (f32[6,16,256]{2,1,0:T(8,128)S(1)}, f32[6,16,256]{2,1,0:T(8,128)S(1)}, u32[]{:S(2)}, u32[]{:S(2)}) collective-permute-start(f32[6,16,256]{2,1,0:T(8,128)S(1)} %get-tuple-element.37), channel_id=1, source_target_pairs={{0,124},{4,8},{8,4},{12,16},{16,12},{20,24},{24,20},{28,32},{32,28... | collective-permute-start | bytes 294920 | tf_op jit(solution)/shard_map/ppermute | solution.py:292
  20.3 8.1 %collective-permute-start.6 = (f32[6,8,256]{2,1,0:T(8,128)S(1)}, f32[6,8,256]{2,1,0:T(8,128)S(1)}, u32[]{:S(2)}, u32[]{:S(2)}) collective-permute-start(f32[6,8,256]{2,1,0:T(8,128)S(1)} %get-tuple-element.38), channel_id=1, source_target_pairs={{0,1},{1,0},{2,3},{3,2},{4,5},{5,4},{6,7},{7,6},{8,9},{9,8},{10,11... | collective-permute-start | bytes 147464 | tf_op jit(solution)/shard_map/ppermute | solution.py:295
  21.5 6.8 %collective-permute-start.7 = (f32[6,8,256]{2,1,0:T(8,128)S(1)}, f32[6,8,256]{2,1,0:T(8,128)S(1)}, u32[]{:S(2)}, u32[]{:S(2)}) collective-permute-start(f32[6,8,256]{2,1,0:T(8,128)S(1)} %get-tuple-element.39), channel_id=1, source_target_pairs={{0,3},{1,2},{2,1},{3,0},{4,7},{5,6},{6,5},{7,4},{8,11},{9,10},{10,... | collective-permute-start | bytes 147464 | tf_op jit(solution)/shard_map/ppermute | solution.py:293
  24.1 4.2 %copy-start.1 = (f32[512,6,128]{2,0,1:T(8,128)S(1)}, f32[512,6,128]{2,0,1:T(8,128)}, u32[]{:S(2)}) copy-start(f32[512,6,128]{2,0,1:T(8,128)} %param.15) | copy-start | bytes 4718596
  24.1 4.3 %copy-start.2 = (s32[512]{0:T(512)S(1)}, s32[512]{0:T(512)}, u32[]{:S(2)}) copy-start(s32[512]{0:T(512)} %param.14) | copy-start | bytes 6148
  24.1 4.3 %copy-start.3 = (s32[512]{0:T(512)S(1)}, s32[512]{0:T(512)}, u32[]{:S(2)}) copy-start(s32[512]{0:T(512)} %param.13) | copy-start | bytes 6148
  30.4 7.9 %collective-permute-start.10 = (f32[1,128]{1,0:T(1,128)S(1)}, f32[1,128]{1,0:T(1,128)S(1)}, u32[]{:S(2)}, u32[]{:S(2)}) collective-permute-start(f32[1,128]{1,0:T(1,128)S(1)} %get-tuple-element.43), channel_id=1, source_target_pairs={{0,6},{1,7},{2,4},{3,5},{4,10},{5,11},{6,8},{7,9},{8,14},{9,15},{1... | collective-permute-start | bytes 1544 | tf_op jit(solution)/shard_map/ppermute | solution.py:307
  31.2 7.1 %collective-permute-start.8 = (f32[1,128]{1,0:T(1,128)S(1)}, f32[1,128]{1,0:T(1,128)S(1)}, u32[]{:S(2)}, u32[]{:S(2)}) collective-permute-start(f32[1,128]{1,0:T(1,128)S(1)} %get-tuple-element.42), channel_id=1, source_target_pairs={{0,2},{1,3},{2,0},{3,1},{4,6},{5,7},{6,4},{7,5},{8,10},{9,11},{10,... | collective-permute-start | bytes 1544 | tf_op jit(solution)/shard_map/ppermute | solution.py:309
  32.1 6.8 %collective-permute-start.9 = (f32[1,128]{1,0:T(1,128)S(1)}, f32[1,128]{1,0:T(1,128)S(1)}, u32[]{:S(2)}, u32[]{:S(2)}) collective-permute-start(f32[1,128]{1,0:T(1,128)S(1)} %get-tuple-element.43), channel_id=1, source_target_pairs={{0,4},{1,5},{2,6},{3,7},{4,8},{5,9},{6,10},{7,11},{8,12},{9,13},{1... | collective-permute-start | bytes 1544 | tf_op jit(solution)/shard_map/ppermute | solution.py:308
  38.9 4.0 %collective-permute-start.11 = (f32[1,128]{1,0:T(1,128)S(1)}, f32[1,128]{1,0:T(1,128)S(1)}, u32[]{:S(2)}, u32[]{:S(2)}) collective-permute-start(f32[1,128]{1,0:T(1,128)S(1)} %add_add_fusion), channel_id=1, source_target_pairs={{0,1},{1,0},{2,3},{3,2},{4,5},{5,4},{6,7},{7,6},{8,9},{9,8},{10,11... | collective-permute-start | bytes 1544 | tf_op jit(solution)/shard_map/ppermute | solution.py:311
